TPU v7x, 32 devices: a whole 2x2x4 slice. The times are simulated.
32 devices in a mesh: groups: 2 (over y), slide: 4 (over x, core), band: 4 (over z).
Axes of the slice: x: 2, y: 2, z: 4, core: 2. Of those that a mesh axis runs over, the one named last changes fastest.
Arguments:
- features: bfloat16 [8, 4, 256, 192], P(('groups', 'slide'), 'band'), parts along dimension 0, may hold values from -6 to 6
- tissue: int32 [8, 4, 2], P(('groups', 'slide'), 'band'), parts along dimension 0, may hold values 0 or 1
- cotangent: bfloat16 [8, 4, 256, 192], P(('groups', 'slide'), None, 'band'), parts along dimension 0, may hold values from -6 to 6
- x_proj: float32 [4, 192, 38], replicated, may hold values from -0.4375 to 0.4375
- dt_proj: float32 [4, 6, 192], replicated, may hold values from -2.5 to 2.5
- dt_bias: float32 [4, 192], replicated, may hold values from -6 to -2
- a_log: float32 [4, 16, 192], replicated, may hold values from 0 to 2.77
- d_skip: float32 [4, 192], replicated, may hold values from 0.5 to 1.5
Outputs:
- mixed: bfloat16 [8, 4, 256, 192], P(('groups', 'slide'), None, 'band'), parts along dimension 0
- grad_features: bfloat16 [8, 4, 256, 192], P(('groups', 'slide'), 'band'), parts along dimension 0
- grad_x_proj: float32 [8, 192, 38], P('groups'), parts along dimension 0
- grad_dt_proj: float32 [8, 6, 192], P('groups'), parts along dimension 0
- grad_dt_bias: float32 [8, 192], P('groups'), parts along dimension 0
- grad_a_log: float32 [8, 16, 192], P('groups'), parts along dimension 0
- grad_d_skip: float32 [8, 192], P('groups'), parts along dimension 0
There are 2 independent parts, one for each index of `groups`. A program takes and returns all parts, laid end to end along the dimension named above; an argument that names none is the same for every part. Nothing has to cross between parts.
Inputs may be any that keep to these rules, and one draw needn't show every extreme that they name: 1 marks a tile of 128 tokens of one row that holds tissue, 0 one without.
All inputs are finite; a program needn't handle non-finite values. No bound on the sum of `tissue` on one device may be relied on, other than what follows from the above.
Results may differ from a plain program's by a relative error of at most 0.015.
Values may be sent and summed in bfloat16 or wider, within the bound.
No kernel may reach another device: no remote copies, remote signals or barrier semaphores. Data moves between devices by JAX's collectives and lax.ppermute only.
A program may use at most 192 MiB of HBM per device.

v0:
```python
import functools

import jax
import jax.numpy as jnp
import numpy as np
from jax import lax
from jax.experimental import pallas as pl
from jax.experimental.pallas import tpu as pltpu
from jax.sharding import PartitionSpec as P

F32 = jnp.float32
BF16 = jnp.bfloat16
LANES = 128
SUB = 8
LOG2E = 1.4426950408889634
LN2 = 0.6931471805599453
VMEM_LIMIT = 34 * 2**20


def dot(a, b, dims=((1,), (0,))):
    return lax.dot_general(a, b, (dims, ((), ())), preferred_element_type=F32)


def split(x):
    hi = x.astype(BF16)
    return hi, (x - hi.astype(F32)).astype(BF16)


def swap64(x):
    return pltpu.roll(x, LANES // 2, axis=1)


def lane_iota(rows):
    return lax.broadcasted_iota(jnp.int32, (rows, LANES), 1)


def pack_tiles(a0, b0, a1, b1):
    low = lane_iota(a0.shape[0]) < LANES // 2
    return [a0, jnp.where(low, b0, swap64(b1)), a1]


class Plan:
    def __init__(self, steps, lines, chunked, channels, states, rank):
        self.steps, self.lines, self.chunked = steps, lines, chunked
        self.rows = steps * lines
        self.groups = lines // SUB
        self.channels, self.states, self.rank = channels, states, rank
        self.half = LANES // 2
        self.unroll = next(k for k in (8, 4, 2, 1) if steps % k == 0)

    def reverse(self, x):
        return jnp.concatenate([x[s * self.lines : (s + 1) * self.lines] for s in reversed(range(self.steps))], axis=0)

    def perm(self):
        r = np.arange(self.rows)
        s, j = r // self.lines, r % self.lines
        first = j * self.steps + s
        second = self.rows - 1 - first
        hot = np.zeros((self.rows, 2 * self.rows), np.float32)
        hot[r, first] = 1.0
        hot[r, self.rows + second] = 1.0
        back = np.concatenate([hot[:, : self.rows].T, hot[:, self.rows :].T], axis=1)
        return jnp.asarray(hot, BF16), jnp.asarray(back, BF16)


def load_weights(plan, side, x_ref, dtp_ref, bias_ref, alog_ref, skip_ref, w):
    ch, nst = plan.channels, plan.states
    pad, half = w["pad"], plan.half
    pad[:, :, ch:] = jnp.zeros((2, pad.shape[1], 2 * LANES - ch), F32)

    def halves(rows):
        first, second = pad[0, 0:rows, :], pad[1, 0:rows, :]
        return first[:, :LANES], first[:, LANES:], second[:, :LANES], second[:, LANES:]

    def diagonal(ref, dst):
        count = ref.shape[0]
        rows = -(-count // SUB) * SUB
        dst[...] = jnp.zeros_like(dst)
        for d in range(2):
            pad[d, rows - SUB : rows, 0:ch] = jnp.zeros((SUB, ch), F32)
            pad[d, 0:count, 0:ch] = ref[:, 2 * side + d, :]
        a0, b0, a1, b1 = halves(rows)
        dst[0:rows, 0:LANES] = a0
        dst[0:rows, LANES : 2 * LANES] = b0
        dst[half : half + rows, LANES : 2 * LANES] = swap64(b1)
        dst[half : half + rows, 2 * LANES :] = a1

    diagonal(x_ref, w["x"])
    diagonal(dtp_ref, w["dtp"])
    for d in range(2):
        pad[d, 0:1, 0:ch] = bias_ref[2 * side + d : 2 * side + d + 1, :]
        pad[d, SUB : SUB + 1, 0:ch] = skip_ref[2 * side + d : 2 * side + d + 1, :]
        pad[d, 2 * SUB : 2 * SUB + nst, 0:ch] = alog_ref[2 * side + d]
    tiles = pack_tiles(*halves(2 * SUB + nst))
    for k in range(3):
        at = slice(k * LANES, (k + 1) * LANES)
        w["small"][0 : 2 * SUB, at] = tiles[k][0 : 2 * SUB]
        rates = -jnp.exp(tiles[k][2 * SUB :])
        w["small"][2 * SUB :, at] = rates
        for n in range(nst):
            w["rate"][n, :, at] = jnp.broadcast_to(rates[n : n + 1, :] * LOG2E, (SUB, LANES))


def place(plan, perm_ref, x, dst, tall=False):
    if plan.chunked:
        dims = ((1,), (1,)) if tall else ((1,), (0,))
        first = dot(perm_ref[:, : plan.rows], x, dims)
        second = dot(perm_ref[:, plan.rows :], x, dims)
    else:
        first, second = x, plan.reverse(x)
    a0, b0, a1, b1 = first[:, :LANES], first[:, LANES:], second[:, :LANES], second[:, LANES:]
    for k, tile in enumerate(pack_tiles(a0, b0, a1, b1)):
        dst[:, k * LANES : (k + 1) * LANES] = tile
    return b0, b1


def unplace(plan, back_ref, packed, stack):
    t0, t1, t2 = packed
    if not plan.chunked:
        return t0 + plan.reverse(t2), t1 + plan.reverse(swap64(t1))
    stack[0 : plan.rows, 0:LANES] = t0
    stack[0 : plan.rows, LANES:] = t1
    stack[plan.rows :, 0:LANES] = t2
    stack[plan.rows :, LANES:] = swap64(t1)
    hi, lo = split(stack[...])
    out = dot(back_ref[...], hi) + dot(back_ref[...], lo)
    return out[:, :LANES], out[:, LANES:]


def prepare(plan, perm_ref, x256, w, t):
    b0, b1 = place(plan, perm_ref, x256, t["u"], plan.chunked)
    low = lane_iota(plan.rows) < plan.half
    m0 = jnp.where(low, swap64(b0), b0)
    m1 = jnp.where(low, swap64(b1), b1)
    masks = [m0, jnp.where(low, m0, m1), m1]
    for k in range(3):
        t["m"][:, k * LANES : (k + 1) * LANES] = masks[k]
    u = t["u"][...].astype(BF16)
    x_hi, x_lo = split(w["x"][...])
    proj = dot(u, x_hi, ((1,), (1,))) + dot(u, x_lo, ((1,), (1,)))
    t["p"][...] = proj
    p_hi, p_lo = split(proj)
    d_hi, d_lo = split(w["dtp"][...])
    z = dot(p_hi, d_hi) + dot(p_lo, d_hi) + dot(p_hi, d_lo) + w["small"][0:1, :]
    t["z"][...] = z
    soft = jnp.maximum(z, 0.0) + jnp.log1p(jnp.exp(-jnp.abs(z)))
    dt = soft * t["m"][...]
    t["dt"][...] = dt
    t["dtu"][...] = dt * t["u"][...]
    spread(plan, t)


def spread(plan, t):
    k = lax.broadcasted_iota(jnp.int32, (2 * LANES, 2 * LANES), 0) % LANES
    l = lax.broadcasted_iota(jnp.int32, (2 * LANES, 2 * LANES), 1)
    ones = jnp.where((k < plan.half) == (l < LANES), 1.0, 0.0).astype(BF16)
    proj = t["p"][...]
    hi = proj.astype(BF16).astype(F32)
    lo = proj - hi
    lane = lane_iota(plan.rows)
    for r in range(2 * plan.states):
        at = plan.rank + r
        mine = (lane == at) | (lane == at + plan.half)
        lhs = jnp.concatenate([jnp.where(mine, hi, 0.0), jnp.where(mine, lo, 0.0)], axis=1).astype(BF16)
        t["bb"][r] = dot(lhs, ones)


def fold(x):
    low = lane_iota(SUB) < LANES // 2
    t0, t1, t2 = x[:, :LANES], x[:, LANES : 2 * LANES], x[:, 2 * LANES :]
    return jnp.concatenate([jnp.where(low, t0, t2) + t1, jnp.where(low, t2, t0)], axis=1)


def gather(plan, t):
    k = lax.broadcasted_iota(jnp.int32, (2 * LANES, LANES), 0)
    l = lax.broadcasted_iota(jnp.int32, (2 * LANES, LANES), 1)
    first = (k < plan.half) | (k >= LANES + plan.half)
    ones = jnp.where(first == (l < plan.half), 1.0, 0.0).astype(BF16)
    lane = lane_iota(plan.rows)
    out = jnp.zeros((plan.rows, LANES), F32)
    for r in range(2 * plan.states):
        at = plan.rank + r
        mine = (lane == at) | (lane == at + plan.half)
        out = jnp.where(mine, dot(t["prod"][r].astype(BF16), ones), out)
    return out


def coefs(plan, t, row, n, which):
    r = which * plan.states + n
    lo = t["bb"][r, pl.ds(row, SUB), 0:LANES]
    hi = t["bb"][r, pl.ds(row, SUB), LANES:]
    mid = jnp.where(lane_iota(SUB) < plan.half, lo, hi)
    return jnp.concatenate([lo, mid, hi], axis=1)


def over_steps(plan, g, body, carry, backwards=False):
    u = plan.unroll

    def chunk(i, carry):
        for k in range(u):
            s = i * u + k
            if backwards:
                s = plan.steps - 1 - s
            row = s * plan.lines + g * SUB
            if not isinstance(row, int):
                row = pl.multiple_of(row, SUB)
            carry = body(s, row, carry)
        return carry

    if plan.steps == u:
        return chunk(0, carry)
    return lax.fori_loop(0, plan.steps // u, chunk, carry)


def over_groups(plan, body):
    if plan.groups == 1:
        body(0)
    else:
        lax.fori_loop(0, plan.groups, lambda g, c: (body(g), c)[1], 0)


def chunk_scan(decay, end, backwards):
    at = lax.broadcasted_iota(jnp.int32, end.shape, 0)
    for shift in (1, 2, 4):
        if backwards:
            inside, amount = at < SUB - shift, SUB - shift
        else:
            inside, amount = at >= shift, shift
        prev_end, prev_decay = pltpu.roll(end, amount, axis=0), pltpu.roll(decay, amount, axis=0)
        end = jnp.where(inside, decay * prev_end + end, end)
        decay = jnp.where(inside, decay * prev_decay, decay)
    if backwards:
        return jnp.where(at < SUB - 1, pltpu.roll(end, SUB - 1, axis=0), 0.0)
    return jnp.where(at >= 1, pltpu.roll(end, 1, axis=0), 0.0)


def chunk_decay(plan, w, t, n):
    total = functools.reduce(lambda a, b: a + b, [t["dt"][s * SUB : (s + 1) * SUB, :] for s in range(plan.steps)])
    return [jnp.exp2(total * w["rate"][k]) for k in n]


def forward(plan, w, t, keep_states):
    nst, per = plan.states, 8
    zero = jnp.zeros((SUB, 3 * LANES), F32)
    for n0 in range(0, nst, per):
        ns = list(range(n0, n0 + per))

        def group(g, ns=ns, n0=n0):
            start = tuple(zero for _ in ns)
            if plan.chunked:

                def local(s, row, hs):
                    dt, dtu = t["dt"][pl.ds(row, SUB), :], t["dtu"][pl.ds(row, SUB), :]
                    return tuple(
                        jnp.exp2(dt * w["rate"][n]) * h + coefs(plan, t, row, n, 0) * dtu for n, h in zip(ns, hs)
                    )

                ends = over_steps(plan, g, local, start)
                start = tuple(chunk_scan(d, e, False) for d, e in zip(chunk_decay(plan, w, t, ns), ends))
            if keep_states:
                for n, h in zip(ns, start):
                    t["h"][0, n, pl.ds(g * SUB, SUB), :] = h

            def full(s, row, hs):
                dt, dtu = t["dt"][pl.ds(row, SUB), :], t["dtu"][pl.ds(row, SUB), :]
                y = t["u"][pl.ds(row, SUB), :] * w["small"][SUB : SUB + 1, :] if n0 == 0 else t["y"][pl.ds(row, SUB), :]
                new = []
                for n, h in zip(ns, hs):
                    h = jnp.exp2(dt * w["rate"][n]) * h + coefs(plan, t, row, n, 0) * dtu
                    y = y + coefs(plan, t, row, n, 1) * h
                    if keep_states:
                        t["h"][s + 1, n, pl.ds(g * SUB, SUB), :] = h
                    new.append(h)
                t["y"][pl.ds(row, SUB), :] = y
                return tuple(new)

            over_steps(plan, g, full, start)

        over_groups(plan, group)


def backward(plan, w, t):
    nst, per = plan.states, 4
    zero = jnp.zeros((SUB, 3 * LANES), F32)
    for n0 in range(0, nst, per):
        ns = list(range(n0, n0 + per))

        def group(g, ns=ns, n0=n0):
            start = tuple(zero for _ in ns)
            if plan.chunked:

                def local(s, row, gs):
                    dt, gy = t["dt"][pl.ds(row, SUB), :], t["gy"][pl.ds(row, SUB), :]
                    return tuple(
                        jnp.exp2(dt * w["rate"][n]) * (coefs(plan, t, row, n, 1) * gy + c) for n, c in zip(ns, gs)
                    )

                ends = over_steps(plan, g, local, start, backwards=True)
                start = tuple(chunk_scan(d, e, True) for d, e in zip(chunk_decay(plan, w, t, ns), ends))

            def full(s, row, carry):
                gs, rs = carry
                dt, dtu = t["dt"][pl.ds(row, SUB), :], t["dtu"][pl.ds(row, SUB), :]
                gy = t["gy"][pl.ds(row, SUB), :]
                if n0 == 0:
                    sb, wq = zero, zero
                else:
                    sb, wq = t["sb"][pl.ds(row, SUB), :], t["wq"][pl.ds(row, SUB), :]
                new_g, new_r = [], []
                for n, c, r in zip(ns, gs, rs):
                    h_now = t["h"][s + 1, n, pl.ds(g * SUB, SUB), :]
                    h_prev = t["h"][s, n, pl.ds(g * SUB, SUB), :]
                    gh = coefs(plan, t, row, n, 1) * gy + c
                    t["prod"][n, pl.ds(row, SUB), :] = fold(gh * dtu)
                    t["prod"][nst + n, pl.ds(row, SUB), :] = fold(gy * h_now)
                    sb = sb + gh * coefs(plan, t, row, n, 0)
                    c = jnp.exp2(dt * w["rate"][n]) * gh
                    q = c * h_prev
                    wq = wq + q * w["rate"][n]
                    new_g.append(c)
                    new_r.append(r + q * dt)
                t["sb"][pl.ds(row, SUB), :] = sb
                t["wq"][pl.ds(row, SUB), :] = wq
                return tuple(new_g), tuple(new_r)

            _, rs = over_steps(plan, g, full, (start, tuple(zero for _ in ns)), backwards=True)
            for n, r in zip(ns, rs):
                t["gr"][n] = r if plan.groups == 1 else t["gr"][n] + r

        if plan.groups > 1:
            for n in ns:
                t["gr"][n] = zero
        over_groups(plan, group)


def finish(plan, back_ref, w, t):
    nst, rank = plan.states, plan.rank
    u, dt, gy, sb = t["u"][...], t["dt"][...], t["gy"][...], t["sb"][...]
    g_dt = t["wq"][...] * LN2 + sb * u
    gz = g_dt * t["m"][...] * (1.0 / (1.0 + jnp.exp(-t["z"][...])))
    gz_b = gz.astype(BF16)
    dtp_b = w["dtp"][...].astype(BF16)
    gp = gather(plan, t) + dot(gz_b, dtp_b, ((1,), (1,)))
    gp_b = gp.astype(BF16)
    u_b = u.astype(BF16)
    g_x = dot(gp_b, u_b, ((0,), (0,)))
    g_d = dot(t["p"][...].astype(BF16), gz_b, ((0,), (0,)))
    lane = lax.broadcasted_iota(jnp.int32, (SUB, 3 * LANES), 1)
    first = lane < plan.channels
    wide = -(-(rank + 2 * nst) // SUB) * SUB
    blocks = [jnp.where(first, g_x[r : r + SUB, :], g_x[plan.half + r : plan.half + r + SUB, :]) for r in range(0, wide, SUB)]
    row = lax.broadcasted_iota(jnp.int32, (SUB, 3 * LANES), 0)
    small = jnp.where(first, g_d[0:SUB, :], g_d[plan.half : plan.half + SUB, :])
    small = jnp.where(row == SUB - 2, jnp.sum(gz, axis=0, keepdims=True), small)
    blocks.append(jnp.where(row == SUB - 1, jnp.sum(gy * u, axis=0, keepdims=True), small))
    for n0 in range(0, nst, SUB):
        part = jnp.zeros((SUB, 3 * LANES), F32)
        for n in range(n0, n0 + SUB):
            part = jnp.where(row == n - n0, jnp.sum(t["gr"][n], axis=0, keepdims=True), part)
        blocks.append(part * w["small"][2 * SUB + n0 : 3 * SUB + n0, :])
    grads = jnp.concatenate(blocks, axis=0)
    gu = sb * dt + gy * w["small"][SUB : SUB + 1, :] + dot(gp_b, w["x"][...].astype(BF16))
    tiles = [gu[:, k * LANES : (k + 1) * LANES] for k in range(3)]
    return grads, unplace(plan, back_ref, tiles, t["stack"])


def weight_shapes(plan):
    up = -(-(plan.rank + 2 * plan.states) // SUB) * SUB
    return {
        "x": (LANES, 3 * LANES),
        "small": (2 * SUB + plan.states, 3 * LANES),
        "rate": (plan.states, SUB, 3 * LANES),
        "dtp": (LANES, 3 * LANES),
    }, {"pad": (2, max(2 * SUB + plan.states, up), 2 * LANES)}


def token_shapes(plan):
    wide, narrow = (plan.rows, 3 * LANES), (plan.rows, LANES)
    kept = {"u": wide, "m": wide, "z": wide, "dt": wide, "dtu": wide, "p": narrow,
            "bb": (2 * plan.states, plan.rows, 2 * LANES),
            "h": (plan.steps + 1, plan.states, plan.lines, 3 * LANES)}
    own = {"y": wide, "stack": (2 * plan.rows, 2 * LANES), "x256": (plan.rows, 2 * LANES)}
    grads = {"gy": wide, "sb": wide, "wq": wide, "prod": (2 * plan.states, plan.rows, 2 * LANES),
             "gr": (plan.states, SUB, 3 * LANES), "x256": (plan.rows, 2 * LANES), "stack": (2 * plan.rows, 2 * LANES)}
    return kept, own, grads


def token_mask(plan, tissue_ref, shape, axis):
    per = plan.rows // tissue_ref.shape[0]
    token = lax.broadcasted_iota(jnp.int32, shape, axis)
    mask = jnp.zeros(shape, F32)
    for k in range(tissue_ref.shape[0]):
        mask = jnp.where((token >= k * per) & (token < (k + 1) * per), tissue_ref[k].astype(F32), mask)
    return mask


def masked_rows(plan, tissue_ref, feat_ref):
    ch = plan.channels
    mask = token_mask(plan, tissue_ref, (SUB, plan.rows), 1)
    tall = jnp.concatenate([mask] * (ch // SUB), axis=0)
    fill = jnp.concatenate([mask] * ((2 * LANES - ch) // SUB), axis=0)
    return jnp.concatenate([feat_ref[...].astype(F32) * tall, fill], axis=0).astype(BF16)


def partner_rows(count, rows, s):
    return pl.ds(pl.multiple_of((lax.axis_index("band") ^ s) * (rows // count), SUB), rows // count)


def send_blocks(refs, tiles, scratch, width):
    scratch[:, :LANES], scratch[:, LANES:] = tiles
    if len(refs) == 1:
        refs[0][...] = scratch[:, :width].astype(BF16)
        return
    for s, ref in enumerate(refs):
        ref[...] = scratch[partner_rows(len(refs), scratch.shape[0], s), :width].astype(BF16)


def receive_blocks(refs, scratch):
    width = refs[0].shape[1]
    if len(refs) == 1:
        scratch[:, :width] = refs[0][...].astype(F32)
        return
    for s, ref in enumerate(refs):
        scratch[partner_rows(len(refs), scratch.shape[0], s), :width] = ref[...].astype(F32)


def rows_forward_kernel(plan, side, *refs):
    count = 9
    far, (send_refs, w, kept, rest, near, sems) = refs[:count], refs[count:]
    copies = [pltpu.make_async_copy(a, b, sems.at[k]) for k, (a, b) in enumerate(zip(far, near))]
    for copy in copies:
        copy.start()
    for copy in copies:
        copy.wait()
    tissue_ref, feat_ref, perm_ref, back_ref, x_ref, dtp_ref, bias_ref, alog_ref, skip_ref = near
    t = kept | rest
    w = w | rest
    load_weights(plan, side, x_ref, dtp_ref, bias_ref, alog_ref, skip_ref, w)
    prepare(plan, perm_ref, masked_rows(plan, tissue_ref, feat_ref), w, t)
    forward(plan, w, t, True)
    tiles = [t["y"][:, k * LANES : (k + 1) * LANES] for k in range(3)]
    a, b = unplace(plan, back_ref, tiles, t["stack"])
    mask = token_mask(plan, tissue_ref, (plan.rows, LANES), 0)
    send_blocks(send_refs, (a, jnp.where(lane_iota(plan.rows) < plan.half, b, mask)), t["x256"], 2 * LANES)


def rows_backward_kernel(plan, side, tissue_ref, gy_refs, perm_ref, back_ref, w, kept, grads_v_ref,
                         out_ref, mine_ref, theirs_ref, rest):
    t = kept | rest
    receive_blocks(gy_refs, t["x256"])
    place(plan, perm_ref, t["x256"][...].astype(BF16), t["gy"])
    backward(plan, w, t)
    grads, (a, b) = finish(plan, back_ref, w, t)
    mask = token_mask(plan, tissue_ref, (plan.rows, LANES), 0)
    out_ref[:, :LANES] = (a * mask).astype(BF16)
    out_ref[:, LANES:] = (b * mask)[:, : plan.channels - LANES].astype(BF16)
    other = grads_v_ref[...].astype(F32)
    odd = lax.axis_index("slide") % 2 == 1
    mine_ref[...] = jnp.where(odd, other, grads).astype(BF16)
    theirs_ref[...] = jnp.where(odd, grads, other).astype(BF16)


def columns_kernel(plan, side, recv_refs, gy_ref, x_ref, dtp_ref, bias_ref, alog_ref, skip_ref,
                   mixed_ref, out_refs, grads_ref, t):
    ch = plan.channels
    w = t
    load_weights(plan, side, x_ref, dtp_ref, bias_ref, alog_ref, skip_ref, w)
    receive_blocks(recv_refs, t["x256"])
    low = lane_iota(plan.rows) < plan.half
    last = t["x256"][:, LANES:]
    mask = jnp.where(low, swap64(last), last)
    prepare(plan, None, jnp.concatenate([t["x256"][:, :LANES] * mask, last * mask], axis=1), w, t)
    t["x256"][:, 0:ch] = gy_ref[...].astype(F32)
    place(plan, None, t["x256"][...], t["gy"])
    forward(plan, w, t, True)
    tiles = [t["y"][:, k * LANES : (k + 1) * LANES] for k in range(3)]
    a, b = unplace(plan, None, tiles, None)
    mixed_ref[:, :LANES] = a.astype(BF16)
    mixed_ref[:, LANES:] = b[:, : ch - LANES].astype(BF16)
    backward(plan, w, t)
    grads, (a, b) = finish(plan, None, w, t)
    grads_ref[...] = grads.astype(BF16)
    mask = t["m"][:, :LANES]
    send_blocks(out_refs, (a * mask, b * mask), t["x256"], ch)


def unpack_kernel(plan, mine_ref, theirs_ref, gx_ref, gd_ref, gb_ref, ga_ref, gs_ref):
    nst, rank, ch = plan.states, plan.rank, plan.channels
    wide = rank + 2 * nst
    up = -(-wide // SUB) * SUB
    odd = lax.axis_index("slide") % 2 == 1
    mine, theirs = mine_ref[...].astype(F32), theirs_ref[...].astype(F32)
    for side, total in enumerate((jnp.where(odd, theirs, mine), jnp.where(odd, mine, theirs))):
        tiles = [total[:, k * LANES : (k + 1) * LANES] for k in range(3)]
        for d, (a, b) in enumerate(((tiles[0], tiles[1]), (tiles[2], swap64(tiles[1])))):
            k = 2 * side + d
            for lo, hi, part in ((0, LANES, a), (LANES, ch, b[:, : ch - LANES])):
                gx_ref[:, k, lo:hi] = part[0:wide, :]
                gd_ref[:, k, lo:hi] = part[up : up + rank, :]
                gb_ref[k : k + 1, lo:hi] = part[up + SUB - 2 : up + SUB - 1, :]
                gs_ref[k : k + 1, lo:hi] = part[up + SUB - 1 : up + SUB, :]
                ga_ref[k, :, lo:hi] = part[up + SUB : up + SUB + nst, :]


def call(kernel, plan, side, out_shape, args, scratch, name, cost, scalars=0, far=()):
    whole = pl.BlockSpec(memory_space=pltpu.VMEM)
    specs = list(jax.tree.map(lambda _: whole, tuple(args)))
    if scalars:
        specs[0] = pl.BlockSpec(memory_space=pltpu.SMEM)
    scratches = [{k: pltpu.VMEM(v, F32) for k, v in scratch.items()}]
    if far:
        args = [pltpu.with_memory_space_constraint(a, pltpu.HBM) if k in far else a for k, a in enumerate(args)]
        for k in far:
            specs[k] = pl.BlockSpec(memory_space=pltpu.HBM)
        scratches += [[(pltpu.SMEM if args[k].ndim == 1 else pltpu.VMEM)(args[k].shape, args[k].dtype) for k in far], pltpu.SemaphoreType.DMA((len(far),))]
    return pl.pallas_call(
        functools.partial(kernel, plan, side), out_shape=out_shape, in_specs=tuple(specs),
        out_specs=jax.tree.map(lambda _: whole, out_shape), scratch_shapes=scratches,
        name=name, cost_estimate=pl.CostEstimate(flops=cost * 10**6, bytes_accessed=4 * 10**6, transcendentals=0),
        compiler_params=pltpu.CompilerParams(vmem_limit_bytes=VMEM_LIMIT),
    )(*args)


def arrays(shapes):
    return {k: jax.ShapeDtypeStruct(v, F32) for k, v in shapes.items()}


def swap(x, axis, step):
    return lax.ppermute(x, axis, [(i, i ^ step) for i in range(lax.axis_size(axis))])


def exchange(x, axis, step):
    return (x.astype(F32) + swap(x, axis, step).astype(F32)).astype(BF16)


def deliver(blocks, rows):
    bands = lax.axis_size("band")
    if len(blocks) == 1:
        block = blocks[0].reshape(bands, rows // bands, -1)
        return [lax.all_to_all(block, "band", split_axis=0, concat_axis=0, tiled=True).reshape(rows, -1)]
    return [blocks[0]] + [swap(blocks[s], "band", s) for s in range(1, bands)]


def shards(features, tissue, cotangent, x_proj, dt_proj, dt_bias, a_log, d_skip):
    _, _, width, channels = features.shape
    _, height, cols_here, _ = cotangent.shape
    bands = lax.axis_size("band")
    dirs, rank, states = dt_proj.shape[0], dt_proj.shape[1], a_log.shape[1]
    rows_plan = Plan(width // SUB, SUB, True, channels, states, rank)
    cols_plan = Plan(height, cols_here, False, channels, states, rank)
    weights = [jnp.transpose(x_proj, (2, 0, 1)), jnp.transpose(dt_proj, (1, 0, 2)), dt_bias, a_log, d_skip]
    feat = jnp.transpose(features.reshape(width, channels))
    keep = tissue.reshape(-1)
    packed = -(-(rank + 2 * states) // SUB) * SUB + SUB + states
    grads_shape = jax.ShapeDtypeStruct((packed, 3 * LANES), BF16)

    perm, back = rows_plan.perm()
    w_kept, w_own = weight_shapes(rows_plan)
    kept, own, grads = token_shapes(rows_plan)
    count = bands if bands in (2, 4) else 1
    tokens = height * cols_here

    def blocks(rows, lanes):
        return [jax.ShapeDtypeStruct((rows // count, lanes), BF16)] * count

    send, w_rows, t_rows = call(
        rows_forward_kernel, rows_plan, 0, (blocks(width, 2 * LANES), arrays(w_kept), arrays(kept)),
        [keep, feat, perm, back] + weights, own | w_own, "rows_forward", 4000, 0, tuple(range(9)))
    moved = deliver(send, width)
    w_kept, w_own = weight_shapes(cols_plan)
    kept_c, own_c, grads_c = token_shapes(cols_plan)
    mixed, grad_carried, grads_v = call(
        columns_kernel, cols_plan, 1,
        (jax.ShapeDtypeStruct((tokens, channels), BF16), blocks(tokens, channels), grads_shape),
        [moved, cotangent.reshape(tokens, channels)] + weights,
        kept_c | own_c | grads_c | w_kept | w_own, "columns", 8000)
    returned = deliver(grad_carried, tokens)
    grad_features, mine, theirs = call(
        rows_backward_kernel, rows_plan, 0, (jax.ShapeDtypeStruct((width, channels), BF16), grads_shape, grads_shape),
        [keep, returned, perm, back, w_rows, t_rows, grads_v], grads, "rows_backward", 8000, 1)
    mine = (mine.astype(F32) + swap(theirs, "slide", 1).astype(F32)).astype(BF16)
    for axis in ("slide", "band"):
        step = 2 if axis == "slide" else 1
        while step < lax.axis_size(axis):
            mine = exchange(mine, axis, step)
            step *= 2
    theirs = swap(mine, "slide", 1)
    shapes = [(rank + 2 * states, dirs, channels), (rank, dirs, channels), (dirs, channels), (dirs, states, channels), (dirs, channels)]
    gx, gd, gb, ga, gs = pl.pallas_call(
        functools.partial(unpack_kernel, rows_plan), out_shape=[jax.ShapeDtypeStruct(s, F32) for s in shapes], name="unpack",
        compiler_params=pltpu.CompilerParams(vmem_limit_bytes=VMEM_LIMIT),
    )(mine, theirs)
    return (mixed.reshape(cotangent.shape), grad_features.reshape(features.shape), jnp.transpose(gx, (1, 2, 0)),
            jnp.transpose(gd, (1, 0, 2)), gb, ga, gs)


def solution(mesh):
    in_specs = (
        P(("groups", "slide"), "band", None, None),
        P(("groups", "slide"), "band", None),
        P(("groups", "slide"), None, "band", None),
        P(), P(), P(), P(), P(),
    )
    out_specs = (
        P(("groups", "slide"), None, "band", None),
        P(("groups", "slide"), "band", None, None),
        P("groups", None, None),
        P("groups", None, None),
        P("groups", None),
        P("groups", None, None),
        P("groups", None),
    )
    return jax.shard_map(shards, mesh=mesh, in_specs=in_specs, out_specs=out_specs, check_vma=False)
```

profile of v0, /device:TPU:0, one launch (start us, length us, event | category | flops | bytes accessed | tf_op | source)
XLA Modules:
  0.0 61.8 jit_solution(1764444254198213632)
XLA Ops:
  0.6 0.0 copy-start.5
  0.6 0.0 copy-start.2
  0.7 0.0 copy-start.4
  0.7 0.0 copy-start.3
  0.7 0.0 copy-start
  0.7 0.0 copy-start.1
  0.7 7.3 %rows_forward.1 = (bf16[64,256]{1,0:T(8,128)(2,1)S(1)}, bf16[64,256]{1,0:T(8,128)(2,1)S(1)}, bf16[64,256]{1,0:T(8,128)(2,1)S(1)}, bf16[64,256]{1,0:T(8,128)(2,1)...) custom-call(s32[2]{0:T(128)} %bitcast.17, ...), custom_call_target="tpu_custom_call" | custom-call | flops 4000000000 | bytes 4000000 | tf_op jit(solution)/shard_map/rows_forward/pallas_call | solution.py:516
  8.0 3.1 %collective-permute-start = (bf16[64,256]{1,0:T(8,128)(2,1)S(1)}, bf16[64,256]{1,0:T(8,128)(2,1)S(1)}, u32[]{:S(2)}, u32[]{:S(2)}) collective-permute-start(bf16[64,256]{1,0:T(8,128)(2,1)S(1)} %get-tuple-element.38), channel_id=1, source_target_pairs={{0,1},{1,0},{2,3},{3,2},{4,5},{5,4},{6,7},{7,6},{8,9},{9,8},{10,11... | collective-permute-start | bytes 98312 | tf_op jit(solution)/shard_map/ppermute | solution.py:529
  11.1 2.6 %collective-permute-start.1 = (bf16[64,256]{1,0:T(8,128)(2,1)S(1)}, bf16[64,256]{1,0:T(8,128)(2,1)S(1)}, u32[]{:S(2)}, u32[]{:S(2)}) collective-permute-start(bf16[64,256]{1,0:T(8,128)(2,1)S(1)} %get-tuple-element.39), channel_id=1, source_target_pairs={{0,2},{1,3},{2,0},{3,1},{4,6},{5,7},{6,4},{7,5},{8,10},{9,11},{10,... | collective-permute-start | bytes 98312 | tf_op jit(solution)/shard_map/ppermute | solution.py:529
  13.7 0.0 collective-permute-start.2
  13.7 0.0 collective-permute-done.recv_refs_1_
  13.7 2.8 %collective-permute-done.1.recv_refs_2_ = bf16[64,256]{1,0:T(8,128)(2,1)S(1)} collective-permute-done((bf16[64,256]{1,0:T(8,128)(2,1)S(1)}, bf16[64,256]{1,0:T(8,128)(2,1)S(1)}, u32[]{:S(2)}, u32[]{:S(2)}) %collective-permute-start.1) | collective-permute-done | bytes 32800 | tf_op jit(solution)/shard_map/ppermute | solution.py:529
  16.5 2.9 %collective-permute-done.2.recv_refs_3_ = bf16[64,256]{1,0:T(8,128)(2,1)S(1)} collective-permute-done((bf16[64,256]{1,0:T(8,128)(2,1)S(1)}, bf16[64,256]{1,0:T(8,128)(2,1)S(1)}, u32[]{:S(2)}, u32[]{:S(2)}) %collective-permute-start.2) | collective-permute-done | bytes 32800 | tf_op jit(solution)/shard_map/ppermute | solution.py:529
  19.4 0.0 copy-done.5
  19.4 0.0 copy-done.2
  19.4 0.0 copy-done.4
  19.4 0.0 copy-done.3
  19.4 0.0 copy-done
  19.4 0.0 copy-done.1
  19.4 0.0 copy-start.6
  19.4 0.0 copy-start.7
  19.5 0.0 copy-start.8
  19.5 10.4 %columns.1 = (bf16[256,192]{1,0:T(8,128)(2,1)}, bf16[64,192]{1,0:T(8,128)(2,1)S(1)}, bf16[64,192]{1,0:T(8,128)(2,1)S(1)}, bf16[64,192]{1,0:T(8,128)(2,1)S(1)}, b...) custom-call(bf16[64,256]{1,0:T(8,128)(2,1)S(1)} %get-tuple-element.37.recv_refs_0_, ...), custom_call_target="tpu_custom_call" | custom-call | flops 8000000000 | bytes 4000000 | tf_op jit(solution)/shard_map/columns/pallas_call | solution.py:516
  29.8 0.0 collective-permute-start.3
  29.8 0.9 %collective-permute-start.4 = (bf16[64,192]{1,0:T(8,128)(2,1)S(1)}, bf16[64,192]{1,0:T(8,128)(2,1)S(1)}, u32[]{:S(2)}, u32[]{:S(2)}) collective-permute-start(bf16[64,192]{1,0:T(8,128)(2,1)S(1)} %get-tuple-element.44), channel_id=1, source_target_pairs={{0,2},{1,3},{2,0},{3,1},{4,6},{5,7},{6,4},{7,5},{8,10},{9,11},{10,... | collective-permute-start | bytes 73736 | tf_op jit(solution)/shard_map/ppermute | solution.py:529
  30.8 3.5 %collective-permute-start.5 = (bf16[64,192]{1,0:T(8,128)(2,1)S(1)}, bf16[64,192]{1,0:T(8,128)(2,1)S(1)}, u32[]{:S(2)}, u32[]{:S(2)}) collective-permute-start(bf16[64,192]{1,0:T(8,128)(2,1)S(1)} %get-tuple-element.45), channel_id=1, source_target_pairs={{0,3},{1,2},{2,1},{3,0},{4,7},{5,6},{6,5},{7,4},{8,11},{9,10},{10,... | collective-permute-start | bytes 73736 | tf_op jit(solution)/shard_map/ppermute | solution.py:529
  34.2 0.0 collective-permute-done.3.gy_refs_1_
  34.2 0.4 collective-permute-done.4.gy_refs_2_
  34.7 1.8 %collective-permute-done.5.gy_refs_3_ = bf16[64,192]{1,0:T(8,128)(2,1)S(1)} collective-permute-done((bf16[64,192]{1,0:T(8,128)(2,1)S(1)}, bf16[64,192]{1,0:T(8,128)(2,1)S(1)}, u32[]{:S(2)}, u32[]{:S(2)}) %collective-permute-start.5) | collective-permute-done | bytes 24608 | tf_op jit(solution)/shard_map/ppermute | solution.py:529
  36.5 0.0 copy-done.6
  36.5 0.0 copy-done.7
  36.5 0.0 copy-done.8
  36.5 8.4 %rows_backward.1 = (bf16[256,192]{1,0:T(8,128)(2,1)S(1)}, bf16[64,384]{1,0:T(8,128)(2,1)S(1)}, bf16[64,384]{1,0:T(8,128)(2,1)S(1)}) custom-call(s32[2]{0:T(128)S(1)} %bitcast.18, bf16[64,192]{1,0:T(8,128)(2,1)S(1)} %get-tuple-element.42.gy_refs_0_, bf16[64,192]{1,0:T(8,128)(2,1)S(1)} %collective-permute-done.3.gy_refs_1_, ...), custom_call_target="tpu_custom_call" | custom-call | flops 8000000000 | bytes 4000000 | tf_op jit(solution)/shard_map/rows_backward/pallas_call | solution.py:516
  44.9 0.1 collective-permute-start.6
  45.0 1.2 %collective-permute-done.6 = bf16[64,384]{1,0:T(8,128)(2,1)S(1)} collective-permute-done((bf16[64,384]{1,0:T(8,128)(2,1)S(1)}, bf16[64,384]{1,0:T(8,128)(2,1)S(1)}, u32[]{:S(2)}, u32[]{:S(2)}) %collective-permute-start.6) | collective-permute-done | bytes 49184 | tf_op jit(solution)/shard_map/ppermute | solution.py:529
  46.3 1.5 %collective-permute-start.7 = (bf16[64,384]{1,0:T(8,128)(2,1)S(1)}, bf16[64,384]{1,0:T(8,128)(2,1)S(1)}, u32[]{:S(2)}, u32[]{:S(2)}) collective-permute-start(bf16[64,384]{1,0:T(8,128)(2,1)S(1)} %add_convert_fusion.3), channel_id=1, source_target_pairs={{0,8},{4,12},{8,0},{12,4},{1,9},{5,13},{9,1},{13,5},{2,10},{6,14},... | collective-permute-start | bytes 147464 | tf_op jit(solution)/shard_map/ppermute | solution.py:529
  47.8 2.6 %collective-permute-done.7 = bf16[64,384]{1,0:T(8,128)(2,1)S(1)} collective-permute-done((bf16[64,384]{1,0:T(8,128)(2,1)S(1)}, bf16[64,384]{1,0:T(8,128)(2,1)S(1)}, u32[]{:S(2)}, u32[]{:S(2)}) %collective-permute-start.7) | collective-permute-done | bytes 49184 | tf_op jit(solution)/shard_map/ppermute | solution.py:529
  50.4 0.3 collective-permute-start.8
  50.7 3.9 %collective-permute-done.8 = bf16[64,384]{1,0:T(8,128)(2,1)S(1)} collective-permute-done((bf16[64,384]{1,0:T(8,128)(2,1)S(1)}, bf16[64,384]{1,0:T(8,128)(2,1)S(1)}, u32[]{:S(2)}, u32[]{:S(2)}) %collective-permute-start.8) | collective-permute-done | bytes 49184 | tf_op jit(solution)/shard_map/ppermute | solution.py:529
  54.6 2.1 %collective-permute-start.9 = (bf16[64,384]{1,0:T(8,128)(2,1)S(1)}, bf16[64,384]{1,0:T(8,128)(2,1)S(1)}, u32[]{:S(2)}, u32[]{:S(2)}) collective-permute-start(bf16[64,384]{1,0:T(8,128)(2,1)S(1)} %add_convert_fusion.1), channel_id=1, source_target_pairs={{0,2},{1,3},{2,0},{3,1},{4,6},{5,7},{6,4},{7,5},{8,10},{9,11},{10,... | collective-permute-start | bytes 147464 | tf_op jit(solution)/shard_map/ppermute | solution.py:529
  56.7 3.0 %collective-permute-done.9 = bf16[64,384]{1,0:T(8,128)(2,1)S(1)} collective-permute-done((bf16[64,384]{1,0:T(8,128)(2,1)S(1)}, bf16[64,384]{1,0:T(8,128)(2,1)S(1)}, u32[]{:S(2)}, u32[]{:S(2)}) %collective-permute-start.9) | collective-permute-done | bytes 49184 | tf_op jit(solution)/shard_map/ppermute | solution.py:529
  59.7 0.1 collective-permute-start.10
  59.8 0.7 %copy.17 = bf16[1,1,256,192]{2,3,1,0:T(8,128)(2,1)} copy(bf16[1,1,256,192]{3,2,1,0:T(8,128)(2,1)S(1)} %bitcast.11) | data formatting | bytes 196608
  60.5 0.5 collective-permute-done.10.theirs_ref
  61.0 0.8 %unpack.1 = (f32[38,4,192]{2,1,0:T(4,128)}, f32[6,4,192]{2,1,0:T(4,128)}, f32[4,192]{1,0:T(4,128)}, f32[4,16,192]{2,1,0:T(8,128)}, f32[4,192]{1,0:T(4,128)}) custom-call(bf16[64,384]{1,0:T(8,128)(2,1)S(1)} %add_convert_fusion.mine_ref, bf16[64,384]{1,0:T(8,128)(2,1)S(1)} %collective-permute-done.10.theirs_ref), custom_call_target="tpu_custom_call" | custom-call | tf_op jit(solution)/shard_map/unpack/pallas_call | solution.py:589
  (4 shorter events, 0.1 us)
Async XLA Ops:
  0.6 18.8 %copy-start.5 = (f32[4,192]{1,0:T(4,128)S(1)}, f32[4,192]{1,0:T(4,128)}, u32[]{:S(2)}) copy-start(f32[4,192]{1,0:T(4,128)} %skip_ref.1) | copy-start | bytes 9220
  0.6 18.8 %copy-start.2 = (f32[4,16,192]{2,1,0:T(8,128)S(1)}, f32[4,16,192]{2,1,0:T(8,128)}, u32[]{:S(2)}) copy-start(f32[4,16,192]{2,1,0:T(8,128)} %alog_ref.1) | copy-start | bytes 147460
  0.7 18.7 %copy-start.4 = (f32[4,192]{1,0:T(4,128)S(1)}, f32[4,192]{1,0:T(4,128)}, u32[]{:S(2)}) copy-start(f32[4,192]{1,0:T(4,128)} %bias_ref.1) | copy-start | bytes 9220
  0.7 18.7 %copy-start.3 = (f32[4,6,192]{2,0,1:T(4,128)S(1)}, f32[4,6,192]{2,0,1:T(4,128)}, u32[]{:S(2)}) copy-start(f32[4,6,192]{2,0,1:T(4,128)} %param.14) | copy-start | bytes 55300
  0.7 18.7 %copy-start = (f32[4,192,38]{1,0,2:T(4,128)S(1)}, f32[4,192,38]{1,0,2:T(4,128)}, u32[]{:S(2)}) copy-start(f32[4,192,38]{1,0,2:T(4,128)} %param.13) | copy-start | bytes 350212
  0.7 18.7 %copy-start.1 = (bf16[1,4,64,192]{3,2,1,0:T(8,128)(2,1)S(1)}, bf16[1,4,64,192]{3,2,1,0:T(8,128)(2,1)}, u32[]{:S(2)}) copy-start(bf16[1,4,64,192]{3,2,1,0:T(8,128)(2,1)} %param.12) | copy-start | bytes 294916
  8.0 5.7 %collective-permute-start = (bf16[64,256]{1,0:T(8,128)(2,1)S(1)}, bf16[64,256]{1,0:T(8,128)(2,1)S(1)}, u32[]{:S(2)}, u32[]{:S(2)}) collective-permute-start(bf16[64,256]{1,0:T(8,128)(2,1)S(1)} %get-tuple-element.38), channel_id=1, source_target_pairs={{0,1},{1,0},{2,3},{3,2},{4,5},{5,4},{6,7},{7,6},{8,9},{9,8},{10,11... | collective-permute-start | bytes 98312 | tf_op jit(solution)/shard_map/ppermute | solution.py:529
  11.1 5.4 %collective-permute-start.1 = (bf16[64,256]{1,0:T(8,128)(2,1)S(1)}, bf16[64,256]{1,0:T(8,128)(2,1)S(1)}, u32[]{:S(2)}, u32[]{:S(2)}) collective-permute-start(bf16[64,256]{1,0:T(8,128)(2,1)S(1)} %get-tuple-element.39), channel_id=1, source_target_pairs={{0,2},{1,3},{2,0},{3,1},{4,6},{5,7},{6,4},{7,5},{8,10},{9,11},{10,... | collective-permute-start | bytes 98312 | tf_op jit(solution)/shard_map/ppermute | solution.py:529
  13.7 5.7 %collective-permute-start.2 = (bf16[64,256]{1,0:T(8,128)(2,1)S(1)}, bf16[64,256]{1,0:T(8,128)(2,1)S(1)}, u32[]{:S(2)}, u32[]{:S(2)}) collective-permute-start(bf16[64,256]{1,0:T(8,128)(2,1)S(1)} %get-tuple-element.40), channel_id=1, source_target_pairs={{0,3},{1,2},{2,1},{3,0},{4,7},{5,6},{6,5},{7,4},{8,11},{9,10},{10,... | collective-permute-start | bytes 98312 | tf_op jit(solution)/shard_map/ppermute | solution.py:529
  19.4 17.0 %copy-start.6 = (s32[1,1,2]{2,1,0:T(1,128)S(1)}, s32[1,1,2]{2,1,0:T(1,128)}, u32[]{:S(2)}) copy-start(s32[1,1,2]{2,1,0:T(1,128)} %param.11) | copy-start | bytes 28
  19.4 17.0 %copy-start.7 = (bf16[256,512]{1,0:T(8,128)(2,1)S(1)}, bf16[256,512]{1,0:T(8,128)(2,1)}, u32[]{:S(2)}) copy-start(bf16[256,512]{1,0:T(8,128)(2,1)} %constant.5.clone.refs_3_.back_ref) | copy-start | bytes 786436
  19.5 17.0 %copy-start.8 = (bf16[256,512]{1,0:T(8,128)(2,1)S(1)}, bf16[256,512]{1,0:T(8,128)(2,1)}, u32[]{:S(2)}) copy-start(bf16[256,512]{1,0:T(8,128)(2,1)} %constant.4.clone.refs_2_.perm_ref) | copy-start | bytes 786436
  29.8 4.4 %collective-permute-start.3 = (bf16[64,192]{1,0:T(8,128)(2,1)S(1)}, bf16[64,192]{1,0:T(8,128)(2,1)S(1)}, u32[]{:S(2)}, u32[]{:S(2)}) collective-permute-start(bf16[64,192]{1,0:T(8,128)(2,1)S(1)} %get-tuple-element.43), channel_id=1, source_target_pairs={{0,1},{1,0},{2,3},{3,2},{4,5},{5,4},{6,7},{7,6},{8,9},{9,8},{10,11... | collective-permute-start | bytes 73736 | tf_op jit(solution)/shard_map/ppermute | solution.py:529
  29.8 4.8 %collective-permute-start.4 = (bf16[64,192]{1,0:T(8,128)(2,1)S(1)}, bf16[64,192]{1,0:T(8,128)(2,1)S(1)}, u32[]{:S(2)}, u32[]{:S(2)}) collective-permute-start(bf16[64,192]{1,0:T(8,128)(2,1)S(1)} %get-tuple-element.44), channel_id=1, source_target_pairs={{0,2},{1,3},{2,0},{3,1},{4,6},{5,7},{6,4},{7,5},{8,10},{9,11},{10,... | collective-permute-start | bytes 73736 | tf_op jit(solution)/shard_map/ppermute | solution.py:529
  30.8 5.7 %collective-permute-start.5 = (bf16[64,192]{1,0:T(8,128)(2,1)S(1)}, bf16[64,192]{1,0:T(8,128)(2,1)S(1)}, u32[]{:S(2)}, u32[]{:S(2)}) collective-permute-start(bf16[64,192]{1,0:T(8,128)(2,1)S(1)} %get-tuple-element.45), channel_id=1, source_target_pairs={{0,3},{1,2},{2,1},{3,0},{4,7},{5,6},{6,5},{7,4},{8,11},{9,10},{10,... | collective-permute-start | bytes 73736 | tf_op jit(solution)/shard_map/ppermute | solution.py:529
  44.9 1.3 %collective-permute-start.6 = (bf16[64,384]{1,0:T(8,128)(2,1)S(1)}, bf16[64,384]{1,0:T(8,128)(2,1)S(1)}, u32[]{:S(2)}, u32[]{:S(2)}) collective-permute-start(bf16[64,384]{1,0:T(8,128)(2,1)S(1)} %get-tuple-element.61), channel_id=1, source_target_pairs={{0,4},{4,0},{8,12},{12,8},{1,5},{5,1},{9,13},{13,9},{2,6},{6,2},{1... | collective-permute-start | bytes 147464 | tf_op jit(solution)/shard_map/ppermute | solution.py:529
  46.3 4.2 %collective-permute-start.7 = (bf16[64,384]{1,0:T(8,128)(2,1)S(1)}, bf16[64,384]{1,0:T(8,128)(2,1)S(1)}, u32[]{:S(2)}, u32[]{:S(2)}) collective-permute-start(bf16[64,384]{1,0:T(8,128)(2,1)S(1)} %add_convert_fusion.3), channel_id=1, source_target_pairs={{0,8},{4,12},{8,0},{12,4},{1,9},{5,13},{9,1},{13,5},{2,10},{6,14},... | collective-permute-start | bytes 147464 | tf_op jit(solution)/shard_map/ppermute | solution.py:529
  50.4 4.2 %collective-permute-start.8 = (bf16[64,384]{1,0:T(8,128)(2,1)S(1)}, bf16[64,384]{1,0:T(8,128)(2,1)S(1)}, u32[]{:S(2)}, u32[]{:S(2)}) collective-permute-start(bf16[64,384]{1,0:T(8,128)(2,1)S(1)} %add_convert_fusion.2), channel_id=1, source_target_pairs={{0,1},{1,0},{2,3},{3,2},{4,5},{5,4},{6,7},{7,6},{8,9},{9,8},{10,11... | collective-permute-start | bytes 147464 | tf_op jit(solution)/shard_map/ppermute | solution.py:529
  54.6 5.1 %collective-permute-start.9 = (bf16[64,384]{1,0:T(8,128)(2,1)S(1)}, bf16[64,384]{1,0:T(8,128)(2,1)S(1)}, u32[]{:S(2)}, u32[]{:S(2)}) collective-permute-start(bf16[64,384]{1,0:T(8,128)(2,1)S(1)} %add_convert_fusion.1), channel_id=1, source_target_pairs={{0,2},{1,3},{2,0},{3,1},{4,6},{5,7},{6,4},{7,5},{8,10},{9,11},{10,... | collective-permute-start | bytes 147464 | tf_op jit(solution)/shard_map/ppermute | solution.py:529
  59.7 1.3 %collective-permute-start.10 = (bf16[64,384]{1,0:T(8,128)(2,1)S(1)}, bf16[64,384]{1,0:T(8,128)(2,1)S(1)}, u32[]{:S(2)}, u32[]{:S(2)}) collective-permute-start(bf16[64,384]{1,0:T(8,128)(2,1)S(1)} %add_convert_fusion.mine_ref), channel_id=1, source_target_pairs={{0,4},{4,0},{8,12},{12,8},{1,5},{5,1},{9,13},{13,9},{2,6},{6,2},{1... | collective-permute-start | bytes 147464 | tf_op jit(solution)/shard_map/ppermute | solution.py:529
where the time goes:
time: 61.9 us; the launch traced here: 61.8 us
  Pallas kernels  26.9 us (43%)
  waiting for transfers between devices  19.1 us (31%)
  starting transfers between devices  14.1 us (23%)
  between operations  0.8 us (1%)
  local copies, waits for them, and re-layouts  0.79 us (1%)
    pallas_call x3, Pallas kernels, call(): pl.pallas_call(functools.partial(kernel, plan, side), out_shape=out_shape...  26.1 us
    ppermute x11, waiting for transfers between devices, swap(): lax.ppermute(x, axis, [(i, i ^ step) for i in range(lax.axis_size(axis))])  19.1 us
    ppermute x11, starting transfers between devices, swap(): lax.ppermute(x, axis, [(i, i ^ step) for i in range(lax.axis_size(axis))])  14.1 us
  transfers between devices with their start and end apart: 11, of which 9 were waited for; matrix products, arithmetic and copies ran while one was open for 1% of the time, Pallas kernels for 0%

commit v1 on v0

--- a/solution.py
+++ b/solution.py
@@ -14,7 +14,9 @@
 SUB = 8
 LOG2E = 1.4426950408889634
 LN2 = 0.6931471805599453
-VMEM_LIMIT = 34 * 2**20
+VMEM_LIMIT = 8 * 2**20
+VMEM_SPARE = 4 * 2**20
+PER = 8
 
 
 def dot(a, b, dims=((1,), (0,))):
@@ -147,22 +149,21 @@
     dt = soft * t["m"][...]
     t["dt"][...] = dt
     t["dtu"][...] = dt * t["u"][...]
-    spread(plan, t)
+
+
+def own_lanes(plan, r, width):
+    lane = lax.broadcasted_iota(jnp.int32, (plan.rows, width), 1) % plan.half
+    return lane == plan.rank + r
 
 
 def spread(plan, t):
     k = lax.broadcasted_iota(jnp.int32, (2 * LANES, 2 * LANES), 0) % LANES
     l = lax.broadcasted_iota(jnp.int32, (2 * LANES, 2 * LANES), 1)
     ones = jnp.where((k < plan.half) == (l < LANES), 1.0, 0.0).astype(BF16)
-    proj = t["p"][...]
-    hi = proj.astype(BF16).astype(F32)
-    lo = proj - hi
-    lane = lane_iota(plan.rows)
+    hi = t["p"][...].astype(BF16).astype(F32)
+    both = jnp.concatenate([hi, t["p"][...] - hi], axis=1)
     for r in range(2 * plan.states):
-        at = plan.rank + r
-        mine = (lane == at) | (lane == at + plan.half)
-        lhs = jnp.concatenate([jnp.where(mine, hi, 0.0), jnp.where(mine, lo, 0.0)], axis=1).astype(BF16)
-        t["bb"][r] = dot(lhs, ones)
+        t["bc"][r] = dot(jnp.where(own_lanes(plan, r, 2 * LANES), both, 0.0).astype(BF16), ones)
 
 
 def fold(x):
@@ -176,19 +177,15 @@
     l = lax.broadcasted_iota(jnp.int32, (2 * LANES, LANES), 1)
     first = (k < plan.half) | (k >= LANES + plan.half)
     ones = jnp.where(first == (l < plan.half), 1.0, 0.0).astype(BF16)
-    lane = lane_iota(plan.rows)
     out = jnp.zeros((plan.rows, LANES), F32)
     for r in range(2 * plan.states):
-        at = plan.rank + r
-        mine = (lane == at) | (lane == at + plan.half)
-        out = jnp.where(mine, dot(t["prod"][r].astype(BF16), ones), out)
+        out = jnp.where(own_lanes(plan, r, LANES), dot(t["prod"][r].astype(BF16), ones), out)
     return out
 
 
 def coefs(plan, t, row, n, which):
-    r = which * plan.states + n
-    lo = t["bb"][r, pl.ds(row, SUB), 0:LANES]
-    hi = t["bb"][r, pl.ds(row, SUB), LANES:]
+    lo = t["bc"][which * plan.states + n, pl.ds(row, SUB), 0:LANES]
+    hi = t["bc"][which * plan.states + n, pl.ds(row, SUB), LANES:]
     mid = jnp.where(lane_iota(SUB) < plan.half, lo, hi)
     return jnp.concatenate([lo, mid, hi], axis=1)
 
@@ -240,10 +237,11 @@
 
 
 def forward(plan, w, t, keep_states):
-    nst, per = plan.states, 8
+    nst = plan.states
     zero = jnp.zeros((SUB, 3 * LANES), F32)
-    for n0 in range(0, nst, per):
-        ns = list(range(n0, n0 + per))
+    spread(plan, t)
+    for n0 in range(0, nst, PER):
+        ns = list(range(n0, n0 + PER))
 
         def group(g, ns=ns, n0=n0):
             start = tuple(zero for _ in ns)
@@ -251,9 +249,12 @@
 
                 def local(s, row, hs):
                     dt, dtu = t["dt"][pl.ds(row, SUB), :], t["dtu"][pl.ds(row, SUB), :]
-                    return tuple(
-                        jnp.exp2(dt * w["rate"][n]) * h + coefs(plan, t, row, n, 0) * dtu for n, h in zip(ns, hs)
-                    )
+                    new = []
+                    for n, h in zip(ns, hs):
+                        a = jnp.exp2(dt * w["rate"][n])
+                        t["a"][s, n] = a
+                        new.append(a * h + coefs(plan, t, row, n, 0) * dtu)
+                    return tuple(new)
 
                 ends = over_steps(plan, g, local, start)
                 start = tuple(chunk_scan(d, e, False) for d, e in zip(chunk_decay(plan, w, t, ns), ends))
@@ -266,7 +267,8 @@
                 y = t["u"][pl.ds(row, SUB), :] * w["small"][SUB : SUB + 1, :] if n0 == 0 else t["y"][pl.ds(row, SUB), :]
                 new = []
                 for n, h in zip(ns, hs):
-                    h = jnp.exp2(dt * w["rate"][n]) * h + coefs(plan, t, row, n, 0) * dtu
+                    a = t["a"][s, n] if plan.chunked else jnp.exp2(dt * w["rate"][n])
+                    h = a * h + coefs(plan, t, row, n, 0) * dtu
                     y = y + coefs(plan, t, row, n, 1) * h
                     if keep_states:
                         t["h"][s + 1, n, pl.ds(g * SUB, SUB), :] = h
@@ -290,10 +292,8 @@
             if plan.chunked:
 
                 def local(s, row, gs):
-                    dt, gy = t["dt"][pl.ds(row, SUB), :], t["gy"][pl.ds(row, SUB), :]
-                    return tuple(
-                        jnp.exp2(dt * w["rate"][n]) * (coefs(plan, t, row, n, 1) * gy + c) for n, c in zip(ns, gs)
-                    )
+                    gy = t["gy"][pl.ds(row, SUB), :]
+                    return tuple(t["a"][s, n] * (coefs(plan, t, row, n, 1) * gy + c) for n, c in zip(ns, gs))
 
                 ends = over_steps(plan, g, local, start, backwards=True)
                 start = tuple(chunk_scan(d, e, True) for d, e in zip(chunk_decay(plan, w, t, ns), ends))
@@ -314,7 +314,8 @@
                     t["prod"][n, pl.ds(row, SUB), :] = fold(gh * dtu)
                     t["prod"][nst + n, pl.ds(row, SUB), :] = fold(gy * h_now)
                     sb = sb + gh * coefs(plan, t, row, n, 0)
-                    c = jnp.exp2(dt * w["rate"][n]) * gh
+                    a = t["a"][s, n] if plan.chunked else jnp.exp2(dt * w["rate"][n])
+                    c = a * gh
                     q = c * h_prev
                     wq = wq + q * w["rate"][n]
                     new_g.append(c)
@@ -361,7 +362,7 @@
     grads = jnp.concatenate(blocks, axis=0)
     gu = sb * dt + gy * w["small"][SUB : SUB + 1, :] + dot(gp_b, w["x"][...].astype(BF16))
     tiles = [gu[:, k * LANES : (k + 1) * LANES] for k in range(3)]
-    return grads, unplace(plan, back_ref, tiles, t["stack"])
+    return grads, unplace(plan, back_ref, tiles, t.get("stack"))
 
 
 def weight_shapes(plan):
@@ -375,13 +376,17 @@
 
 
 def token_shapes(plan):
-    wide, narrow = (plan.rows, 3 * LANES), (plan.rows, LANES)
+    wide, narrow, double = (plan.rows, 3 * LANES), (plan.rows, LANES), (plan.rows, 2 * LANES)
     kept = {"u": wide, "m": wide, "z": wide, "dt": wide, "dtu": wide, "p": narrow,
-            "bb": (2 * plan.states, plan.rows, 2 * LANES),
+            "bc": (2 * plan.states,) + double,
             "h": (plan.steps + 1, plan.states, plan.lines, 3 * LANES)}
-    own = {"y": wide, "stack": (2 * plan.rows, 2 * LANES), "x256": (plan.rows, 2 * LANES)}
-    grads = {"gy": wide, "sb": wide, "wq": wide, "prod": (2 * plan.states, plan.rows, 2 * LANES),
-             "gr": (plan.states, SUB, 3 * LANES), "x256": (plan.rows, 2 * LANES), "stack": (2 * plan.rows, 2 * LANES)}
+    if plan.chunked:
+        kept["a"] = (plan.steps, plan.states, plan.lines, 3 * LANES)
+    own = {"y": wide, "x256": double}
+    grads = {"gy": wide, "sb": wide, "wq": wide, "prod": (2 * plan.states,) + double,
+             "gr": (plan.states, SUB, 3 * LANES), "x256": double}
+    if plan.chunked:
+        own["stack"] = grads["stack"] = (2 * plan.rows, 2 * LANES)
     return kept, own, grads
 
 
@@ -439,7 +444,7 @@
     prepare(plan, perm_ref, masked_rows(plan, tissue_ref, feat_ref), w, t)
     forward(plan, w, t, True)
     tiles = [t["y"][:, k * LANES : (k + 1) * LANES] for k in range(3)]
-    a, b = unplace(plan, back_ref, tiles, t["stack"])
+    a, b = unplace(plan, back_ref, tiles, t.get("stack"))
     mask = token_mask(plan, tissue_ref, (plan.rows, LANES), 0)
     send_blocks(send_refs, (a, jnp.where(lane_iota(plan.rows) < plan.half, b, mask)), t["x256"], 2 * LANES)
 
@@ -507,7 +512,8 @@
     specs = list(jax.tree.map(lambda _: whole, tuple(args)))
     if scalars:
         specs[0] = pl.BlockSpec(memory_space=pltpu.SMEM)
-    scratches = [{k: pltpu.VMEM(v, F32) for k, v in scratch.items()}]
+    scratches = [arrays(scratch, pltpu.VMEM)]
+    limit = VMEM_SPARE + sum(int(np.prod(x.shape)) * x.dtype.itemsize for x in jax.tree.leaves(arrays(scratch)))
     if far:
         args = [pltpu.with_memory_space_constraint(a, pltpu.HBM) if k in far else a for k, a in enumerate(args)]
         for k in far:
@@ -517,12 +523,15 @@
         functools.partial(kernel, plan, side), out_shape=out_shape, in_specs=tuple(specs),
         out_specs=jax.tree.map(lambda _: whole, out_shape), scratch_shapes=scratches,
         name=name, cost_estimate=pl.CostEstimate(flops=cost * 10**6, bytes_accessed=4 * 10**6, transcendentals=0),
-        compiler_params=pltpu.CompilerParams(vmem_limit_bytes=VMEM_LIMIT),
+        compiler_params=pltpu.CompilerParams(vmem_limit_bytes=limit),
     )(*args)
 
 
-def arrays(shapes):
-    return {k: jax.ShapeDtypeStruct(v, F32) for k, v in shapes.items()}
+def arrays(shapes, make=jax.ShapeDtypeStruct):
+    def one(shape):
+        return make(shape, F32) if isinstance(shape[-1], int) else make(shape[:-1], shape[-1])
+
+    return jax.tree.map(one, shapes, is_leaf=lambda x: isinstance(x, tuple))
 
 
 def swap(x, axis, step):
@@ -538,7 +547,8 @@
     if len(blocks) == 1:
         block = blocks[0].reshape(bands, rows // bands, -1)
         return [lax.all_to_all(block, "band", split_axis=0, concat_axis=0, tiled=True).reshape(rows, -1)]
-    return [blocks[0]] + [swap(blocks[s], "band", s) for s in range(1, bands)]
+    got = {s: swap(blocks[s], "band", s) for s in reversed(range(1, bands))}
+    return [blocks[0]] + [got[s] for s in range(1, bands)]
 
 
 def shards(features, tissue, cotangent, x_proj, dt_proj, dt_bias, a_log, d_skip):
@@ -581,6 +591,10 @@
     mine = (mine.astype(F32) + swap(theirs, "slide", 1).astype(F32)).astype(BF16)
     for axis in ("slide", "band"):
         step = 2 if axis == "slide" else 1
+        if axis == "band" and lax.axis_size(axis) == 4:
+            far = [swap(mine, axis, s).astype(F32) for s in (3, 2, 1)]
+            mine = ((mine.astype(F32) + far[2]) + (far[1] + far[0])).astype(BF16)
+            continue
         while step < lax.axis_size(axis):
             mine = exchange(mine, axis, step)
             step *= 2

time: 61.9 us -> 60.2 us (0.973)
  waiting for transfers between devices: 19.1 us -> 16.3 us
  starting transfers between devices: 14.1 us -> 16.3 us
  Pallas kernels: 26.9 us -> 25.9 us
    ppermute x11 -> x12, waiting for transfers between devices: 19.1 us -> 16.3 us  [swap(): lax.ppermute(x, axis, [(i, i ^ step) for i in range(lax.axis_size(axis))])]
    ppermute x11 -> x12, starting transfers between devices: 14.1 us -> 16.3 us  [swap(): lax.ppermute(x, axis, [(i, i ^ step) for i in range(lax.axis_size(axis))])]
    pallas_call x3, Pallas kernels: 26.1 us -> 25.1 us  [call(): pl.pallas_call(functools.partial(kernel, plan, side), out_shape=out_shape...]
  transfers between devices with their start and end apart: 11 -> 12, of which waited for: 9 -> 9; matrix products, arithmetic and copies ran while one was open for 1% -> 1% of each run, Pallas kernels for 0% -> 0%
where the time goes in v1:
time: 60.2 us; the launch traced here: 60.1 us
  Pallas kernels  25.9 us (43%)
  starting transfers between devices  16.3 us (27%)
  waiting for transfers between devices  16.3 us (27%)
  local copies, waits for them, and re-layouts  0.79 us (1%)
  between operations  0.79 us (1%)
    pallas_call x3, Pallas kernels, call(): pl.pallas_call(functools.partial(kernel, plan, side), out_shape=out_shape...  25.1 us
    ppermute x12, waiting for transfers between devices, swap(): lax.ppermute(x, axis, [(i, i ^ step) for i in range(lax.axis_size(axis))])  16.3 us
    ppermute x12, starting transfers between devices, swap(): lax.ppermute(x, axis, [(i, i ^ step) for i in range(lax.axis_size(axis))])  16.3 us
  transfers between devices with their start and end apart: 12, of which 9 were waited for; matrix products, arithmetic and copies ran while one was open for 1% of the time, Pallas kernels for 0%

profile of v1, /device:TPU:0, one launch (start us, length us, event | category | flops | bytes accessed | tf_op | source)
XLA Modules:
  0.0 60.1 jit_solution(2388578407253889780)
XLA Ops:
  0.6 0.0 copy-start
  0.6 0.0 copy-start.1
  0.7 0.0 copy-start.2
  0.7 0.0 copy-start.3
  0.7 0.0 copy-start.4
  0.7 0.0 copy-start.5
  0.7 6.9 %rows_forward.1 = (bf16[64,256]{1,0:T(8,128)(2,1)S(1)}, bf16[64,256]{1,0:T(8,128)(2,1)S(1)}, bf16[64,256]{1,0:T(8,128)(2,1)S(1)}, bf16[64,256]{1,0:T(8,128)(2,1)...) custom-call(s32[2]{0:T(128)} %bitcast.17, ...), custom_call_target="tpu_custom_call" | custom-call | flops 4000000000 | bytes 4000000 | tf_op jit(solution)/shard_map/rows_forward/pallas_call | solution.py:522
  7.6 3.1 %collective-permute-start = (bf16[64,256]{1,0:T(8,128)(2,1)S(1)}, bf16[64,256]{1,0:T(8,128)(2,1)S(1)}, u32[]{:S(2)}, u32[]{:S(2)}) collective-permute-start(bf16[64,256]{1,0:T(8,128)(2,1)S(1)} %get-tuple-element.39), channel_id=1, source_target_pairs={{0,1},{1,0},{2,3},{3,2},{4,5},{5,4},{6,7},{7,6},{8,9},{9,8},{10,11... | collective-permute-start | bytes 98312 | tf_op jit(solution)/shard_map/ppermute | solution.py:538
  10.7 2.6 %collective-permute-start.1 = (bf16[64,256]{1,0:T(8,128)(2,1)S(1)}, bf16[64,256]{1,0:T(8,128)(2,1)S(1)}, u32[]{:S(2)}, u32[]{:S(2)}) collective-permute-start(bf16[64,256]{1,0:T(8,128)(2,1)S(1)} %get-tuple-element.40), channel_id=1, source_target_pairs={{0,2},{1,3},{2,0},{3,1},{4,6},{5,7},{6,4},{7,5},{8,10},{9,11},{10,... | collective-permute-start | bytes 98312 | tf_op jit(solution)/shard_map/ppermute | solution.py:538
  13.3 0.0 collective-permute-start.2
  13.3 0.0 collective-permute-done.recv_refs_1_
  13.3 2.8 %collective-permute-done.1.recv_refs_2_ = bf16[64,256]{1,0:T(8,128)(2,1)S(1)} collective-permute-done((bf16[64,256]{1,0:T(8,128)(2,1)S(1)}, bf16[64,256]{1,0:T(8,128)(2,1)S(1)}, u32[]{:S(2)}, u32[]{:S(2)}) %collective-permute-start.1) | collective-permute-done | bytes 32800 | tf_op jit(solution)/shard_map/ppermute | solution.py:538
  16.1 2.9 %collective-permute-done.2.recv_refs_3_ = bf16[64,256]{1,0:T(8,128)(2,1)S(1)} collective-permute-done((bf16[64,256]{1,0:T(8,128)(2,1)S(1)}, bf16[64,256]{1,0:T(8,128)(2,1)S(1)}, u32[]{:S(2)}, u32[]{:S(2)}) %collective-permute-start.2) | collective-permute-done | bytes 32800 | tf_op jit(solution)/shard_map/ppermute | solution.py:538
  19.0 0.0 copy-done
  19.0 0.0 copy-done.1
  19.0 0.0 copy-done.2
  19.0 0.0 copy-done.3
  19.0 0.0 copy-done.4
  19.0 0.0 copy-done.5
  19.0 0.0 copy-start.6
  19.1 0.0 copy-start.7
  19.1 0.0 copy-start.8
  19.1 10.2 %columns.1 = (bf16[256,192]{1,0:T(8,128)(2,1)}, bf16[64,192]{1,0:T(8,128)(2,1)S(1)}, bf16[64,192]{1,0:T(8,128)(2,1)S(1)}, bf16[64,192]{1,0:T(8,128)(2,1)S(1)}, b...) custom-call(bf16[64,256]{1,0:T(8,128)(2,1)S(1)} %get-tuple-element.38.recv_refs_0_, ...), custom_call_target="tpu_custom_call" | custom-call | flops 8000000000 | bytes 4000000 | tf_op jit(solution)/shard_map/columns/pallas_call | solution.py:522
  29.3 0.0 collective-permute-start.3
  29.3 0.9 %collective-permute-start.4 = (bf16[64,192]{1,0:T(8,128)(2,1)S(1)}, bf16[64,192]{1,0:T(8,128)(2,1)S(1)}, u32[]{:S(2)}, u32[]{:S(2)}) collective-permute-start(bf16[64,192]{1,0:T(8,128)(2,1)S(1)} %get-tuple-element.45), channel_id=1, source_target_pairs={{0,2},{1,3},{2,0},{3,1},{4,6},{5,7},{6,4},{7,5},{8,10},{9,11},{10,... | collective-permute-start | bytes 73736 | tf_op jit(solution)/shard_map/ppermute | solution.py:538
  30.2 3.5 %collective-permute-start.5 = (bf16[64,192]{1,0:T(8,128)(2,1)S(1)}, bf16[64,192]{1,0:T(8,128)(2,1)S(1)}, u32[]{:S(2)}, u32[]{:S(2)}) collective-permute-start(bf16[64,192]{1,0:T(8,128)(2,1)S(1)} %get-tuple-element.46), channel_id=1, source_target_pairs={{0,3},{1,2},{2,1},{3,0},{4,7},{5,6},{6,5},{7,4},{8,11},{9,10},{10,... | collective-permute-start | bytes 73736 | tf_op jit(solution)/shard_map/ppermute | solution.py:538
  33.7 0.0 collective-permute-done.3.gy_refs_1_
  33.7 0.4 collective-permute-done.4.gy_refs_2_
  34.1 1.8 %collective-permute-done.5.gy_refs_3_ = bf16[64,192]{1,0:T(8,128)(2,1)S(1)} collective-permute-done((bf16[64,192]{1,0:T(8,128)(2,1)S(1)}, bf16[64,192]{1,0:T(8,128)(2,1)S(1)}, u32[]{:S(2)}, u32[]{:S(2)}) %collective-permute-start.5) | collective-permute-done | bytes 24608 | tf_op jit(solution)/shard_map/ppermute | solution.py:538
  35.9 0.0 copy-done.6
  35.9 0.0 copy-done.7
  35.9 0.0 copy-done.8
  35.9 8.0 %rows_backward.1 = (bf16[256,192]{1,0:T(8,128)(2,1)S(1)}, bf16[64,384]{1,0:T(8,128)(2,1)S(1)}, bf16[64,384]{1,0:T(8,128)(2,1)S(1)}) custom-call(s32[2]{0:T(128)S(1)} %bitcast.18, bf16[64,192]{1,0:T(8,128)(2,1)S(1)} %get-tuple-element.43.gy_refs_0_, bf16[64,192]{1,0:T(8,128)(2,1)S(1)} %collective-permute-done.3.gy_refs_1_, ...), custom_call_target="tpu_custom_call" | custom-call | flops 8000000000 | bytes 4000000 | tf_op jit(solution)/shard_map/rows_backward/pallas_call | solution.py:522
  43.9 0.1 collective-permute-start.6
  44.0 1.2 %collective-permute-done.6 = bf16[64,384]{1,0:T(8,128)(2,1)S(1)} collective-permute-done((bf16[64,384]{1,0:T(8,128)(2,1)S(1)}, bf16[64,384]{1,0:T(8,128)(2,1)S(1)}, u32[]{:S(2)}, u32[]{:S(2)}) %collective-permute-start.6) | collective-permute-done | bytes 49184 | tf_op jit(solution)/shard_map/ppermute | solution.py:538
  45.2 1.6 %collective-permute-start.7 = (bf16[64,384]{1,0:T(8,128)(2,1)S(1)}, bf16[64,384]{1,0:T(8,128)(2,1)S(1)}, u32[]{:S(2)}, u32[]{:S(2)}) collective-permute-start(bf16[64,384]{1,0:T(8,128)(2,1)S(1)} %add_convert_fusion.2), channel_id=1, source_target_pairs={{0,8},{4,12},{8,0},{12,4},{1,9},{5,13},{9,1},{13,5},{2,10},{6,14},... | collective-permute-start | bytes 147464 | tf_op jit(solution)/shard_map/ppermute | solution.py:538
  46.8 2.6 %collective-permute-done.7 = bf16[64,384]{1,0:T(8,128)(2,1)S(1)} collective-permute-done((bf16[64,384]{1,0:T(8,128)(2,1)S(1)}, bf16[64,384]{1,0:T(8,128)(2,1)S(1)}, u32[]{:S(2)}, u32[]{:S(2)}) %collective-permute-start.7) | collective-permute-done | bytes 49184 | tf_op jit(solution)/shard_map/ppermute | solution.py:538
  49.4 3.5 %collective-permute-start.10 = (bf16[64,384]{1,0:T(8,128)(2,1)S(1)}, bf16[64,384]{1,0:T(8,128)(2,1)S(1)}, u32[]{:S(2)}, u32[]{:S(2)}) collective-permute-start(bf16[64,384]{1,0:T(8,128)(2,1)S(1)} %add_convert_fusion.1), channel_id=1, source_target_pairs={{0,3},{1,2},{2,1},{3,0},{4,7},{5,6},{6,5},{7,4},{8,11},{9,10},{10,... | collective-permute-start | bytes 147464 | tf_op jit(solution)/shard_map/ppermute | solution.py:538
  53.0 0.0 collective-permute-start.9
  53.0 0.9 %collective-permute-start.8 = (bf16[64,384]{1,0:T(8,128)(2,1)S(1)}, bf16[64,384]{1,0:T(8,128)(2,1)S(1)}, u32[]{:S(2)}, u32[]{:S(2)}) collective-permute-start(bf16[64,384]{1,0:T(8,128)(2,1)S(1)} %add_convert_fusion.1), channel_id=1, source_target_pairs={{0,1},{1,0},{2,3},{3,2},{4,5},{5,4},{6,7},{7,6},{8,9},{9,8},{10,11... | collective-permute-start | bytes 147464 | tf_op jit(solution)/shard_map/ppermute | solution.py:538
  53.9 1.5 %collective-permute-done.10 = bf16[64,384]{1,0:T(8,128)(2,1)S(1)} collective-permute-done((bf16[64,384]{1,0:T(8,128)(2,1)S(1)}, bf16[64,384]{1,0:T(8,128)(2,1)S(1)}, u32[]{:S(2)}, u32[]{:S(2)}) %collective-permute-start.10) | collective-permute-done | bytes 49184 | tf_op jit(solution)/shard_map/ppermute | solution.py:538
  55.4 2.6 %collective-permute-done.9 = bf16[64,384]{1,0:T(8,128)(2,1)S(1)} collective-permute-done((bf16[64,384]{1,0:T(8,128)(2,1)S(1)}, bf16[64,384]{1,0:T(8,128)(2,1)S(1)}, u32[]{:S(2)}, u32[]{:S(2)}) %collective-permute-start.9) | collective-permute-done | bytes 49184 | tf_op jit(solution)/shard_map/ppermute | solution.py:538
  57.9 0.0 collective-permute-done.8
  58.0 0.1 collective-permute-start.11
  58.1 0.7 %copy.17 = bf16[1,1,256,192]{2,3,1,0:T(8,128)(2,1)} copy(bf16[1,1,256,192]{3,2,1,0:T(8,128)(2,1)S(1)} %bitcast.11) | data formatting | bytes 196608
  58.8 0.5 collective-permute-done.11.theirs_ref
  59.3 0.8 %unpack.1 = (f32[38,4,192]{2,1,0:T(4,128)}, f32[6,4,192]{2,1,0:T(4,128)}, f32[4,192]{1,0:T(4,128)}, f32[4,16,192]{2,1,0:T(8,128)}, f32[4,192]{1,0:T(4,128)}) custom-call(bf16[64,384]{1,0:T(8,128)(2,1)S(1)} %add_convert_fusion.mine_ref, bf16[64,384]{1,0:T(8,128)(2,1)S(1)} %collective-permute-done.11.theirs_ref), custom_call_target="tpu_custom_call" | custom-call | tf_op jit(solution)/shard_map/unpack/pallas_call | solution.py:603
  (3 shorter events, 0.1 us)
Async XLA Ops:
  0.6 18.4 %copy-start = (f32[4,192,38]{1,0,2:T(4,128)S(1)}, f32[4,192,38]{1,0,2:T(4,128)}, u32[]{:S(2)}) copy-start(f32[4,192,38]{1,0,2:T(4,128)} %param.13) | copy-start | bytes 350212
  0.6 18.4 %copy-start.1 = (bf16[1,4,64,192]{3,2,1,0:T(8,128)(2,1)S(1)}, bf16[1,4,64,192]{3,2,1,0:T(8,128)(2,1)}, u32[]{:S(2)}) copy-start(bf16[1,4,64,192]{3,2,1,0:T(8,128)(2,1)} %param.12) | copy-start | bytes 294916
  0.7 18.4 %copy-start.2 = (f32[4,16,192]{2,1,0:T(8,128)S(1)}, f32[4,16,192]{2,1,0:T(8,128)}, u32[]{:S(2)}) copy-start(f32[4,16,192]{2,1,0:T(8,128)} %alog_ref.1) | copy-start | bytes 147460
  0.7 18.3 %copy-start.3 = (f32[4,6,192]{2,0,1:T(4,128)S(1)}, f32[4,6,192]{2,0,1:T(4,128)}, u32[]{:S(2)}) copy-start(f32[4,6,192]{2,0,1:T(4,128)} %param.14) | copy-start | bytes 55300
  0.7 18.3 %copy-start.4 = (f32[4,192]{1,0:T(4,128)S(1)}, f32[4,192]{1,0:T(4,128)}, u32[]{:S(2)}) copy-start(f32[4,192]{1,0:T(4,128)} %bias_ref.1) | copy-start | bytes 9220
  0.7 18.3 %copy-start.5 = (f32[4,192]{1,0:T(4,128)S(1)}, f32[4,192]{1,0:T(4,128)}, u32[]{:S(2)}) copy-start(f32[4,192]{1,0:T(4,128)} %skip_ref.1) | copy-start | bytes 9220
  7.6 5.7 %collective-permute-start = (bf16[64,256]{1,0:T(8,128)(2,1)S(1)}, bf16[64,256]{1,0:T(8,128)(2,1)S(1)}, u32[]{:S(2)}, u32[]{:S(2)}) collective-permute-start(bf16[64,256]{1,0:T(8,128)(2,1)S(1)} %get-tuple-element.39), channel_id=1, source_target_pairs={{0,1},{1,0},{2,3},{3,2},{4,5},{5,4},{6,7},{7,6},{8,9},{9,8},{10,11... | collective-permute-start | bytes 98312 | tf_op jit(solution)/shard_map/ppermute | solution.py:538
  10.7 5.4 %collective-permute-start.1 = (bf16[64,256]{1,0:T(8,128)(2,1)S(1)}, bf16[64,256]{1,0:T(8,128)(2,1)S(1)}, u32[]{:S(2)}, u32[]{:S(2)}) collective-permute-start(bf16[64,256]{1,0:T(8,128)(2,1)S(1)} %get-tuple-element.40), channel_id=1, source_target_pairs={{0,2},{1,3},{2,0},{3,1},{4,6},{5,7},{6,4},{7,5},{8,10},{9,11},{10,... | collective-permute-start | bytes 98312 | tf_op jit(solution)/shard_map/ppermute | solution.py:538
  13.3 5.7 %collective-permute-start.2 = (bf16[64,256]{1,0:T(8,128)(2,1)S(1)}, bf16[64,256]{1,0:T(8,128)(2,1)S(1)}, u32[]{:S(2)}, u32[]{:S(2)}) collective-permute-start(bf16[64,256]{1,0:T(8,128)(2,1)S(1)} %get-tuple-element.41), channel_id=1, source_target_pairs={{0,3},{1,2},{2,1},{3,0},{4,7},{5,6},{6,5},{7,4},{8,11},{9,10},{10,... | collective-permute-start | bytes 98312 | tf_op jit(solution)/shard_map/ppermute | solution.py:538
  19.0 16.9 %copy-start.6 = (s32[1,1,2]{2,1,0:T(1,128)S(1)}, s32[1,1,2]{2,1,0:T(1,128)}, u32[]{:S(2)}) copy-start(s32[1,1,2]{2,1,0:T(1,128)} %param.11) | copy-start | bytes 28
  19.1 16.9 %copy-start.7 = (bf16[256,512]{1,0:T(8,128)(2,1)S(1)}, bf16[256,512]{1,0:T(8,128)(2,1)}, u32[]{:S(2)}) copy-start(bf16[256,512]{1,0:T(8,128)(2,1)} %constant.5.clone.refs_3_.back_ref) | copy-start | bytes 786436
  19.1 16.9 %copy-start.8 = (bf16[256,512]{1,0:T(8,128)(2,1)S(1)}, bf16[256,512]{1,0:T(8,128)(2,1)}, u32[]{:S(2)}) copy-start(bf16[256,512]{1,0:T(8,128)(2,1)} %constant.4.clone.refs_2_.perm_ref) | copy-start | bytes 786436
  29.3 4.4 %collective-permute-start.3 = (bf16[64,192]{1,0:T(8,128)(2,1)S(1)}, bf16[64,192]{1,0:T(8,128)(2,1)S(1)}, u32[]{:S(2)}, u32[]{:S(2)}) collective-permute-start(bf16[64,192]{1,0:T(8,128)(2,1)S(1)} %get-tuple-element.44), channel_id=1, source_target_pairs={{0,1},{1,0},{2,3},{3,2},{4,5},{5,4},{6,7},{7,6},{8,9},{9,8},{10,11... | collective-permute-start | bytes 73736 | tf_op jit(solution)/shard_map/ppermute | solution.py:538
  29.3 4.8 %collective-permute-start.4 = (bf16[64,192]{1,0:T(8,128)(2,1)S(1)}, bf16[64,192]{1,0:T(8,128)(2,1)S(1)}, u32[]{:S(2)}, u32[]{:S(2)}) collective-permute-start(bf16[64,192]{1,0:T(8,128)(2,1)S(1)} %get-tuple-element.45), channel_id=1, source_target_pairs={{0,2},{1,3},{2,0},{3,1},{4,6},{5,7},{6,4},{7,5},{8,10},{9,11},{10,... | collective-permute-start | bytes 73736 | tf_op jit(solution)/shard_map/ppermute | solution.py:538
  30.2 5.7 %collective-permute-start.5 = (bf16[64,192]{1,0:T(8,128)(2,1)S(1)}, bf16[64,192]{1,0:T(8,128)(2,1)S(1)}, u32[]{:S(2)}, u32[]{:S(2)}) collective-permute-start(bf16[64,192]{1,0:T(8,128)(2,1)S(1)} %get-tuple-element.46), channel_id=1, source_target_pairs={{0,3},{1,2},{2,1},{3,0},{4,7},{5,6},{6,5},{7,4},{8,11},{9,10},{10,... | collective-permute-start | bytes 73736 | tf_op jit(solution)/shard_map/ppermute | solution.py:538
  43.9 1.3 %collective-permute-start.6 = (bf16[64,384]{1,0:T(8,128)(2,1)S(1)}, bf16[64,384]{1,0:T(8,128)(2,1)S(1)}, u32[]{:S(2)}, u32[]{:S(2)}) collective-permute-start(bf16[64,384]{1,0:T(8,128)(2,1)S(1)} %get-tuple-element.63), channel_id=1, source_target_pairs={{0,4},{4,0},{8,12},{12,8},{1,5},{5,1},{9,13},{13,9},{2,6},{6,2},{1... | collective-permute-start | bytes 147464 | tf_op jit(solution)/shard_map/ppermute | solution.py:538
  45.2 4.2 %collective-permute-start.7 = (bf16[64,384]{1,0:T(8,128)(2,1)S(1)}, bf16[64,384]{1,0:T(8,128)(2,1)S(1)}, u32[]{:S(2)}, u32[]{:S(2)}) collective-permute-start(bf16[64,384]{1,0:T(8,128)(2,1)S(1)} %add_convert_fusion.2), channel_id=1, source_target_pairs={{0,8},{4,12},{8,0},{12,4},{1,9},{5,13},{9,1},{13,5},{2,10},{6,14},... | collective-permute-start | bytes 147464 | tf_op jit(solution)/shard_map/ppermute | solution.py:538
  49.4 6.0 %collective-permute-start.10 = (bf16[64,384]{1,0:T(8,128)(2,1)S(1)}, bf16[64,384]{1,0:T(8,128)(2,1)S(1)}, u32[]{:S(2)}, u32[]{:S(2)}) collective-permute-start(bf16[64,384]{1,0:T(8,128)(2,1)S(1)} %add_convert_fusion.1), channel_id=1, source_target_pairs={{0,3},{1,2},{2,1},{3,0},{4,7},{5,6},{6,5},{7,4},{8,11},{9,10},{10,... | collective-permute-start | bytes 147464 | tf_op jit(solution)/shard_map/ppermute | solution.py:538
  53.0 5.0 %collective-permute-start.9 = (bf16[64,384]{1,0:T(8,128)(2,1)S(1)}, bf16[64,384]{1,0:T(8,128)(2,1)S(1)}, u32[]{:S(2)}, u32[]{:S(2)}) collective-permute-start(bf16[64,384]{1,0:T(8,128)(2,1)S(1)} %add_convert_fusion.1), channel_id=1, source_target_pairs={{0,2},{1,3},{2,0},{3,1},{4,6},{5,7},{6,4},{7,5},{8,10},{9,11},{10,... | collective-permute-start | bytes 147464 | tf_op jit(solution)/shard_map/ppermute | solution.py:538
  53.0 5.0 %collective-permute-start.8 = (bf16[64,384]{1,0:T(8,128)(2,1)S(1)}, bf16[64,384]{1,0:T(8,128)(2,1)S(1)}, u32[]{:S(2)}, u32[]{:S(2)}) collective-permute-start(bf16[64,384]{1,0:T(8,128)(2,1)S(1)} %add_convert_fusion.1), channel_id=1, source_target_pairs={{0,1},{1,0},{2,3},{3,2},{4,5},{5,4},{6,7},{7,6},{8,9},{9,8},{10,11... | collective-permute-start | bytes 147464 | tf_op jit(solution)/shard_map/ppermute | solution.py:538
  58.0 1.3 %collective-permute-start.11 = (bf16[64,384]{1,0:T(8,128)(2,1)S(1)}, bf16[64,384]{1,0:T(8,128)(2,1)S(1)}, u32[]{:S(2)}, u32[]{:S(2)}) collective-permute-start(bf16[64,384]{1,0:T(8,128)(2,1)S(1)} %add_convert_fusion.mine_ref), channel_id=1, source_target_pairs={{0,4},{4,0},{8,12},{12,8},{1,5},{5,1},{9,13},{13,9},{2,6},{6,2},{1... | collective-permute-start | bytes 147464 | tf_op jit(solution)/shard_map/ppermute | solution.py:538

commit v2 on v1

--- a/solution.py
+++ b/solution.py
@@ -17,6 +17,7 @@
 VMEM_LIMIT = 8 * 2**20
 VMEM_SPARE = 4 * 2**20
 PER = 8
+HOPS = 2
 
 
 def dot(a, b, dims=((1,), (0,))):
@@ -26,6 +27,10 @@
 def split(x):
     hi = x.astype(BF16)
     return hi, (x - hi.astype(F32)).astype(BF16)
+
+
+def lane_tile(k):
+    return slice(k * LANES, (k + 1) * LANES)
 
 
 def swap64(x):
@@ -334,7 +339,7 @@
         over_groups(plan, group)
 
 
-def finish(plan, back_ref, w, t):
+def finish(plan, w, t):
     nst, rank = plan.states, plan.rank
     u, dt, gy, sb = t["u"][...], t["dt"][...], t["gy"][...], t["sb"][...]
     g_dt = t["wq"][...] * LN2 + sb * u
@@ -360,9 +365,12 @@
             part = jnp.where(row == n - n0, jnp.sum(t["gr"][n], axis=0, keepdims=True), part)
         blocks.append(part * w["small"][2 * SUB + n0 : 3 * SUB + n0, :])
     grads = jnp.concatenate(blocks, axis=0)
-    gu = sb * dt + gy * w["small"][SUB : SUB + 1, :] + dot(gp_b, w["x"][...].astype(BF16))
-    tiles = [gu[:, k * LANES : (k + 1) * LANES] for k in range(3)]
-    return grads, unplace(plan, back_ref, tiles, t.get("stack"))
+    return grads, gp_b
+
+
+def input_gradient(plan, back_ref, w, t, gp_b, stack):
+    gu = t["sb"][...] * t["dt"][...] + t["gy"][...] * w["small"][SUB : SUB + 1, :] + dot(gp_b, w["x"][...].astype(BF16))
+    return unplace(plan, back_ref, [gu[:, lane_tile(k)] for k in range(3)], stack)
 
 
 def weight_shapes(plan):
@@ -386,7 +394,7 @@
     grads = {"gy": wide, "sb": wide, "wq": wide, "prod": (2 * plan.states,) + double,
              "gr": (plan.states, SUB, 3 * LANES), "x256": double}
     if plan.chunked:
-        own["stack"] = grads["stack"] = (2 * plan.rows, 2 * LANES)
+        own["stack"] = (2 * plan.rows, 2 * LANES)
     return kept, own, grads
 
 
@@ -413,6 +421,10 @@
 
 def send_blocks(refs, tiles, scratch, width):
     scratch[:, :LANES], scratch[:, LANES:] = tiles
+    send_from(refs, scratch, width)
+
+
+def send_from(refs, scratch, width):
     if len(refs) == 1:
         refs[0][...] = scratch[:, :width].astype(BF16)
         return
@@ -449,20 +461,25 @@
     send_blocks(send_refs, (a, jnp.where(lane_iota(plan.rows) < plan.half, b, mask)), t["x256"], 2 * LANES)
 
 
-def rows_backward_kernel(plan, side, tissue_ref, gy_refs, perm_ref, back_ref, w, kept, grads_v_ref,
-                         out_ref, mine_ref, theirs_ref, rest):
-    t = kept | rest
+def rows_backward_kernel(plan, side, gy_refs, perm_ref, w, kept, grads_v_ref, mine_ref, theirs_ref, late, rest):
+    t = kept | rest | late
     receive_blocks(gy_refs, t["x256"])
     place(plan, perm_ref, t["x256"][...].astype(BF16), t["gy"])
     backward(plan, w, t)
-    grads, (a, b) = finish(plan, back_ref, w, t)
-    mask = token_mask(plan, tissue_ref, (plan.rows, LANES), 0)
-    out_ref[:, :LANES] = (a * mask).astype(BF16)
-    out_ref[:, LANES:] = (b * mask)[:, : plan.channels - LANES].astype(BF16)
+    grads, gp_b = finish(plan, w, t)
+    late["gp"][...] = gp_b
     other = grads_v_ref[...].astype(F32)
     odd = lax.axis_index("slide") % 2 == 1
     mine_ref[...] = jnp.where(odd, other, grads).astype(BF16)
     theirs_ref[...] = jnp.where(odd, grads, other).astype(BF16)
+
+
+def rows_output_kernel(plan, side, tissue_ref, back_ref, w, kept, late, out_ref, own):
+    a, b = input_gradient(plan, back_ref, w, kept | late, late["gp"][...], own["stack"])
+    own["x256"][:, :LANES], own["x256"][:, LANES:] = a, b
+    mask = token_mask(plan, tissue_ref, (SUB, plan.rows), 1)
+    turned = jnp.transpose(own["x256"][...])[: plan.channels]
+    out_ref[...] = (turned * jnp.concatenate([mask] * (plan.channels // SUB), axis=0)).astype(BF16)
 
 
 def columns_kernel(plan, side, recv_refs, gy_ref, x_ref, dtp_ref, bias_ref, alog_ref, skip_ref,
@@ -483,10 +500,252 @@
     mixed_ref[:, :LANES] = a.astype(BF16)
     mixed_ref[:, LANES:] = b[:, : ch - LANES].astype(BF16)
     backward(plan, w, t)
-    grads, (a, b) = finish(plan, None, w, t)
+    grads, gp_b = finish(plan, w, t)
     grads_ref[...] = grads.astype(BF16)
+    a, b = input_gradient(plan, None, w, t, gp_b, None)
     mask = t["m"][:, :LANES]
     send_blocks(out_refs, (a * mask, b * mask), t["x256"], ch)
+
+
+def tall_shapes(plan):
+    steps, ch, nst = plan.steps, plan.channels, plan.states
+    up = -(-(plan.rank + 2 * nst) // SUB) * SUB
+    field = (steps, ch, LANES)
+    ready = {"xs": (2 * up, ch), "ds": (2 * SUB, ch), "al": (2 * (nst + SUB), ch), "rb": (nst + 1, ch, LANES), "gy": field}
+    kept = {"u": field, "bc": (steps, 2 * nst, SUB, LANES), "h": (steps, nst, ch, LANES)}
+    rest = {
+        "z": field, "dt": field, "dtu": field, "sb": field, "wq": field,
+        "m": (steps, SUB, LANES), "p": (steps, up, LANES), "acc": (steps, 2 * nst, SUB, LANES),
+        "a": (steps, nst, ch, LANES), "gr": (nst, ch, LANES),
+        "x256": (plan.rows, 2 * LANES), "pad": (2, up + SUB + nst, 2 * LANES),
+    }
+    return ready, kept, rest
+
+
+def tall_hot(plan):
+    part = plan.states + SUB
+    hot = np.zeros((6 * part, (plan.states + 1) * LANES), np.float32)
+    for k in range(6 * part):
+        d, n = k % (2 * part) // part, k % part
+        if n <= plan.states:
+            at = n * LANES + d * plan.half
+            hot[k, at : at + plan.half] = 1.0
+    return jnp.asarray(hot, BF16)
+
+
+def by_step(plan, tiles):
+    low = lane_iota(tiles[0].shape[0]) < plan.half
+    out = []
+    for s in range(plan.steps):
+        mine, other = tiles[s // 2], tiles[(plan.steps - 1 - s) // 2]
+        out.append(jnp.where(low, mine, other) if s % 2 == 0 else swap64(jnp.where(low, other, mine)))
+    return out
+
+
+def by_row(plan, fields):
+    low = lane_iota(fields[0].shape[0]) < plan.half
+    sums = []
+    for s in range(0, plan.steps, 2):
+        other = plan.steps - 1 - s
+        even = fields[s] + swap64(fields[other])
+        odd = swap64(fields[s + 1]) + fields[other - 1]
+        sums.append(jnp.where(low, even, odd))
+    return jnp.transpose(jnp.concatenate(sums, axis=1))
+
+
+def tall_setup_kernel(plan, side, after_ref, gy_ref, hot_ref, x_ref, dtp_ref, bias_ref, alog_ref, skip_ref, t, own):
+    ch, nst, rank = plan.channels, plan.states, plan.rank
+    wide = rank + 2 * nst
+    up = t["xs"].shape[0] // 2
+    part = nst + SUB
+    t["xs"][...] = jnp.zeros_like(t["xs"])
+    t["ds"][...] = jnp.zeros_like(t["ds"])
+    t["al"][...] = jnp.zeros_like(t["al"])
+    for d in range(2):
+        k = 2 * side + d
+        t["xs"][d * up : d * up + wide, :] = x_ref[:, k, :]
+        t["ds"][d * SUB : d * SUB + rank, :] = dtp_ref[:, k, :]
+        t["ds"][d * SUB + rank : d * SUB + rank + 1, :] = bias_ref[k : k + 1, :]
+        t["al"][d * part : d * part + nst, :] = -jnp.exp(alog_ref[k])
+        t["al"][d * part + nst : d * part + nst + 1, :] = skip_ref[k : k + 1, :]
+    scale = jnp.where(lax.broadcasted_iota(jnp.int32, (2 * part, ch), 0) % part < nst, LOG2E, 1.0)
+    rest = t["al"][...] * scale
+    parts = []
+    for _ in range(3):
+        parts.append(rest.astype(BF16))
+        rest = rest - parts[-1].astype(F32)
+    spread_rates = dot(jnp.concatenate(parts, axis=0), hot_ref[...], ((0,), (0,)))
+    for n in range(nst + 1):
+        t["rb"][n] = spread_rates[:, lane_tile(n)]
+    own["x256"][:, 0:ch] = gy_ref[...].astype(F32)
+    turned = jnp.transpose(own["x256"][...])
+    for s, field in enumerate(by_step(plan, [turned[:ch, lane_tile(k)] for k in range(plan.steps // 2)])):
+        t["gy"][s] = field
+
+
+def tall_output_kernel(plan, side, kept, gain, mixed_ref, own):
+    steps, ch, nst = plan.steps, plan.channels, plan.states
+
+    def channels(c, carry):
+        at = pl.ds(pl.multiple_of(c * SUB, SUB), SUB)
+        for s in range(steps):
+            terms = [gain[nst, at, :] * kept["u"][s, at, :]]
+            terms += [kept["bc"][s, nst + n] * kept["h"][s, n, at, :] for n in range(nst)]
+            while len(terms) > 1:
+                terms = [a + b for a, b in zip(terms[::2], terms[1::2])] + terms[len(terms) // 2 * 2 :]
+            own["y"][s, at, :] = terms[0]
+        return carry
+
+    lax.fori_loop(0, ch // SUB, channels, 0)
+    mixed_ref[...] = by_row(plan, [own["y"][s] for s in range(steps)]).astype(BF16)
+
+
+def tall_columns_kernel(plan, side, recv_refs, ready, out_refs, grads_ref, kept, rest):
+    steps, ch, nst, rank = plan.steps, plan.channels, plan.states, plan.rank
+    t = ready | kept | rest
+    up = t["p"].shape[1]
+    part = nst + SUB
+    rows0 = ((0,), (0,))
+    lanes1 = ((1,), (1,))
+    lanes = lane_tile
+    x_hi, x_lo = split(t["xs"][...])
+    d_hi, d_lo = split(t["ds"][...])
+
+    low8 = lane_iota(SUB) < plan.half
+    row8 = lax.broadcasted_iota(jnp.int32, (SUB, LANES), 0)
+    receive_blocks(recv_refs, t["x256"])
+    turned = jnp.transpose(t["x256"][...])
+    for s, field in enumerate(by_step(plan, [turned[: ch + SUB, lanes(k)] for k in range(steps // 2)])):
+        t["m"][s] = field[ch:]
+        t["u"][s] = field[:ch] * jnp.concatenate([field[ch:]] * (ch // SUB), axis=0)
+    u_b = jnp.concatenate([t["u"][s].astype(BF16) for s in range(steps)], axis=1)
+    proj = dot(x_hi, u_b) + dot(x_lo, u_b)
+    low_up = lane_iota(up) < plan.half
+    ranks = []
+    for s in range(steps):
+        p = jnp.where(low_up, proj[:up, lanes(s)], proj[up:, lanes(s)])
+        t["p"][s] = p
+        one = jnp.where(row8 < rank, p[:SUB], jnp.where(row8 == rank, 1.0, 0.0))
+        ranks.append(jnp.concatenate([jnp.where(low8, one, 0.0), jnp.where(low8, 0.0, one)], axis=0))
+        for r in range(2 * nst):
+            t["bc"][s, r] = jnp.broadcast_to(p[rank + r : rank + r + 1, :], (SUB, LANES))
+    r_hi, r_lo = split(jnp.concatenate(ranks, axis=1))
+    z = dot(d_hi, r_hi, rows0) + dot(d_lo, r_hi, rows0) + dot(d_hi, r_lo, rows0)
+    for s in range(steps):
+        z_s = z[:, lanes(s)]
+        t["z"][s] = z_s
+        soft = jnp.maximum(z_s, 0.0) + jnp.log1p(jnp.exp(-jnp.abs(z_s)))
+        dt = soft * jnp.concatenate([t["m"][s]] * (ch // SUB), axis=0)
+        t["dt"][s] = dt
+        t["dtu"][s] = dt * t["u"][s]
+
+    each = 2 if ch % (2 * SUB) == 0 else 1
+
+    def channels_at(c):
+        return [pl.ds(pl.multiple_of((c * each + k) * SUB, SUB), SUB) for k in range(each)]
+
+    def scan_forward(c, carry):
+        ats = channels_at(c)
+        dts = [[t["dt"][s, at, :] for s in range(steps)] for at in ats]
+        dtus = [[t["dtu"][s, at, :] for s in range(steps)] for at in ats]
+        for n in range(nst):
+            hs = [None] * each
+            for s in range(steps):
+                b = t["bc"][s, n]
+                for k, at in enumerate(ats):
+                    h = b * dtus[k][s]
+                    if s:
+                        a = jnp.exp2(dts[k][s] * t["rb"][n, at, :])
+                        t["a"][s, n, at, :] = a
+                        h = a * hs[k] + h
+                    t["h"][s, n, at, :] = h
+                    hs[k] = h
+        return carry
+
+    lax.fori_loop(0, ch // (each * SUB), scan_forward, 0)
+    t["acc"][...] = jnp.zeros_like(t["acc"])
+
+    def scan_backward(c, carry):
+        ats = channels_at(c)
+        zero = jnp.zeros((SUB, LANES), F32)
+        sbs, wqs = [[zero] * steps for _ in ats], [[zero] * steps for _ in ats]
+        for n in range(nst):
+            after, g_rates = [None] * each, [None] * each
+            for s in reversed(range(steps)):
+                b, c_now = t["bc"][s, n], t["bc"][s, nst + n]
+                to_b, to_c = t["acc"][s, n], t["acc"][s, nst + n]
+                for k, at in enumerate(ats):
+                    gy = t["gy"][s, at, :]
+                    gh = c_now * gy
+                    if after[k] is not None:
+                        gh = gh + after[k]
+                    to_b = to_b + gh * t["dtu"][s, at, :]
+                    to_c = to_c + gy * t["h"][s, n, at, :]
+                    sbs[k][s] = sbs[k][s] + gh * b
+                    if s:
+                        after[k] = t["a"][s, n, at, :] * gh
+                        q = after[k] * t["h"][s - 1, n, at, :]
+                        wqs[k][s] = wqs[k][s] + q * t["rb"][n, at, :]
+                        more = q * t["dt"][s, at, :]
+                        g_rates[k] = more if g_rates[k] is None else g_rates[k] + more
+                t["acc"][s, n], t["acc"][s, nst + n] = to_b, to_c
+            for k, at in enumerate(ats):
+                t["gr"][n, at, :] = g_rates[k]
+        for k, at in enumerate(ats):
+            for s in range(steps):
+                t["sb"][s, at, :] = sbs[k][s]
+                t["wq"][s, at, :] = wqs[k][s]
+        return carry
+
+    lax.fori_loop(0, ch // (each * SUB), scan_backward, 0)
+
+    gzs, gyus = [], []
+    for s in range(steps):
+        mask = jnp.concatenate([t["m"][s]] * (ch // SUB), axis=0)
+        g_dt = t["wq"][s] * LN2 + t["sb"][s] * t["u"][s]
+        gzs.append((g_dt * mask * (1.0 / (1.0 + jnp.exp(-t["z"][s])))).astype(BF16))
+        gyus.append((t["gy"][s] * t["u"][s]).astype(BF16))
+    gz_b, gyu_b = jnp.concatenate(gzs, axis=1), jnp.concatenate(gyus, axis=1)
+    g_rank = dot(d_hi, gz_b)
+    row_up = lax.broadcasted_iota(jnp.int32, (SUB, LANES), 0)
+    g_ps = []
+    for s in range(steps):
+        tiles = [jnp.where(low8, g_rank[:SUB, lanes(s)], g_rank[SUB:, lanes(s)])]
+        tiles += [jnp.zeros((SUB, LANES), F32)] * (up // SUB - 1)
+        tiles[0] = jnp.where(row_up < rank, tiles[0], 0.0)
+        for r in range(2 * nst):
+            k, j = divmod(rank + r, SUB)
+            tiles[k] = jnp.where(row_up == j, jnp.sum(t["acc"][s, r], axis=0, keepdims=True), tiles[k])
+        g_p = jnp.concatenate(tiles, axis=0)
+        g_ps.append(jnp.concatenate([jnp.where(low_up, g_p, 0.0), jnp.where(low_up, 0.0, g_p)], axis=0))
+    gp_b = jnp.concatenate(g_ps, axis=1).astype(BF16)
+    through = dot(x_hi, gp_b, rows0)
+    gus = []
+    for s in range(steps):
+        mask = jnp.concatenate([t["m"][s]] * (ch // SUB), axis=0)
+        gus.append((t["sb"][s] * t["dt"][s] + t["rb"][nst] * t["gy"][s] + through[:, lanes(s)]) * mask)
+    t["x256"][:, 0:ch] = by_row(plan, gus)
+    send_from(out_refs, t["x256"], ch)
+    g_x = dot(gp_b, u_b, lanes1)
+    g_d = dot(r_hi, gz_b, lanes1)
+    halves = jnp.where(row8 == 0, jnp.where(low8, 1.0, 0.0), jnp.where(row8 == 1, jnp.where(low8, 0.0, 1.0), 0.0)).astype(BF16)
+    g_skip = dot(jnp.concatenate([halves] * steps, axis=1), gyu_b, lanes1)
+    pad = t["pad"]
+    row_d = lax.broadcasted_iota(jnp.int32, (SUB, ch), 0)
+    for d in range(2):
+        pad[d, 0:up, 0:ch] = g_x[d * up : (d + 1) * up]
+        pad[d, up : up + SUB, 0:ch] = jnp.where(row_d == SUB - 1, g_skip[d : d + 1], g_d[d * SUB : (d + 1) * SUB])
+    for n0 in range(0, nst, SUB):
+        both = [jnp.zeros((SUB, ch), F32)] * 2
+        for n in range(n0, n0 + SUB):
+            sums = dot(halves, t["gr"][n].astype(BF16), lanes1)
+            both = [jnp.where(row_d == n - n0, sums[d : d + 1], both[d]) for d in range(2)]
+        for d in range(2):
+            pad[d, up + SUB + n0 : up + 2 * SUB + n0, 0:ch] = both[d] * t["al"][d * part + n0 : d * part + n0 + SUB, :]
+    first, second = pad[0], pad[1]
+    tiles = pack_tiles(first[:, :LANES], first[:, LANES:], second[:, :LANES], second[:, LANES:])
+    for k in range(3):
+        grads_ref[:, lanes(k)] = tiles[k].astype(BF16)
 
 
 def unpack_kernel(plan, mine_ref, theirs_ref, gx_ref, gd_ref, gb_ref, ga_ref, gs_ref):
@@ -538,8 +797,9 @@
     return lax.ppermute(x, axis, [(i, i ^ step) for i in range(lax.axis_size(axis))])
 
 
-def exchange(x, axis, step):
-    return (x.astype(F32) + swap(x, axis, step).astype(F32)).astype(BF16)
+def cross(x, mask):
+    axes = ("slide", "band")
+    return lax.ppermute(x, axes, [(i, i ^ mask) for i in range(lax.axis_size(axes))])
 
 
 def deliver(blocks, rows):
@@ -577,34 +837,58 @@
         rows_forward_kernel, rows_plan, 0, (blocks(width, 2 * LANES), arrays(w_kept), arrays(kept)),
         [keep, feat, perm, back] + weights, own | w_own, "rows_forward", 4000, 0, tuple(range(9)))
     moved = deliver(send, width)
-    w_kept, w_own = weight_shapes(cols_plan)
-    kept_c, own_c, grads_c = token_shapes(cols_plan)
-    mixed, grad_carried, grads_v = call(
-        columns_kernel, cols_plan, 1,
-        (jax.ShapeDtypeStruct((tokens, channels), BF16), blocks(tokens, channels), grads_shape),
-        [moved, cotangent.reshape(tokens, channels)] + weights,
-        kept_c | own_c | grads_c | w_kept | w_own, "columns", 8000)
+    cols_out = (jax.ShapeDtypeStruct((tokens, channels), BF16), blocks(tokens, channels), grads_shape)
+    cols_in = [moved, cotangent.reshape(tokens, channels)]
+    if 2 * cols_here == LANES and height % 2 == 0 and rank < SUB - 1:
+        ready, kept_c, own_c = tall_shapes(cols_plan)
+        ready = call(tall_setup_kernel, cols_plan, 1, arrays(ready),
+                     [w_rows["small"], cols_in[1], tall_hot(cols_plan)] + weights, {"x256": own_c["x256"]}, "columns_setup", 1000)
+        grad_carried, grads_v, kept_c = call(
+            tall_columns_kernel, cols_plan, 1, (*cols_out[1:], arrays(kept_c)), [moved, ready], own_c, "columns", 8000)
+        mixed = call(tall_output_kernel, cols_plan, 1, cols_out[0], [kept_c, ready["rb"]], {"y": own_c["z"]}, "columns_output", 1000)
+    else:
+        w_kept, w_own = weight_shapes(cols_plan)
+        kept_c, own_c, grads_c = token_shapes(cols_plan)
+        mixed, grad_carried, grads_v = call(
+            columns_kernel, cols_plan, 1, cols_out, cols_in + weights,
+            kept_c | own_c | grads_c | w_kept | w_own, "columns", 8000)
     returned = deliver(grad_carried, tokens)
-    grad_features, mine, theirs = call(
-        rows_backward_kernel, rows_plan, 0, (jax.ShapeDtypeStruct((width, channels), BF16), grads_shape, grads_shape),
-        [keep, returned, perm, back, w_rows, t_rows, grads_v], grads, "rows_backward", 8000, 1)
+    late = {k: grads.pop(k) for k in ("sb", "gy")} | {"gp": (width, LANES, BF16)}
+    mine, theirs, late = call(
+        rows_backward_kernel, rows_plan, 0, (grads_shape, grads_shape, arrays(late)),
+        [returned, perm, w_rows, t_rows, grads_v], grads, "rows_backward", 8000)
+    needed = {k: t_rows[k] for k in ("dt",)}
+    grad_features = call(
+        rows_output_kernel, rows_plan, 0, jax.ShapeDtypeStruct((channels, width), BF16),
+        [keep, back, {k: w_rows[k] for k in ("small", "x")}, needed, late], {k: own[k] for k in ("stack", "x256")}, "rows_output", 1000, 1)
     mine = (mine.astype(F32) + swap(theirs, "slide", 1).astype(F32)).astype(BF16)
-    for axis in ("slide", "band"):
-        step = 2 if axis == "slide" else 1
-        if axis == "band" and lax.axis_size(axis) == 4:
-            far = [swap(mine, axis, s).astype(F32) for s in (3, 2, 1)]
-            mine = ((mine.astype(F32) + far[2]) + (far[1] + far[0])).astype(BF16)
-            continue
-        while step < lax.axis_size(axis):
-            mine = exchange(mine, axis, step)
-            step *= 2
+    hops = [bands << k for k in range(1, (lax.axis_size("slide") - 1).bit_length())]
+    hops += [1 << k for k in range((bands - 1).bit_length())]
+    late = [mixed, grad_features]
+    while hops:
+        first, hops = hops[:HOPS], hops[HOPS:]
+        masks = [0]
+        for hop in first:
+            masks += [mask ^ hop for mask in masks]
+        got = {mask: cross(mine, mask) for mask in reversed(masks[1:])}
+        if late:
+            hidden = late.pop(0)
+            got, hidden = lax.optimization_barrier((got, hidden))
+            if late:
+                mixed = hidden
+            else:
+                grad_features = hidden
+        terms = [mine.astype(F32)] + [got[mask].astype(F32) for mask in masks[1:]]
+        while len(terms) > 1:
+            terms = [a + b for a, b in zip(terms[::2], terms[1::2])]
+        mine = terms[0].astype(BF16)
     theirs = swap(mine, "slide", 1)
     shapes = [(rank + 2 * states, dirs, channels), (rank, dirs, channels), (dirs, channels), (dirs, states, channels), (dirs, channels)]
     gx, gd, gb, ga, gs = pl.pallas_call(
         functools.partial(unpack_kernel, rows_plan), out_shape=[jax.ShapeDtypeStruct(s, F32) for s in shapes], name="unpack",
         compiler_params=pltpu.CompilerParams(vmem_limit_bytes=VMEM_LIMIT),
     )(mine, theirs)
-    return (mixed.reshape(cotangent.shape), grad_features.reshape(features.shape), jnp.transpose(gx, (1, 2, 0)),
+    return (mixed.reshape(cotangent.shape), jnp.transpose(grad_features).reshape(features.shape), jnp.transpose(gx, (1, 2, 0)),
             jnp.transpose(gd, (1, 0, 2)), gb, ga, gs)
 
 

time: 60.2 us -> 54.3 us (0.902)
  waiting for transfers between devices: 16.3 us -> 10.7 us
  starting transfers between devices: 16.3 us -> 17.7 us
  Pallas kernels: 25.9 us -> 24.9 us
  local copies, waits for them, and re-layouts: 0.79 us -> 0.05 us
    ppermute x0 -> x4, starting transfers between devices: none -> 7.41 us  [cross(): lax.ppermute(x, axes, [(i, i ^ mask) for i in range(lax.axis_size(axes))])]
    ppermute x12 -> x8, waiting for transfers between devices: 16.3 us -> 9.83 us  [swap(): lax.ppermute(x, axis, [(i, i ^ step) for i in range(lax.axis_size(axis))])]
    ppermute x12 -> x8, starting transfers between devices: 16.3 us -> 10.3 us  [swap(): lax.ppermute(x, axis, [(i, i ^ step) for i in range(lax.axis_size(axis))])]
    pallas_call x3 -> x6, Pallas kernels: 25.1 us -> 24.1 us  [call(): pl.pallas_call(functools.partial(kernel, plan, side), out_shape=out_shape...]
    ppermute x0 -> x4, waiting for transfers between devices: none -> 0.87 us  [cross(): lax.ppermute(x, axes, [(i, i ^ mask) for i in range(lax.axis_size(axes))])]
    unnamed x19 -> x20, local copies, waits for them, and re-layouts: 0.79 us -> 0.05 us
  transfers between devices with their start and end apart: 12 -> 12, of which waited for: 9 -> 8; matrix products, arithmetic and copies ran while one was open for 1% -> 0% of each run, Pallas kernels for 0% -> 8%
where the time goes in v2:
time: 54.3 us; the launch traced here: 54.2 us
  Pallas kernels  24.9 us (46%)
  starting transfers between devices  17.7 us (33%)
  waiting for transfers between devices  10.7 us (20%)
  between operations  0.82 us (2%)
    pallas_call x6, Pallas kernels, call(): pl.pallas_call(functools.partial(kernel, plan, side), out_shape=out_shape...  24.1 us
    ppermute x8, starting transfers between devices, swap(): lax.ppermute(x, axis, [(i, i ^ step) for i in range(lax.axis_size(axis))])  10.3 us
    ppermute x8, waiting for transfers between devices, swap(): lax.ppermute(x, axis, [(i, i ^ step) for i in range(lax.axis_size(axis))])  9.83 us
    ppermute x4, starting transfers between devices, cross(): lax.ppermute(x, axes, [(i, i ^ mask) for i in range(lax.axis_size(axes))])  7.41 us
  transfers between devices with their start and end apart: 12, of which 8 were waited for; matrix products, arithmetic and copies ran while one was open for 0% of the time, Pallas kernels for 8%

profile of v2, /device:TPU:0, one launch (start us, length us, event | category | flops | bytes accessed | tf_op | source)
XLA Modules:
  0.0 54.2 jit_solution(15790725855269441870)
XLA Ops:
  0.6 0.0 copy-start
  0.6 0.0 copy-start.1
  0.7 0.0 copy-start.2
  0.7 0.0 copy-start.3
  0.7 0.0 copy-start.4
  0.7 0.0 copy-start.5
  0.7 0.0 copy-start.7
  0.7 6.8 %rows_forward.1 = (bf16[64,256]{1,0:T(8,128)(2,1)S(1)}, bf16[64,256]{1,0:T(8,128)(2,1)S(1)}, bf16[64,256]{1,0:T(8,128)(2,1)S(1)}, bf16[64,256]{1,0:T(8,128)(2,1)...) custom-call(s32[2]{0:T(128)} %bitcast.18, ...), custom_call_target="tpu_custom_call" | custom-call | flops 4000000000 | bytes 4000000 | tf_op jit(solution)/shard_map/rows_forward/pallas_call | solution.py:781
  7.6 3.1 %collective-permute-start = (bf16[64,256]{1,0:T(8,128)(2,1)S(1)}, bf16[64,256]{1,0:T(8,128)(2,1)S(1)}, u32[]{:S(2)}, u32[]{:S(2)}) collective-permute-start(bf16[64,256]{1,0:T(8,128)(2,1)S(1)} %get-tuple-element.54), channel_id=1, source_target_pairs={{0,1},{1,0},{2,3},{3,2},{4,5},{5,4},{6,7},{7,6},{8,9},{9,8},{10,11... | collective-permute-start | bytes 98312 | tf_op jit(solution)/shard_map/ppermute | solution.py:797
  10.7 2.6 %collective-permute-start.1 = (bf16[64,256]{1,0:T(8,128)(2,1)S(1)}, bf16[64,256]{1,0:T(8,128)(2,1)S(1)}, u32[]{:S(2)}, u32[]{:S(2)}) collective-permute-start(bf16[64,256]{1,0:T(8,128)(2,1)S(1)} %get-tuple-element.55), channel_id=1, source_target_pairs={{0,2},{1,3},{2,0},{3,1},{4,6},{5,7},{6,4},{7,5},{8,10},{9,11},{10,... | collective-permute-start | bytes 98312 | tf_op jit(solution)/shard_map/ppermute | solution.py:797
  13.3 0.0 collective-permute-start.2
  13.3 0.0 copy-done
  13.3 0.0 copy-done.1
  13.3 0.0 copy-done.2
  13.3 0.0 copy-done.3
  13.3 0.0 copy-done.4
  13.3 0.0 copy-done.5
  13.3 0.0 copy-done.7
  13.3 0.5 columns_setup.1
  13.8 0.0 collective-permute-done.recv_refs_1_
  13.8 2.2 %collective-permute-done.1.recv_refs_2_ = bf16[64,256]{1,0:T(8,128)(2,1)S(1)} collective-permute-done((bf16[64,256]{1,0:T(8,128)(2,1)S(1)}, bf16[64,256]{1,0:T(8,128)(2,1)S(1)}, u32[]{:S(2)}, u32[]{:S(2)}) %collective-permute-start.1) | collective-permute-done | bytes 32800 | tf_op jit(solution)/shard_map/ppermute | solution.py:797
  16.1 2.9 %collective-permute-done.2.recv_refs_3_ = bf16[64,256]{1,0:T(8,128)(2,1)S(1)} collective-permute-done((bf16[64,256]{1,0:T(8,128)(2,1)S(1)}, bf16[64,256]{1,0:T(8,128)(2,1)S(1)}, u32[]{:S(2)}, u32[]{:S(2)}) %collective-permute-start.2) | collective-permute-done | bytes 32800 | tf_op jit(solution)/shard_map/ppermute | solution.py:797
  19.0 6.0 %columns.1 = (bf16[64,192]{1,0:T(8,128)(2,1)S(1)}, bf16[64,192]{1,0:T(8,128)(2,1)S(1)}, bf16[64,192]{1,0:T(8,128)(2,1)S(1)}, bf16[64,192]{1,0:T(8,128)(2,1)S(1)}...) custom-call(bf16[64,256]{1,0:T(8,128)(2,1)S(1)} %get-tuple-element.5, ...), custom_call_target="tpu_custom_call" | custom-call | flops 8000000000 | bytes 4000000 | tf_op jit(solution)/shard_map/columns/pallas_call | solution.py:781
  25.0 0.0 collective-permute-start.3
  25.0 0.9 %collective-permute-start.4 = (bf16[64,192]{1,0:T(8,128)(2,1)S(1)}, bf16[64,192]{1,0:T(8,128)(2,1)S(1)}, u32[]{:S(2)}, u32[]{:S(2)}) collective-permute-start(bf16[64,192]{1,0:T(8,128)(2,1)S(1)} %get-tuple-element.65), channel_id=1, source_target_pairs={{0,2},{1,3},{2,0},{3,1},{4,6},{5,7},{6,4},{7,5},{8,10},{9,11},{10,... | collective-permute-start | bytes 73736 | tf_op jit(solution)/shard_map/ppermute | solution.py:797
  25.9 3.5 %collective-permute-start.5 = (bf16[64,192]{1,0:T(8,128)(2,1)S(1)}, bf16[64,192]{1,0:T(8,128)(2,1)S(1)}, u32[]{:S(2)}, u32[]{:S(2)}) collective-permute-start(bf16[64,192]{1,0:T(8,128)(2,1)S(1)} %get-tuple-element.66), channel_id=1, source_target_pairs={{0,3},{1,2},{2,1},{3,0},{4,7},{5,6},{6,5},{7,4},{8,11},{9,10},{10,... | collective-permute-start | bytes 73736 | tf_op jit(solution)/shard_map/ppermute | solution.py:797
  29.4 0.0 collective-permute-done.3.gy_refs_1_
  29.4 0.5 collective-permute-done.4.gy_refs_2_
  29.9 1.7 %collective-permute-done.5.gy_refs_3_ = bf16[64,192]{1,0:T(8,128)(2,1)S(1)} collective-permute-done((bf16[64,192]{1,0:T(8,128)(2,1)S(1)}, bf16[64,192]{1,0:T(8,128)(2,1)S(1)}, u32[]{:S(2)}, u32[]{:S(2)}) %collective-permute-start.5) | collective-permute-done | bytes 24608 | tf_op jit(solution)/shard_map/ppermute | solution.py:797
  31.6 0.0 copy-done.9
  31.6 6.7 %rows_backward.1 = (bf16[64,384]{1,0:T(8,128)(2,1)S(1)}, bf16[64,384]{1,0:T(8,128)(2,1)S(1)}, bf16[256,128]{1,0:T(8,128)(2,1)S(1)}, f32[256,384]{1,0:T(8,128)S(1)}, f32[256,384]{1,0:T(8,128)S(1)}) custom-call(bf16[64,192]{1,0:T(8,128)(2,1)S(1)} %get-tuple-element.63.gy_refs_0_, bf16[64,192]{1,0:T(8,128)(2,1)S(1)} %collective-permute-done.3.gy_refs_1_, ...), custom_call_target="tpu_custom_call" | custom-call | flops 8000000000 | bytes 4000000 | tf_op jit(solution)/shard_map/rows_backward/pallas_call | solution.py:781
  38.4 0.0 copy-start.6
  38.4 0.0 copy-start.8
  38.4 0.1 collective-permute-start.6
  38.5 1.2 %collective-permute-done.6 = bf16[64,384]{1,0:T(8,128)(2,1)S(1)} collective-permute-done((bf16[64,384]{1,0:T(8,128)(2,1)S(1)}, bf16[64,384]{1,0:T(8,128)(2,1)S(1)}, u32[]{:S(2)}, u32[]{:S(2)}) %collective-permute-start.6) | collective-permute-done | bytes 49184 | tf_op jit(solution)/shard_map/ppermute | solution.py:797
  39.7 1.2 %collective-permute-start.9 = (bf16[64,384]{1,0:T(8,128)(2,1)S(1)}, bf16[64,384]{1,0:T(8,128)(2,1)S(1)}, u32[]{:S(2)}, u32[]{:S(2)}) collective-permute-start(bf16[64,384]{1,0:T(8,128)(2,1)S(1)} %add_convert_fusion.2), channel_id=1, source_target_pairs={{0,9},{1,8},{2,11},{3,10},{4,13},{5,12},{6,15},{7,14},{8,1},{9,0},... | collective-permute-start | bytes 147464 | tf_op jit(solution)/shard_map/ppermute | solution.py:802
  40.9 0.5 collective-permute-start.8
  41.4 1.8 %collective-permute-start.7 = (bf16[64,384]{1,0:T(8,128)(2,1)S(1)}, bf16[64,384]{1,0:T(8,128)(2,1)S(1)}, u32[]{:S(2)}, u32[]{:S(2)}) collective-permute-start(bf16[64,384]{1,0:T(8,128)(2,1)S(1)} %add_convert_fusion.2), channel_id=1, source_target_pairs={{0,1},{1,0},{2,3},{3,2},{4,5},{5,4},{6,7},{7,6},{8,9},{9,8},{10,11... | collective-permute-start | bytes 147464 | tf_op jit(solution)/shard_map/ppermute | solution.py:802
  43.2 2.2 %columns_output.1 = bf16[256,192]{1,0:T(8,128)(2,1)} custom-call(f32[4,32,8,128]{3,2,1,0:T(8,128)S(1)} %get-tuple-element.82.kept__bc__, f32[4,16,192,128]{3,2,1,0:T(8,128)S(1)} %get-tuple-element.83.kept__h__, f32[4,192,128]{2,1,0:T(8,128)S(1)} %get-tuple-element.84.kept__u__, f32[17,192,128]{2,1,0:T(8,128)S(1)} %get-tuple-element.61.ready__rb__.gain), custom_call_target="tpu_custom_call" | custom-call | flops 1000000000 | bytes 4000000 | tf_op jit(solution)/shard_map/columns_output/pallas_call | solution.py:781
  45.5 0.0 collective-permute-done.9
  45.5 0.0 collective-permute-done.8
  45.5 0.1 collective-permute-done.7
  45.6 3.9 %collective-permute-start.10 = (bf16[64,384]{1,0:T(8,128)(2,1)S(1)}, bf16[64,384]{1,0:T(8,128)(2,1)S(1)}, u32[]{:S(2)}, u32[]{:S(2)}) collective-permute-start(bf16[64,384]{1,0:T(8,128)(2,1)S(1)} %add_convert_fusion.1), channel_id=1, source_target_pairs={{0,2},{1,3},{2,0},{3,1},{4,6},{5,7},{6,4},{7,5},{8,10},{9,11},{10,... | collective-permute-start | bytes 147464 | tf_op jit(solution)/shard_map/ppermute | solution.py:802
  49.4 1.8 %rows_output.1 = bf16[192,256]{1,0:T(8,128)(2,1)} custom-call(s32[2]{0:T(128)S(1)} %bitcast.19, bf16[256,512]{1,0:T(8,128)(2,1)S(1)} %copy-done.8, f32[32,384]{1,0:T(8,128)S(1)} %get-tuple-element.57.after_ref.w__small__, f32[128,384]{1,0:T(8,128)S(1)} %get-tuple-element.69.w__x__, f32[256,384]{1,0:T(8,128)S(1)} %get-tuple-element.72.kept__dt__, ...), custom_call_target="tpu_custom_call" | custom-call | flops 1000000000 | bytes 4000000 | tf_op jit(solution)/shard_map/rows_output/pallas_call | solution.py:781
  51.3 0.8 %collective-permute-done.10 = bf16[64,384]{1,0:T(8,128)(2,1)S(1)} collective-permute-done((bf16[64,384]{1,0:T(8,128)(2,1)S(1)}, bf16[64,384]{1,0:T(8,128)(2,1)S(1)}, u32[]{:S(2)}, u32[]{:S(2)}) %collective-permute-start.10) | collective-permute-done | bytes 49184 | tf_op jit(solution)/shard_map/ppermute | solution.py:802
  52.1 0.1 collective-permute-start.11
  52.1 1.2 %collective-permute-done.11.theirs_ref = bf16[64,384]{1,0:T(8,128)(2,1)S(1)} collective-permute-done((bf16[64,384]{1,0:T(8,128)(2,1)S(1)}, bf16[64,384]{1,0:T(8,128)(2,1)S(1)}, u32[]{:S(2)}, u32[]{:S(2)}) %collective-permute-start.11) | collective-permute-done | bytes 49184 | tf_op jit(solution)/shard_map/ppermute | solution.py:797
  53.4 0.8 %unpack.1 = (f32[38,4,192]{2,1,0:T(4,128)}, f32[6,4,192]{2,1,0:T(4,128)}, f32[4,192]{1,0:T(4,128)}, f32[4,16,192]{2,1,0:T(8,128)}, f32[4,192]{1,0:T(4,128)}) custom-call(bf16[64,384]{1,0:T(8,128)(2,1)S(1)} %add_convert_fusion.mine_ref, bf16[64,384]{1,0:T(8,128)(2,1)S(1)} %collective-permute-done.11.theirs_ref), custom_call_target="tpu_custom_call" | custom-call | tf_op jit(solution)/shard_map/unpack/pallas_call | solution.py:887
  (6 shorter events, 0.1 us)
Async XLA Ops:
  0.6 12.6 %copy-start = (f32[4,192,38]{1,0,2:T(4,128)S(1)}, f32[4,192,38]{1,0,2:T(4,128)}, u32[]{:S(2)}) copy-start(f32[4,192,38]{1,0,2:T(4,128)} %param.14) | copy-start | bytes 350212
  0.6 12.6 %copy-start.1 = (bf16[1,4,64,192]{3,2,1,0:T(8,128)(2,1)S(1)}, bf16[1,4,64,192]{3,2,1,0:T(8,128)(2,1)}, u32[]{:S(2)}) copy-start(bf16[1,4,64,192]{3,2,1,0:T(8,128)(2,1)} %param.13) | copy-start | bytes 294916
  0.7 12.6 %copy-start.2 = (f32[4,16,192]{2,1,0:T(8,128)S(1)}, f32[4,16,192]{2,1,0:T(8,128)}, u32[]{:S(2)}) copy-start(f32[4,16,192]{2,1,0:T(8,128)} %alog_ref.1) | copy-start | bytes 147460
  0.7 12.6 %copy-start.3 = (f32[4,6,192]{2,0,1:T(4,128)S(1)}, f32[4,6,192]{2,0,1:T(4,128)}, u32[]{:S(2)}) copy-start(f32[4,6,192]{2,0,1:T(4,128)} %param.15) | copy-start | bytes 55300
  0.7 12.6 %copy-start.4 = (f32[4,192]{1,0:T(4,128)S(1)}, f32[4,192]{1,0:T(4,128)}, u32[]{:S(2)}) copy-start(f32[4,192]{1,0:T(4,128)} %bias_ref.1) | copy-start | bytes 9220
  0.7 12.6 %copy-start.5 = (f32[4,192]{1,0:T(4,128)S(1)}, f32[4,192]{1,0:T(4,128)}, u32[]{:S(2)}) copy-start(f32[4,192]{1,0:T(4,128)} %skip_ref.1) | copy-start | bytes 9220
  0.7 12.6 %copy-start.7 = (bf16[144,2176]{1,0:T(8,128)(2,1)S(1)}, bf16[144,2176]{1,0:T(8,128)(2,1)}, u32[]{:S(2)}) copy-start(bf16[144,2176]{1,0:T(8,128)(2,1)} %constant.8.clone.hot_ref) | copy-start | bytes 1880068
  7.6 6.3 %collective-permute-start = (bf16[64,256]{1,0:T(8,128)(2,1)S(1)}, bf16[64,256]{1,0:T(8,128)(2,1)S(1)}, u32[]{:S(2)}, u32[]{:S(2)}) collective-permute-start(bf16[64,256]{1,0:T(8,128)(2,1)S(1)} %get-tuple-element.54), channel_id=1, source_target_pairs={{0,1},{1,0},{2,3},{3,2},{4,5},{5,4},{6,7},{7,6},{8,9},{9,8},{10,11... | collective-permute-start | bytes 98312 | tf_op jit(solution)/shard_map/ppermute | solution.py:797
  10.7 5.4 %collective-permute-start.1 = (bf16[64,256]{1,0:T(8,128)(2,1)S(1)}, bf16[64,256]{1,0:T(8,128)(2,1)S(1)}, u32[]{:S(2)}, u32[]{:S(2)}) collective-permute-start(bf16[64,256]{1,0:T(8,128)(2,1)S(1)} %get-tuple-element.55), channel_id=1, source_target_pairs={{0,2},{1,3},{2,0},{3,1},{4,6},{5,7},{6,4},{7,5},{8,10},{9,11},{10,... | collective-permute-start | bytes 98312 | tf_op jit(solution)/shard_map/ppermute | solution.py:797
  13.3 5.7 %collective-permute-start.2 = (bf16[64,256]{1,0:T(8,128)(2,1)S(1)}, bf16[64,256]{1,0:T(8,128)(2,1)S(1)}, u32[]{:S(2)}, u32[]{:S(2)}) collective-permute-start(bf16[64,256]{1,0:T(8,128)(2,1)S(1)} %get-tuple-element.56), channel_id=1, source_target_pairs={{0,3},{1,2},{2,1},{3,0},{4,7},{5,6},{6,5},{7,4},{8,11},{9,10},{10,... | collective-permute-start | bytes 98312 | tf_op jit(solution)/shard_map/ppermute | solution.py:797
  19.0 12.7 %copy-start.9 = (bf16[256,512]{1,0:T(8,128)(2,1)S(1)}, bf16[256,512]{1,0:T(8,128)(2,1)}, u32[]{:S(2)}) copy-start(bf16[256,512]{1,0:T(8,128)(2,1)} %constant.6.clone.refs_2_.perm_ref) | copy-start | bytes 786436
  25.0 4.4 %collective-permute-start.3 = (bf16[64,192]{1,0:T(8,128)(2,1)S(1)}, bf16[64,192]{1,0:T(8,128)(2,1)S(1)}, u32[]{:S(2)}, u32[]{:S(2)}) collective-permute-start(bf16[64,192]{1,0:T(8,128)(2,1)S(1)} %get-tuple-element.64), channel_id=1, source_target_pairs={{0,1},{1,0},{2,3},{3,2},{4,5},{5,4},{6,7},{7,6},{8,9},{9,8},{10,11... | collective-permute-start | bytes 73736 | tf_op jit(solution)/shard_map/ppermute | solution.py:797
  25.0 4.9 %collective-permute-start.4 = (bf16[64,192]{1,0:T(8,128)(2,1)S(1)}, bf16[64,192]{1,0:T(8,128)(2,1)S(1)}, u32[]{:S(2)}, u32[]{:S(2)}) collective-permute-start(bf16[64,192]{1,0:T(8,128)(2,1)S(1)} %get-tuple-element.65), channel_id=1, source_target_pairs={{0,2},{1,3},{2,0},{3,1},{4,6},{5,7},{6,4},{7,5},{8,10},{9,11},{10,... | collective-permute-start | bytes 73736 | tf_op jit(solution)/shard_map/ppermute | solution.py:797
  25.9 5.7 %collective-permute-start.5 = (bf16[64,192]{1,0:T(8,128)(2,1)S(1)}, bf16[64,192]{1,0:T(8,128)(2,1)S(1)}, u32[]{:S(2)}, u32[]{:S(2)}) collective-permute-start(bf16[64,192]{1,0:T(8,128)(2,1)S(1)} %get-tuple-element.66), channel_id=1, source_target_pairs={{0,3},{1,2},{2,1},{3,0},{4,7},{5,6},{6,5},{7,4},{8,11},{9,10},{10,... | collective-permute-start | bytes 73736 | tf_op jit(solution)/shard_map/ppermute | solution.py:797
  38.4 11.1 %copy-start.6 = (s32[1,1,2]{2,1,0:T(1,128)S(1)}, s32[1,1,2]{2,1,0:T(1,128)}, u32[]{:S(2)}) copy-start(s32[1,1,2]{2,1,0:T(1,128)} %param.12) | copy-start | bytes 28
  38.4 11.1 %copy-start.8 = (bf16[256,512]{1,0:T(8,128)(2,1)S(1)}, bf16[256,512]{1,0:T(8,128)(2,1)}, u32[]{:S(2)}) copy-start(bf16[256,512]{1,0:T(8,128)(2,1)} %constant.7.clone.refs_3_.back_ref) | copy-start | bytes 786436
  38.4 1.3 %collective-permute-start.6 = (bf16[64,384]{1,0:T(8,128)(2,1)S(1)}, bf16[64,384]{1,0:T(8,128)(2,1)S(1)}, u32[]{:S(2)}, u32[]{:S(2)}) collective-permute-start(bf16[64,384]{1,0:T(8,128)(2,1)S(1)} %get-tuple-element.81), channel_id=1, source_target_pairs={{0,4},{4,0},{8,12},{12,8},{1,5},{5,1},{9,13},{13,9},{2,6},{6,2},{1... | collective-permute-start | bytes 147464 | tf_op jit(solution)/shard_map/ppermute | solution.py:797
  39.7 5.8 %collective-permute-start.9 = (bf16[64,384]{1,0:T(8,128)(2,1)S(1)}, bf16[64,384]{1,0:T(8,128)(2,1)S(1)}, u32[]{:S(2)}, u32[]{:S(2)}) collective-permute-start(bf16[64,384]{1,0:T(8,128)(2,1)S(1)} %add_convert_fusion.2), channel_id=1, source_target_pairs={{0,9},{1,8},{2,11},{3,10},{4,13},{5,12},{6,15},{7,14},{8,1},{9,0},... | collective-permute-start | bytes 147464 | tf_op jit(solution)/shard_map/ppermute | solution.py:802
  40.9 4.6 %collective-permute-start.8 = (bf16[64,384]{1,0:T(8,128)(2,1)S(1)}, bf16[64,384]{1,0:T(8,128)(2,1)S(1)}, u32[]{:S(2)}, u32[]{:S(2)}) collective-permute-start(bf16[64,384]{1,0:T(8,128)(2,1)S(1)} %add_convert_fusion.2), channel_id=1, source_target_pairs={{0,8},{1,9},{2,10},{3,11},{4,12},{5,13},{6,14},{7,15},{8,0},{9,1},... | collective-permute-start | bytes 147464 | tf_op jit(solution)/shard_map/ppermute | solution.py:802
  41.4 4.1 %collective-permute-start.7 = (bf16[64,384]{1,0:T(8,128)(2,1)S(1)}, bf16[64,384]{1,0:T(8,128)(2,1)S(1)}, u32[]{:S(2)}, u32[]{:S(2)}) collective-permute-start(bf16[64,384]{1,0:T(8,128)(2,1)S(1)} %add_convert_fusion.2), channel_id=1, source_target_pairs={{0,1},{1,0},{2,3},{3,2},{4,5},{5,4},{6,7},{7,6},{8,9},{9,8},{10,11... | collective-permute-start | bytes 147464 | tf_op jit(solution)/shard_map/ppermute | solution.py:802
  45.6 6.5 %collective-permute-start.10 = (bf16[64,384]{1,0:T(8,128)(2,1)S(1)}, bf16[64,384]{1,0:T(8,128)(2,1)S(1)}, u32[]{:S(2)}, u32[]{:S(2)}) collective-permute-start(bf16[64,384]{1,0:T(8,128)(2,1)S(1)} %add_convert_fusion.1), channel_id=1, source_target_pairs={{0,2},{1,3},{2,0},{3,1},{4,6},{5,7},{6,4},{7,5},{8,10},{9,11},{10,... | collective-permute-start | bytes 147464 | tf_op jit(solution)/shard_map/ppermute | solution.py:802
  52.1 1.3 %collective-permute-start.11 = (bf16[64,384]{1,0:T(8,128)(2,1)S(1)}, bf16[64,384]{1,0:T(8,128)(2,1)S(1)}, u32[]{:S(2)}, u32[]{:S(2)}) collective-permute-start(bf16[64,384]{1,0:T(8,128)(2,1)S(1)} %add_convert_fusion.mine_ref), channel_id=1, source_target_pairs={{0,4},{4,0},{8,12},{12,8},{1,5},{5,1},{9,13},{13,9},{2,6},{6,2},{1... | collective-permute-start | bytes 147464 | tf_op jit(solution)/shard_map/ppermute | solution.py:797

commit v3 on v2

--- a/solution.py
+++ b/solution.py
@@ -15,8 +15,10 @@
 LOG2E = 1.4426950408889634
 LN2 = 0.6931471805599453
 VMEM_LIMIT = 8 * 2**20
-VMEM_SPARE = 4 * 2**20
+VMEM_SPARE = 2 * 2**20
 PER = 8
+SPREAD_EVERY = 4
+GATHER_EVERY = 3
 HOPS = 2
 
 
@@ -134,8 +136,8 @@
     return out[:, :LANES], out[:, LANES:]
 
 
-def prepare(plan, perm_ref, x256, w, t):
-    b0, b1 = place(plan, perm_ref, x256, t["u"], plan.chunked)
+def prepare(plan, placed, w, t):
+    b0, b1 = placed
     low = lane_iota(plan.rows) < plan.half
     m0 = jnp.where(low, swap64(b0), b0)
     m1 = jnp.where(low, swap64(b1), b1)
@@ -168,6 +170,11 @@
     hi = t["p"][...].astype(BF16).astype(F32)
     both = jnp.concatenate([hi, t["p"][...] - hi], axis=1)
     for r in range(2 * plan.states):
+        if r % SPREAD_EVERY == SPREAD_EVERY - 1:
+            at = plan.rank + r
+            t["bc"][r, :, :LANES] = jnp.broadcast_to(t["p"][:, at : at + 1], (plan.rows, LANES))
+            t["bc"][r, :, LANES:] = jnp.broadcast_to(t["p"][:, plan.half + at : plan.half + at + 1], (plan.rows, LANES))
+            continue
         t["bc"][r] = dot(jnp.where(own_lanes(plan, r, 2 * LANES), both, 0.0).astype(BF16), ones)
 
 
@@ -183,7 +190,14 @@
     first = (k < plan.half) | (k >= LANES + plan.half)
     ones = jnp.where(first == (l < plan.half), 1.0, 0.0).astype(BF16)
     out = jnp.zeros((plan.rows, LANES), F32)
+    lane = lane_iota(plan.rows)
+    low = lane < plan.half
     for r in range(2 * plan.states):
+        if r % GATHER_EVERY == GATHER_EVERY - 1:
+            a, b = t["prod"][r, :, :LANES], t["prod"][r, :, LANES:]
+            out = jnp.where(lane == plan.rank + r, jnp.sum(jnp.where(low, a, b), axis=1, keepdims=True), out)
+            out = jnp.where(lane == plan.half + plan.rank + r, jnp.sum(jnp.where(low, b, a), axis=1, keepdims=True), out)
+            continue
         out = jnp.where(own_lanes(plan, r, LANES), dot(t["prod"][r].astype(BF16), ones), out)
     return out
 
@@ -236,15 +250,18 @@
     return jnp.where(at >= 1, pltpu.roll(end, 1, axis=0), 0.0)
 
 
-def chunk_decay(plan, w, t, n):
+def keep_chunk_decay(plan, w, t):
     total = functools.reduce(lambda a, b: a + b, [t["dt"][s * SUB : (s + 1) * SUB, :] for s in range(plan.steps)])
-    return [jnp.exp2(total * w["rate"][k]) for k in n]
+    for n in range(plan.states):
+        t["decay"][n] = jnp.exp2(total * w["rate"][n])
 
 
 def forward(plan, w, t, keep_states):
     nst = plan.states
     zero = jnp.zeros((SUB, 3 * LANES), F32)
     spread(plan, t)
+    if plan.chunked:
+        keep_chunk_decay(plan, w, t)
     for n0 in range(0, nst, PER):
         ns = list(range(n0, n0 + PER))
 
@@ -262,7 +279,7 @@
                     return tuple(new)
 
                 ends = over_steps(plan, g, local, start)
-                start = tuple(chunk_scan(d, e, False) for d, e in zip(chunk_decay(plan, w, t, ns), ends))
+                start = tuple(chunk_scan(t["decay"][n], e, False) for n, e in zip(ns, ends))
             if keep_states:
                 for n, h in zip(ns, start):
                     t["h"][0, n, pl.ds(g * SUB, SUB), :] = h
@@ -301,7 +318,7 @@
                     return tuple(t["a"][s, n] * (coefs(plan, t, row, n, 1) * gy + c) for n, c in zip(ns, gs))
 
                 ends = over_steps(plan, g, local, start, backwards=True)
-                start = tuple(chunk_scan(d, e, True) for d, e in zip(chunk_decay(plan, w, t, ns), ends))
+                start = tuple(chunk_scan(t["decay"][n], e, True) for n, e in zip(ns, ends))
 
             def full(s, row, carry):
                 gs, rs = carry
@@ -390,6 +407,7 @@
             "h": (plan.steps + 1, plan.states, plan.lines, 3 * LANES)}
     if plan.chunked:
         kept["a"] = (plan.steps, plan.states, plan.lines, 3 * LANES)
+        kept["decay"] = (plan.states, SUB, 3 * LANES)
     own = {"y": wide, "x256": double}
     grads = {"gy": wide, "sb": wide, "wq": wide, "prod": (2 * plan.states,) + double,
              "gr": (plan.states, SUB, 3 * LANES), "x256": double}
@@ -447,14 +465,18 @@
     copies = [pltpu.make_async_copy(a, b, sems.at[k]) for k, (a, b) in enumerate(zip(far, near))]
     for copy in copies:
         copy.start()
-    for copy in copies:
+    for copy in copies[:3]:
         copy.wait()
     tissue_ref, feat_ref, perm_ref, back_ref, x_ref, dtp_ref, bias_ref, alog_ref, skip_ref = near
     t = kept | rest
     w = w | rest
+    placed = place(plan, perm_ref, masked_rows(plan, tissue_ref, feat_ref), t["u"], True)
+    for copy in copies[4:]:
+        copy.wait()
     load_weights(plan, side, x_ref, dtp_ref, bias_ref, alog_ref, skip_ref, w)
-    prepare(plan, perm_ref, masked_rows(plan, tissue_ref, feat_ref), w, t)
+    prepare(plan, placed, w, t)
     forward(plan, w, t, True)
+    copies[3].wait()
     tiles = [t["y"][:, k * LANES : (k + 1) * LANES] for k in range(3)]
     a, b = unplace(plan, back_ref, tiles, t.get("stack"))
     mask = token_mask(plan, tissue_ref, (plan.rows, LANES), 0)
@@ -491,7 +513,8 @@
     low = lane_iota(plan.rows) < plan.half
     last = t["x256"][:, LANES:]
     mask = jnp.where(low, swap64(last), last)
-    prepare(plan, None, jnp.concatenate([t["x256"][:, :LANES] * mask, last * mask], axis=1), w, t)
+    both = jnp.concatenate([t["x256"][:, :LANES] * mask, last * mask], axis=1)
+    prepare(plan, place(plan, None, both, t["u"]), w, t)
     t["x256"][:, 0:ch] = gy_ref[...].astype(F32)
     place(plan, None, t["x256"][...], t["gy"])
     forward(plan, w, t, True)
@@ -516,10 +539,12 @@
     rest = {
         "z": field, "dt": field, "dtu": field, "sb": field, "wq": field,
         "m": (steps, SUB, LANES), "p": (steps, up, LANES), "acc": (steps, 2 * nst, SUB, LANES),
-        "a": (steps, nst, ch, LANES), "gr": (nst, ch, LANES),
-        "x256": (plan.rows, 2 * LANES), "pad": (2, up + SUB + nst, 2 * LANES),
+        "a": (steps, nst, ch, LANES), "x256": (plan.rows, 2 * LANES),
     }
-    return ready, kept, rest
+    every = steps * LANES
+    late = {"gr": (nst, ch, LANES), "gpb": (2 * up, every, BF16), "rk": (2 * SUB, every, BF16),
+            "gzb": (ch, every, BF16), "gyu": (ch, every, BF16), "ub": (ch, every, BF16)}
+    return ready, kept, late, rest, {"pad": (2, up + SUB + nst, 2 * LANES)}
 
 
 def tall_hot(plan):
@@ -586,23 +611,28 @@
 def tall_output_kernel(plan, side, kept, gain, mixed_ref, own):
     steps, ch, nst = plan.steps, plan.channels, plan.states
 
+    each = 2 if ch % (2 * SUB) == 0 else 1
+
     def channels(c, carry):
-        at = pl.ds(pl.multiple_of(c * SUB, SUB), SUB)
+        ats = [pl.ds(pl.multiple_of((c * each + k) * SUB, SUB), SUB) for k in range(each)]
         for s in range(steps):
-            terms = [gain[nst, at, :] * kept["u"][s, at, :]]
-            terms += [kept["bc"][s, nst + n] * kept["h"][s, n, at, :] for n in range(nst)]
-            while len(terms) > 1:
-                terms = [a + b for a, b in zip(terms[::2], terms[1::2])] + terms[len(terms) // 2 * 2 :]
-            own["y"][s, at, :] = terms[0]
+            ys = [[gain[nst, at, :] * kept["u"][s, at, :], None] for at in ats]
+            for n in range(nst):
+                weight = kept["bc"][s, nst + n]
+                for y, at in zip(ys, ats):
+                    more = weight * kept["h"][s, n, at, :]
+                    y[n % 2] = more if y[n % 2] is None else y[n % 2] + more
+            for y, at in zip(ys, ats):
+                own["y"][s, at, :] = y[0] + y[1]
         return carry
 
-    lax.fori_loop(0, ch // SUB, channels, 0)
+    lax.fori_loop(0, ch // (each * SUB), channels, 0)
     mixed_ref[...] = by_row(plan, [own["y"][s] for s in range(steps)]).astype(BF16)
 
 
-def tall_columns_kernel(plan, side, recv_refs, ready, out_refs, grads_ref, kept, rest):
+def tall_columns_kernel(plan, side, recv_refs, ready, out_refs, kept, late, rest):
     steps, ch, nst, rank = plan.steps, plan.channels, plan.states, plan.rank
-    t = ready | kept | rest
+    t = ready | kept | late | rest
     up = t["p"].shape[1]
     part = nst + SUB
     rows0 = ((0,), (0,))
@@ -705,7 +735,8 @@
         g_dt = t["wq"][s] * LN2 + t["sb"][s] * t["u"][s]
         gzs.append((g_dt * mask * (1.0 / (1.0 + jnp.exp(-t["z"][s])))).astype(BF16))
         gyus.append((t["gy"][s] * t["u"][s]).astype(BF16))
-    gz_b, gyu_b = jnp.concatenate(gzs, axis=1), jnp.concatenate(gyus, axis=1)
+    gz_b = jnp.concatenate(gzs, axis=1)
+    t["gzb"][...], t["gyu"][...], t["ub"][...], t["rk"][...] = gz_b, jnp.concatenate(gyus, axis=1), u_b, r_hi
     g_rank = dot(d_hi, gz_b)
     row_up = lax.broadcasted_iota(jnp.int32, (SUB, LANES), 0)
     g_ps = []
@@ -719,6 +750,7 @@
         g_p = jnp.concatenate(tiles, axis=0)
         g_ps.append(jnp.concatenate([jnp.where(low_up, g_p, 0.0), jnp.where(low_up, 0.0, g_p)], axis=0))
     gp_b = jnp.concatenate(g_ps, axis=1).astype(BF16)
+    t["gpb"][...] = gp_b
     through = dot(x_hi, gp_b, rows0)
     gus = []
     for s in range(steps):
@@ -726,11 +758,21 @@
         gus.append((t["sb"][s] * t["dt"][s] + t["rb"][nst] * t["gy"][s] + through[:, lanes(s)]) * mask)
     t["x256"][:, 0:ch] = by_row(plan, gus)
     send_from(out_refs, t["x256"], ch)
+
+
+def tall_grads_kernel(plan, side, t, al_ref, grads_ref, own):
+    steps, ch, nst = plan.steps, plan.channels, plan.states
+    part = nst + SUB
+    lanes1 = ((1,), (1,))
+    gp_b, u_b, r_hi, gz_b, gyu_b = t["gpb"][...], t["ub"][...], t["rk"][...], t["gzb"][...], t["gyu"][...]
+    up = gp_b.shape[0] // 2
+    low8 = lane_iota(SUB) < plan.half
+    row8 = lax.broadcasted_iota(jnp.int32, (SUB, LANES), 0)
     g_x = dot(gp_b, u_b, lanes1)
     g_d = dot(r_hi, gz_b, lanes1)
     halves = jnp.where(row8 == 0, jnp.where(low8, 1.0, 0.0), jnp.where(row8 == 1, jnp.where(low8, 0.0, 1.0), 0.0)).astype(BF16)
     g_skip = dot(jnp.concatenate([halves] * steps, axis=1), gyu_b, lanes1)
-    pad = t["pad"]
+    pad = own["pad"]
     row_d = lax.broadcasted_iota(jnp.int32, (SUB, ch), 0)
     for d in range(2):
         pad[d, 0:up, 0:ch] = g_x[d * up : (d + 1) * up]
@@ -741,11 +783,11 @@
             sums = dot(halves, t["gr"][n].astype(BF16), lanes1)
             both = [jnp.where(row_d == n - n0, sums[d : d + 1], both[d]) for d in range(2)]
         for d in range(2):
-            pad[d, up + SUB + n0 : up + 2 * SUB + n0, 0:ch] = both[d] * t["al"][d * part + n0 : d * part + n0 + SUB, :]
+            pad[d, up + SUB + n0 : up + 2 * SUB + n0, 0:ch] = both[d] * al_ref[d * part + n0 : d * part + n0 + SUB, :]
     first, second = pad[0], pad[1]
     tiles = pack_tiles(first[:, :LANES], first[:, LANES:], second[:, :LANES], second[:, LANES:])
     for k in range(3):
-        grads_ref[:, lanes(k)] = tiles[k].astype(BF16)
+        grads_ref[:, lane_tile(k)] = tiles[k].astype(BF16)
 
 
 def unpack_kernel(plan, mine_ref, theirs_ref, gx_ref, gd_ref, gb_ref, ga_ref, gs_ref):
@@ -777,6 +819,7 @@
         args = [pltpu.with_memory_space_constraint(a, pltpu.HBM) if k in far else a for k, a in enumerate(args)]
         for k in far:
             specs[k] = pl.BlockSpec(memory_space=pltpu.HBM)
+        limit += sum(int(np.prod(args[k].shape)) * 4 for k in far)
         scratches += [[(pltpu.SMEM if args[k].ndim == 1 else pltpu.VMEM)(args[k].shape, args[k].dtype) for k in far], pltpu.SemaphoreType.DMA((len(far),))]
     return pl.pallas_call(
         functools.partial(kernel, plan, side), out_shape=out_shape, in_specs=tuple(specs),
@@ -840,11 +883,12 @@
     cols_out = (jax.ShapeDtypeStruct((tokens, channels), BF16), blocks(tokens, channels), grads_shape)
     cols_in = [moved, cotangent.reshape(tokens, channels)]
     if 2 * cols_here == LANES and height % 2 == 0 and rank < SUB - 1:
-        ready, kept_c, own_c = tall_shapes(cols_plan)
+        ready, kept_c, late_c, own_c, pad_c = tall_shapes(cols_plan)
         ready = call(tall_setup_kernel, cols_plan, 1, arrays(ready),
                      [w_rows["small"], cols_in[1], tall_hot(cols_plan)] + weights, {"x256": own_c["x256"]}, "columns_setup", 1000)
-        grad_carried, grads_v, kept_c = call(
-            tall_columns_kernel, cols_plan, 1, (*cols_out[1:], arrays(kept_c)), [moved, ready], own_c, "columns", 8000)
+        grad_carried, kept_c, late_c = call(
+            tall_columns_kernel, cols_plan, 1, (cols_out[1], arrays(kept_c), arrays(late_c)), [moved, ready], own_c, "columns", 8000)
+        grads_v = call(tall_grads_kernel, cols_plan, 1, grads_shape, [late_c, ready["al"]], pad_c, "columns_grads", 1000)
         mixed = call(tall_output_kernel, cols_plan, 1, cols_out[0], [kept_c, ready["rb"]], {"y": own_c["z"]}, "columns_output", 1000)
     else:
         w_kept, w_own = weight_shapes(cols_plan)

time: 54.3 us -> 53.3 us (0.982)
  Pallas kernels: 24.9 us -> 23.9 us
    pallas_call x6 -> x7, Pallas kernels: 24.1 us -> 23.1 us  [call(): pl.pallas_call(functools.partial(kernel, plan, side), out_shape=out_shape...]
    ppermute x8, waiting for transfers between devices: 9.83 us -> 9.08 us  [swap(): lax.ppermute(x, axis, [(i, i ^ step) for i in range(lax.axis_size(axis))])]
    ppermute x4, waiting for transfers between devices: 0.87 us -> 1.53 us  [cross(): lax.ppermute(x, axes, [(i, i ^ mask) for i in range(lax.axis_size(axes))])]
  transfers between devices with their start and end apart: 12 -> 12, of which waited for: 8 -> 9; matrix products, arithmetic and copies ran while one was open for 0% -> 0% of each run, Pallas kernels for 8% -> 9%
where the time goes in v3:
time: 53.3 us; the launch traced here: 53.2 us
  Pallas kernels  23.9 us (45%)
  starting transfers between devices  17.7 us (33%)
  waiting for transfers between devices  10.6 us (20%)
  between operations  0.83 us (2%)
    pallas_call x7, Pallas kernels, call(): pl.pallas_call(functools.partial(kernel, plan, side), out_shape=out_shape...  23.1 us
    ppermute x8, starting transfers between devices, swap(): lax.ppermute(x, axis, [(i, i ^ step) for i in range(lax.axis_size(axis))])  10.3 us
    ppermute x8, waiting for transfers between devices, swap(): lax.ppermute(x, axis, [(i, i ^ step) for i in range(lax.axis_size(axis))])  9.08 us
    ppermute x4, starting transfers between devices, cross(): lax.ppermute(x, axes, [(i, i ^ mask) for i in range(lax.axis_size(axes))])  7.4 us
    ppermute x4, waiting for transfers between devices, cross(): lax.ppermute(x, axes, [(i, i ^ mask) for i in range(lax.axis_size(axes))])  1.53 us
  transfers between devices with their start and end apart: 12, of which 9 were waited for; matrix products, arithmetic and copies ran while one was open for 0% of the time, Pallas kernels for 9%

profile of v3, /device:TPU:0, one launch (start us, length us, event | category | flops | bytes accessed | tf_op | source)
XLA Modules:
  0.0 53.2 jit_solution(493416932023978430)
XLA Ops:
  0.6 0.0 copy-start
  0.6 0.0 copy-start.1
  0.7 0.0 copy-start.2
  0.7 0.0 copy-start.3
  0.7 0.0 copy-start.4
  0.7 0.0 copy-start.5
  0.7 0.0 copy-start.7
  0.7 6.6 %rows_forward.1 = (bf16[64,256]{1,0:T(8,128)(2,1)S(1)}, bf16[64,256]{1,0:T(8,128)(2,1)S(1)}, bf16[64,256]{1,0:T(8,128)(2,1)S(1)}, bf16[64,256]{1,0:T(8,128)(2,1)...) custom-call(s32[2]{0:T(128)} %bitcast.18, ...), custom_call_target="tpu_custom_call" | custom-call | flops 4000000000 | bytes 4000000 | tf_op jit(solution)/shard_map/rows_forward/pallas_call | solution.py:824
  7.3 3.1 %collective-permute-start = (bf16[64,256]{1,0:T(8,128)(2,1)S(1)}, bf16[64,256]{1,0:T(8,128)(2,1)S(1)}, u32[]{:S(2)}, u32[]{:S(2)}) collective-permute-start(bf16[64,256]{1,0:T(8,128)(2,1)S(1)} %get-tuple-element.60), channel_id=1, source_target_pairs={{0,1},{1,0},{2,3},{3,2},{4,5},{5,4},{6,7},{7,6},{8,9},{9,8},{10,11... | collective-permute-start | bytes 98312 | tf_op jit(solution)/shard_map/ppermute | solution.py:840
  10.4 2.6 %collective-permute-start.1 = (bf16[64,256]{1,0:T(8,128)(2,1)S(1)}, bf16[64,256]{1,0:T(8,128)(2,1)S(1)}, u32[]{:S(2)}, u32[]{:S(2)}) collective-permute-start(bf16[64,256]{1,0:T(8,128)(2,1)S(1)} %get-tuple-element.61), channel_id=1, source_target_pairs={{0,2},{1,3},{2,0},{3,1},{4,6},{5,7},{6,4},{7,5},{8,10},{9,11},{10,... | collective-permute-start | bytes 98312 | tf_op jit(solution)/shard_map/ppermute | solution.py:840
  13.0 0.0 collective-permute-start.2
  13.0 0.0 copy-done.1
  13.0 0.0 copy-done.2
  13.1 0.0 copy-done.3
  13.1 0.0 copy-done.4
  13.1 0.0 copy-done.5
  13.1 0.0 copy-done.7
  13.1 0.5 columns_setup.1
  13.6 0.0 collective-permute-done.recv_refs_1_
  13.6 2.2 %collective-permute-done.1.recv_refs_2_ = bf16[64,256]{1,0:T(8,128)(2,1)S(1)} collective-permute-done((bf16[64,256]{1,0:T(8,128)(2,1)S(1)}, bf16[64,256]{1,0:T(8,128)(2,1)S(1)}, u32[]{:S(2)}, u32[]{:S(2)}) %collective-permute-start.1) | collective-permute-done | bytes 32800 | tf_op jit(solution)/shard_map/ppermute | solution.py:840
  15.8 2.9 %collective-permute-done.2.recv_refs_3_ = bf16[64,256]{1,0:T(8,128)(2,1)S(1)} collective-permute-done((bf16[64,256]{1,0:T(8,128)(2,1)S(1)}, bf16[64,256]{1,0:T(8,128)(2,1)S(1)}, u32[]{:S(2)}, u32[]{:S(2)}) %collective-permute-start.2) | collective-permute-done | bytes 32800 | tf_op jit(solution)/shard_map/ppermute | solution.py:840
  18.8 5.6 %columns.1 = (bf16[64,192]{1,0:T(8,128)(2,1)S(1)}, bf16[64,192]{1,0:T(8,128)(2,1)S(1)}, bf16[64,192]{1,0:T(8,128)(2,1)S(1)}, bf16[64,192]{1,0:T(8,128)(2,1)S(1)}...) custom-call(bf16[64,256]{1,0:T(8,128)(2,1)S(1)} %get-tuple-element.5, ...), custom_call_target="tpu_custom_call" | custom-call | flops 8000000000 | bytes 4000000 | tf_op jit(solution)/shard_map/columns/pallas_call | solution.py:824
  24.4 0.1 collective-permute-start.3
  24.5 0.9 %collective-permute-start.4 = (bf16[64,192]{1,0:T(8,128)(2,1)S(1)}, bf16[64,192]{1,0:T(8,128)(2,1)S(1)}, u32[]{:S(2)}, u32[]{:S(2)}) collective-permute-start(bf16[64,192]{1,0:T(8,128)(2,1)S(1)} %get-tuple-element.71), channel_id=1, source_target_pairs={{0,2},{1,3},{2,0},{3,1},{4,6},{5,7},{6,4},{7,5},{8,10},{9,11},{10,... | collective-permute-start | bytes 73736 | tf_op jit(solution)/shard_map/ppermute | solution.py:840
  25.4 3.5 %collective-permute-start.5 = (bf16[64,192]{1,0:T(8,128)(2,1)S(1)}, bf16[64,192]{1,0:T(8,128)(2,1)S(1)}, u32[]{:S(2)}, u32[]{:S(2)}) collective-permute-start(bf16[64,192]{1,0:T(8,128)(2,1)S(1)} %get-tuple-element.72), channel_id=1, source_target_pairs={{0,3},{1,2},{2,1},{3,0},{4,7},{5,6},{6,5},{7,4},{8,11},{9,10},{10,... | collective-permute-start | bytes 73736 | tf_op jit(solution)/shard_map/ppermute | solution.py:840
  28.8 0.8 %columns_grads.1.grads_v_ref = bf16[64,384]{1,0:T(8,128)(2,1)S(1)} custom-call(bf16[80,512]{1,0:T(8,128)(2,1)S(1)} %get-tuple-element.86.t__gpb__, f32[16,192,128]{2,1,0:T(8,128)S(1)} %get-tuple-element.87.t__gr__, bf16[192,512]{1,0:T(8,128)(2,1)S(1)} %get-tuple-element.88.t__gyu__, bf16[192,512]{1,0:T(8,128)(2,1)S(1)} %get-tuple-element.89.t__gzb__, ...), custom_call_target="tpu_custom_call" | custom-call | flops 1000000000 | bytes 4000000 | tf_op jit(solution)/shard_map/columns_grads/pallas_call | solution.py:824
  29.6 0.0 collective-permute-done.3.gy_refs_1_
  29.6 0.0 collective-permute-done.4.gy_refs_2_
  29.6 1.5 %collective-permute-done.5.gy_refs_3_ = bf16[64,192]{1,0:T(8,128)(2,1)S(1)} collective-permute-done((bf16[64,192]{1,0:T(8,128)(2,1)S(1)}, bf16[64,192]{1,0:T(8,128)(2,1)S(1)}, u32[]{:S(2)}, u32[]{:S(2)}) %collective-permute-start.5) | collective-permute-done | bytes 24608 | tf_op jit(solution)/shard_map/ppermute | solution.py:840
  31.1 6.3 %rows_backward.1 = (bf16[64,384]{1,0:T(8,128)(2,1)S(1)}, bf16[64,384]{1,0:T(8,128)(2,1)S(1)}, bf16[256,128]{1,0:T(8,128)(2,1)S(1)}, f32[256,384]{1,0:T(8,128)S(1)}, f32[256,384]{1,0:T(8,128)S(1)}) custom-call(bf16[64,192]{1,0:T(8,128)(2,1)S(1)} %get-tuple-element.69.gy_refs_0_, bf16[64,192]{1,0:T(8,128)(2,1)S(1)} %collective-permute-done.3.gy_refs_1_, ...), custom_call_target="tpu_custom_call" | custom-call | flops 8000000000 | bytes 4000000 | tf_op jit(solution)/shard_map/rows_backward/pallas_call | solution.py:824
  37.4 0.0 copy-start.6
  37.4 0.0 copy-start.8
  37.4 0.1 collective-permute-start.6
  37.5 1.2 %collective-permute-done.6 = bf16[64,384]{1,0:T(8,128)(2,1)S(1)} collective-permute-done((bf16[64,384]{1,0:T(8,128)(2,1)S(1)}, bf16[64,384]{1,0:T(8,128)(2,1)S(1)}, u32[]{:S(2)}, u32[]{:S(2)}) %collective-permute-start.6) | collective-permute-done | bytes 49184 | tf_op jit(solution)/shard_map/ppermute | solution.py:840
  38.7 1.2 %collective-permute-start.9 = (bf16[64,384]{1,0:T(8,128)(2,1)S(1)}, bf16[64,384]{1,0:T(8,128)(2,1)S(1)}, u32[]{:S(2)}, u32[]{:S(2)}) collective-permute-start(bf16[64,384]{1,0:T(8,128)(2,1)S(1)} %add_convert_fusion.2), channel_id=1, source_target_pairs={{0,9},{1,8},{2,11},{3,10},{4,13},{5,12},{6,15},{7,14},{8,1},{9,0},... | collective-permute-start | bytes 147464 | tf_op jit(solution)/shard_map/ppermute | solution.py:845
  39.9 0.5 collective-permute-start.8
  40.4 1.8 %collective-permute-start.7 = (bf16[64,384]{1,0:T(8,128)(2,1)S(1)}, bf16[64,384]{1,0:T(8,128)(2,1)S(1)}, u32[]{:S(2)}, u32[]{:S(2)}) collective-permute-start(bf16[64,384]{1,0:T(8,128)(2,1)S(1)} %add_convert_fusion.2), channel_id=1, source_target_pairs={{0,1},{1,0},{2,3},{3,2},{4,5},{5,4},{6,7},{7,6},{8,9},{9,8},{10,11... | collective-permute-start | bytes 147464 | tf_op jit(solution)/shard_map/ppermute | solution.py:845
  42.2 1.5 %columns_output.1 = bf16[256,192]{1,0:T(8,128)(2,1)} custom-call(f32[4,32,8,128]{3,2,1,0:T(8,128)S(1)} %get-tuple-element.94.kept__bc__, f32[4,16,192,128]{3,2,1,0:T(8,128)S(1)} %get-tuple-element.95.kept__h__, f32[4,192,128]{2,1,0:T(8,128)S(1)} %get-tuple-element.96.kept__u__, f32[17,192,128]{2,1,0:T(8,128)S(1)} %get-tuple-element.67.ready__rb__.gain), custom_call_target="tpu_custom_call" | custom-call | flops 1000000000 | bytes 4000000 | tf_op jit(solution)/shard_map/columns_output/pallas_call | solution.py:824
  43.8 0.1 collective-permute-done.9
  43.9 0.6 %collective-permute-done.8 = bf16[64,384]{1,0:T(8,128)(2,1)S(1)} collective-permute-done((bf16[64,384]{1,0:T(8,128)(2,1)S(1)}, bf16[64,384]{1,0:T(8,128)(2,1)S(1)}, u32[]{:S(2)}, u32[]{:S(2)}) %collective-permute-start.8) | collective-permute-done | bytes 49184 | tf_op jit(solution)/shard_map/ppermute | solution.py:845
  44.5 0.1 collective-permute-done.7
  44.6 3.9 %collective-permute-start.10 = (bf16[64,384]{1,0:T(8,128)(2,1)S(1)}, bf16[64,384]{1,0:T(8,128)(2,1)S(1)}, u32[]{:S(2)}, u32[]{:S(2)}) collective-permute-start(bf16[64,384]{1,0:T(8,128)(2,1)S(1)} %add_convert_fusion.1), channel_id=1, source_target_pairs={{0,2},{1,3},{2,0},{3,1},{4,6},{5,7},{6,4},{7,5},{8,10},{9,11},{10,... | collective-permute-start | bytes 147464 | tf_op jit(solution)/shard_map/ppermute | solution.py:845
  48.4 0.0 copy-done.8
  48.4 1.8 %rows_output.1 = bf16[192,256]{1,0:T(8,128)(2,1)} custom-call(s32[2]{0:T(128)S(1)} %bitcast.19, bf16[256,512]{1,0:T(8,128)(2,1)S(1)} %copy-done.8, f32[32,384]{1,0:T(8,128)S(1)} %get-tuple-element.63.after_ref.w__small__, f32[128,384]{1,0:T(8,128)S(1)} %get-tuple-element.75.w__x__, f32[256,384]{1,0:T(8,128)S(1)} %get-tuple-element.79.kept__dt__, ...), custom_call_target="tpu_custom_call" | custom-call | flops 1000000000 | bytes 4000000 | tf_op jit(solution)/shard_map/rows_output/pallas_call | solution.py:824
  50.3 0.8 %collective-permute-done.10 = bf16[64,384]{1,0:T(8,128)(2,1)S(1)} collective-permute-done((bf16[64,384]{1,0:T(8,128)(2,1)S(1)}, bf16[64,384]{1,0:T(8,128)(2,1)S(1)}, u32[]{:S(2)}, u32[]{:S(2)}) %collective-permute-start.10) | collective-permute-done | bytes 49184 | tf_op jit(solution)/shard_map/ppermute | solution.py:845
  51.0 0.1 collective-permute-start.11
  51.1 1.2 %collective-permute-done.11.theirs_ref = bf16[64,384]{1,0:T(8,128)(2,1)S(1)} collective-permute-done((bf16[64,384]{1,0:T(8,128)(2,1)S(1)}, bf16[64,384]{1,0:T(8,128)(2,1)S(1)}, u32[]{:S(2)}, u32[]{:S(2)}) %collective-permute-start.11) | collective-permute-done | bytes 49184 | tf_op jit(solution)/shard_map/ppermute | solution.py:840
  52.3 0.8 %unpack.1 = (f32[38,4,192]{2,1,0:T(4,128)}, f32[6,4,192]{2,1,0:T(4,128)}, f32[4,192]{1,0:T(4,128)}, f32[4,16,192]{2,1,0:T(8,128)}, f32[4,192]{1,0:T(4,128)}) custom-call(bf16[64,384]{1,0:T(8,128)(2,1)S(1)} %add_convert_fusion.mine_ref, bf16[64,384]{1,0:T(8,128)(2,1)S(1)} %collective-permute-done.11.theirs_ref), custom_call_target="tpu_custom_call" | custom-call | tf_op jit(solution)/shard_map/unpack/pallas_call | solution.py:931
  (7 shorter events, 0.1 us)
Async XLA Ops:
  0.6 12.4 %copy-start = (f32[4,192,38]{1,0,2:T(4,128)S(1)}, f32[4,192,38]{1,0,2:T(4,128)}, u32[]{:S(2)}) copy-start(f32[4,192,38]{1,0,2:T(4,128)} %param.14) | copy-start | bytes 350212
  0.6 12.4 %copy-start.1 = (bf16[1,4,64,192]{3,2,1,0:T(8,128)(2,1)S(1)}, bf16[1,4,64,192]{3,2,1,0:T(8,128)(2,1)}, u32[]{:S(2)}) copy-start(bf16[1,4,64,192]{3,2,1,0:T(8,128)(2,1)} %param.13) | copy-start | bytes 294916
  0.7 12.4 %copy-start.2 = (f32[4,16,192]{2,1,0:T(8,128)S(1)}, f32[4,16,192]{2,1,0:T(8,128)}, u32[]{:S(2)}) copy-start(f32[4,16,192]{2,1,0:T(8,128)} %alog_ref.1) | copy-start | bytes 147460
  0.7 12.4 %copy-start.3 = (f32[4,6,192]{2,0,1:T(4,128)S(1)}, f32[4,6,192]{2,0,1:T(4,128)}, u32[]{:S(2)}) copy-start(f32[4,6,192]{2,0,1:T(4,128)} %param.15) | copy-start | bytes 55300
  0.7 12.4 %copy-start.4 = (f32[4,192]{1,0:T(4,128)S(1)}, f32[4,192]{1,0:T(4,128)}, u32[]{:S(2)}) copy-start(f32[4,192]{1,0:T(4,128)} %bias_ref.1) | copy-start | bytes 9220
  0.7 12.4 %copy-start.5 = (f32[4,192]{1,0:T(4,128)S(1)}, f32[4,192]{1,0:T(4,128)}, u32[]{:S(2)}) copy-start(f32[4,192]{1,0:T(4,128)} %skip_ref.1) | copy-start | bytes 9220
  0.7 12.4 %copy-start.7 = (bf16[144,2176]{1,0:T(8,128)(2,1)S(1)}, bf16[144,2176]{1,0:T(8,128)(2,1)}, u32[]{:S(2)}) copy-start(bf16[144,2176]{1,0:T(8,128)(2,1)} %constant.8.clone.hot_ref) | copy-start | bytes 1880068
  7.3 6.3 %collective-permute-start = (bf16[64,256]{1,0:T(8,128)(2,1)S(1)}, bf16[64,256]{1,0:T(8,128)(2,1)S(1)}, u32[]{:S(2)}, u32[]{:S(2)}) collective-permute-start(bf16[64,256]{1,0:T(8,128)(2,1)S(1)} %get-tuple-element.60), channel_id=1, source_target_pairs={{0,1},{1,0},{2,3},{3,2},{4,5},{5,4},{6,7},{7,6},{8,9},{9,8},{10,11... | collective-permute-start | bytes 98312 | tf_op jit(solution)/shard_map/ppermute | solution.py:840
  10.4 5.4 %collective-permute-start.1 = (bf16[64,256]{1,0:T(8,128)(2,1)S(1)}, bf16[64,256]{1,0:T(8,128)(2,1)S(1)}, u32[]{:S(2)}, u32[]{:S(2)}) collective-permute-start(bf16[64,256]{1,0:T(8,128)(2,1)S(1)} %get-tuple-element.61), channel_id=1, source_target_pairs={{0,2},{1,3},{2,0},{3,1},{4,6},{5,7},{6,4},{7,5},{8,10},{9,11},{10,... | collective-permute-start | bytes 98312 | tf_op jit(solution)/shard_map/ppermute | solution.py:840
  13.0 5.7 %collective-permute-start.2 = (bf16[64,256]{1,0:T(8,128)(2,1)S(1)}, bf16[64,256]{1,0:T(8,128)(2,1)S(1)}, u32[]{:S(2)}, u32[]{:S(2)}) collective-permute-start(bf16[64,256]{1,0:T(8,128)(2,1)S(1)} %get-tuple-element.62), channel_id=1, source_target_pairs={{0,3},{1,2},{2,1},{3,0},{4,7},{5,6},{6,5},{7,4},{8,11},{9,10},{10,... | collective-permute-start | bytes 98312 | tf_op jit(solution)/shard_map/ppermute | solution.py:840
  18.7 12.3 %copy-start.9 = (bf16[256,512]{1,0:T(8,128)(2,1)S(1)}, bf16[256,512]{1,0:T(8,128)(2,1)}, u32[]{:S(2)}) copy-start(bf16[256,512]{1,0:T(8,128)(2,1)} %constant.6.clone.refs_2_.perm_ref) | copy-start | bytes 786436
  24.4 5.2 %collective-permute-start.3 = (bf16[64,192]{1,0:T(8,128)(2,1)S(1)}, bf16[64,192]{1,0:T(8,128)(2,1)S(1)}, u32[]{:S(2)}, u32[]{:S(2)}) collective-permute-start(bf16[64,192]{1,0:T(8,128)(2,1)S(1)} %get-tuple-element.70), channel_id=1, source_target_pairs={{0,1},{1,0},{2,3},{3,2},{4,5},{5,4},{6,7},{7,6},{8,9},{9,8},{10,11... | collective-permute-start | bytes 73736 | tf_op jit(solution)/shard_map/ppermute | solution.py:840
  24.5 5.1 %collective-permute-start.4 = (bf16[64,192]{1,0:T(8,128)(2,1)S(1)}, bf16[64,192]{1,0:T(8,128)(2,1)S(1)}, u32[]{:S(2)}, u32[]{:S(2)}) collective-permute-start(bf16[64,192]{1,0:T(8,128)(2,1)S(1)} %get-tuple-element.71), channel_id=1, source_target_pairs={{0,2},{1,3},{2,0},{3,1},{4,6},{5,7},{6,4},{7,5},{8,10},{9,11},{10,... | collective-permute-start | bytes 73736 | tf_op jit(solution)/shard_map/ppermute | solution.py:840
  25.4 5.7 %collective-permute-start.5 = (bf16[64,192]{1,0:T(8,128)(2,1)S(1)}, bf16[64,192]{1,0:T(8,128)(2,1)S(1)}, u32[]{:S(2)}, u32[]{:S(2)}) collective-permute-start(bf16[64,192]{1,0:T(8,128)(2,1)S(1)} %get-tuple-element.72), channel_id=1, source_target_pairs={{0,3},{1,2},{2,1},{3,0},{4,7},{5,6},{6,5},{7,4},{8,11},{9,10},{10,... | collective-permute-start | bytes 73736 | tf_op jit(solution)/shard_map/ppermute | solution.py:840
  37.4 11.1 %copy-start.6 = (s32[1,1,2]{2,1,0:T(1,128)S(1)}, s32[1,1,2]{2,1,0:T(1,128)}, u32[]{:S(2)}) copy-start(s32[1,1,2]{2,1,0:T(1,128)} %param.12) | copy-start | bytes 28
  37.4 11.1 %copy-start.8 = (bf16[256,512]{1,0:T(8,128)(2,1)S(1)}, bf16[256,512]{1,0:T(8,128)(2,1)}, u32[]{:S(2)}) copy-start(bf16[256,512]{1,0:T(8,128)(2,1)} %constant.7.clone.refs_3_.back_ref) | copy-start | bytes 786436
  37.4 1.3 %collective-permute-start.6 = (bf16[64,384]{1,0:T(8,128)(2,1)S(1)}, bf16[64,384]{1,0:T(8,128)(2,1)S(1)}, u32[]{:S(2)}, u32[]{:S(2)}) collective-permute-start(bf16[64,384]{1,0:T(8,128)(2,1)S(1)} %get-tuple-element.93), channel_id=1, source_target_pairs={{0,4},{4,0},{8,12},{12,8},{1,5},{5,1},{9,13},{13,9},{2,6},{6,2},{1... | collective-permute-start | bytes 147464 | tf_op jit(solution)/shard_map/ppermute | solution.py:840
  38.7 5.2 %collective-permute-start.9 = (bf16[64,384]{1,0:T(8,128)(2,1)S(1)}, bf16[64,384]{1,0:T(8,128)(2,1)S(1)}, u32[]{:S(2)}, u32[]{:S(2)}) collective-permute-start(bf16[64,384]{1,0:T(8,128)(2,1)S(1)} %add_convert_fusion.2), channel_id=1, source_target_pairs={{0,9},{1,8},{2,11},{3,10},{4,13},{5,12},{6,15},{7,14},{8,1},{9,0},... | collective-permute-start | bytes 147464 | tf_op jit(solution)/shard_map/ppermute | solution.py:845
  39.9 4.6 %collective-permute-start.8 = (bf16[64,384]{1,0:T(8,128)(2,1)S(1)}, bf16[64,384]{1,0:T(8,128)(2,1)S(1)}, u32[]{:S(2)}, u32[]{:S(2)}) collective-permute-start(bf16[64,384]{1,0:T(8,128)(2,1)S(1)} %add_convert_fusion.2), channel_id=1, source_target_pairs={{0,8},{1,9},{2,10},{3,11},{4,12},{5,13},{6,14},{7,15},{8,0},{9,1},... | collective-permute-start | bytes 147464 | tf_op jit(solution)/shard_map/ppermute | solution.py:845
  40.4 4.1 %collective-permute-start.7 = (bf16[64,384]{1,0:T(8,128)(2,1)S(1)}, bf16[64,384]{1,0:T(8,128)(2,1)S(1)}, u32[]{:S(2)}, u32[]{:S(2)}) collective-permute-start(bf16[64,384]{1,0:T(8,128)(2,1)S(1)} %add_convert_fusion.2), channel_id=1, source_target_pairs={{0,1},{1,0},{2,3},{3,2},{4,5},{5,4},{6,7},{7,6},{8,9},{9,8},{10,11... | collective-permute-start | bytes 147464 | tf_op jit(solution)/shard_map/ppermute | solution.py:845
  44.6 6.4 %collective-permute-start.10 = (bf16[64,384]{1,0:T(8,128)(2,1)S(1)}, bf16[64,384]{1,0:T(8,128)(2,1)S(1)}, u32[]{:S(2)}, u32[]{:S(2)}) collective-permute-start(bf16[64,384]{1,0:T(8,128)(2,1)S(1)} %add_convert_fusion.1), channel_id=1, source_target_pairs={{0,2},{1,3},{2,0},{3,1},{4,6},{5,7},{6,4},{7,5},{8,10},{9,11},{10,... | collective-permute-start | bytes 147464 | tf_op jit(solution)/shard_map/ppermute | solution.py:845
  51.0 1.3 %collective-permute-start.11 = (bf16[64,384]{1,0:T(8,128)(2,1)S(1)}, bf16[64,384]{1,0:T(8,128)(2,1)S(1)}, u32[]{:S(2)}, u32[]{:S(2)}) collective-permute-start(bf16[64,384]{1,0:T(8,128)(2,1)S(1)} %add_convert_fusion.mine_ref), channel_id=1, source_target_pairs={{0,4},{4,0},{8,12},{12,8},{1,5},{5,1},{9,13},{13,9},{2,6},{6,2},{1... | collective-permute-start | bytes 147464 | tf_op jit(solution)/shard_map/ppermute | solution.py:840

commit v4 on v3

--- a/solution.py
+++ b/solution.py
@@ -669,7 +669,7 @@
         t["dt"][s] = dt
         t["dtu"][s] = dt * t["u"][s]
 
-    each = 2 if ch % (2 * SUB) == 0 else 1
+    each = 3 if ch % (3 * SUB) == 0 else 1
 
     def channels_at(c):
         return [pl.ds(pl.multiple_of((c * each + k) * SUB, SUB), SUB) for k in range(each)]

time: 53.3 us -> 53.2 us (level)
  no operation moved by 1% of the time
where the time goes in v4:
time: 53.2 us; the launch traced here: 53.1 us
  Pallas kernels  23.8 us (45%)
  starting transfers between devices  17.7 us (33%)
  waiting for transfers between devices  10.6 us (20%)
  between operations  0.83 us (2%)
    pallas_call x7, Pallas kernels, call(): pl.pallas_call(functools.partial(kernel, plan, side), out_shape=out_shape...  23 us
    ppermute x8, starting transfers between devices, swap(): lax.ppermute(x, axis, [(i, i ^ step) for i in range(lax.axis_size(axis))])  10.3 us
    ppermute x8, waiting for transfers between devices, swap(): lax.ppermute(x, axis, [(i, i ^ step) for i in range(lax.axis_size(axis))])  9.08 us
    ppermute x4, starting transfers between devices, cross(): lax.ppermute(x, axes, [(i, i ^ mask) for i in range(lax.axis_size(axes))])  7.39 us
    ppermute x4, waiting for transfers between devices, cross(): lax.ppermute(x, axes, [(i, i ^ mask) for i in range(lax.axis_size(axes))])  1.54 us
  transfers between devices with their start and end apart: 12, of which 9 were waited for; matrix products, arithmetic and copies ran while one was open for 0% of the time, Pallas kernels for 9%

profile of v4, /device:TPU:0, one launch (start us, length us, event | category | flops | bytes accessed | tf_op | source)
XLA Modules:
  0.0 53.1 jit_solution(7674784147495083199)
XLA Ops:
  0.6 0.0 copy-start
  0.6 0.0 copy-start.1
  0.7 0.0 copy-start.2
  0.7 0.0 copy-start.3
  0.7 0.0 copy-start.4
  0.7 0.0 copy-start.7
  0.7 6.6 %rows_forward.1 = (bf16[64,256]{1,0:T(8,128)(2,1)S(1)}, bf16[64,256]{1,0:T(8,128)(2,1)S(1)}, bf16[64,256]{1,0:T(8,128)(2,1)S(1)}, bf16[64,256]{1,0:T(8,128)(2,1)...) custom-call(s32[2]{0:T(128)} %bitcast.18, ...), custom_call_target="tpu_custom_call" | custom-call | flops 4000000000 | bytes 4000000 | tf_op jit(solution)/shard_map/rows_forward/pallas_call | solution.py:824
  7.3 3.1 %collective-permute-start = (bf16[64,256]{1,0:T(8,128)(2,1)S(1)}, bf16[64,256]{1,0:T(8,128)(2,1)S(1)}, u32[]{:S(2)}, u32[]{:S(2)}) collective-permute-start(bf16[64,256]{1,0:T(8,128)(2,1)S(1)} %get-tuple-element.60), channel_id=1, source_target_pairs={{0,1},{1,0},{2,3},{3,2},{4,5},{5,4},{6,7},{7,6},{8,9},{9,8},{10,11... | collective-permute-start | bytes 98312 | tf_op jit(solution)/shard_map/ppermute | solution.py:840
  10.4 2.6 %collective-permute-start.1 = (bf16[64,256]{1,0:T(8,128)(2,1)S(1)}, bf16[64,256]{1,0:T(8,128)(2,1)S(1)}, u32[]{:S(2)}, u32[]{:S(2)}) collective-permute-start(bf16[64,256]{1,0:T(8,128)(2,1)S(1)} %get-tuple-element.61), channel_id=1, source_target_pairs={{0,2},{1,3},{2,0},{3,1},{4,6},{5,7},{6,4},{7,5},{8,10},{9,11},{10,... | collective-permute-start | bytes 98312 | tf_op jit(solution)/shard_map/ppermute | solution.py:840
  13.0 0.0 collective-permute-start.2
  13.0 0.0 copy-done.1
  13.0 0.0 copy-done.2
  13.1 0.0 copy-done.3
  13.1 0.0 copy-done.4
  13.1 0.0 copy-done.5
  13.1 0.0 copy-done.7
  13.1 0.5 columns_setup.1
  13.6 0.0 collective-permute-done.recv_refs_1_
  13.6 2.2 %collective-permute-done.1.recv_refs_2_ = bf16[64,256]{1,0:T(8,128)(2,1)S(1)} collective-permute-done((bf16[64,256]{1,0:T(8,128)(2,1)S(1)}, bf16[64,256]{1,0:T(8,128)(2,1)S(1)}, u32[]{:S(2)}, u32[]{:S(2)}) %collective-permute-start.1) | collective-permute-done | bytes 32800 | tf_op jit(solution)/shard_map/ppermute | solution.py:840
  15.8 2.9 %collective-permute-done.2.recv_refs_3_ = bf16[64,256]{1,0:T(8,128)(2,1)S(1)} collective-permute-done((bf16[64,256]{1,0:T(8,128)(2,1)S(1)}, bf16[64,256]{1,0:T(8,128)(2,1)S(1)}, u32[]{:S(2)}, u32[]{:S(2)}) %collective-permute-start.2) | collective-permute-done | bytes 32800 | tf_op jit(solution)/shard_map/ppermute | solution.py:840
  18.8 5.5 %columns.1 = (bf16[64,192]{1,0:T(8,128)(2,1)S(1)}, bf16[64,192]{1,0:T(8,128)(2,1)S(1)}, bf16[64,192]{1,0:T(8,128)(2,1)S(1)}, bf16[64,192]{1,0:T(8,128)(2,1)S(1)}...) custom-call(bf16[64,256]{1,0:T(8,128)(2,1)S(1)} %get-tuple-element.5, ...), custom_call_target="tpu_custom_call" | custom-call | flops 8000000000 | bytes 4000000 | tf_op jit(solution)/shard_map/columns/pallas_call | solution.py:824
  24.3 0.1 collective-permute-start.3
  24.4 0.9 %collective-permute-start.4 = (bf16[64,192]{1,0:T(8,128)(2,1)S(1)}, bf16[64,192]{1,0:T(8,128)(2,1)S(1)}, u32[]{:S(2)}, u32[]{:S(2)}) collective-permute-start(bf16[64,192]{1,0:T(8,128)(2,1)S(1)} %get-tuple-element.71), channel_id=1, source_target_pairs={{0,2},{1,3},{2,0},{3,1},{4,6},{5,7},{6,4},{7,5},{8,10},{9,11},{10,... | collective-permute-start | bytes 73736 | tf_op jit(solution)/shard_map/ppermute | solution.py:840
  25.3 3.5 %collective-permute-start.5 = (bf16[64,192]{1,0:T(8,128)(2,1)S(1)}, bf16[64,192]{1,0:T(8,128)(2,1)S(1)}, u32[]{:S(2)}, u32[]{:S(2)}) collective-permute-start(bf16[64,192]{1,0:T(8,128)(2,1)S(1)} %get-tuple-element.72), channel_id=1, source_target_pairs={{0,3},{1,2},{2,1},{3,0},{4,7},{5,6},{6,5},{7,4},{8,11},{9,10},{10,... | collective-permute-start | bytes 73736 | tf_op jit(solution)/shard_map/ppermute | solution.py:840
  28.8 0.8 %columns_grads.1.grads_v_ref = bf16[64,384]{1,0:T(8,128)(2,1)S(1)} custom-call(bf16[80,512]{1,0:T(8,128)(2,1)S(1)} %get-tuple-element.86.t__gpb__, f32[16,192,128]{2,1,0:T(8,128)S(1)} %get-tuple-element.87.t__gr__, bf16[192,512]{1,0:T(8,128)(2,1)S(1)} %get-tuple-element.88.t__gyu__, bf16[192,512]{1,0:T(8,128)(2,1)S(1)} %get-tuple-element.89.t__gzb__, ...), custom_call_target="tpu_custom_call" | custom-call | flops 1000000000 | bytes 4000000 | tf_op jit(solution)/shard_map/columns_grads/pallas_call | solution.py:824
  29.5 0.0 collective-permute-done.3.gy_refs_1_
  29.5 0.0 collective-permute-done.4.gy_refs_2_
  29.5 1.5 %collective-permute-done.5.gy_refs_3_ = bf16[64,192]{1,0:T(8,128)(2,1)S(1)} collective-permute-done((bf16[64,192]{1,0:T(8,128)(2,1)S(1)}, bf16[64,192]{1,0:T(8,128)(2,1)S(1)}, u32[]{:S(2)}, u32[]{:S(2)}) %collective-permute-start.5) | collective-permute-done | bytes 24608 | tf_op jit(solution)/shard_map/ppermute | solution.py:840
  31.0 0.0 copy-done.9
  31.0 6.3 %rows_backward.1 = (bf16[64,384]{1,0:T(8,128)(2,1)S(1)}, bf16[64,384]{1,0:T(8,128)(2,1)S(1)}, bf16[256,128]{1,0:T(8,128)(2,1)S(1)}, f32[256,384]{1,0:T(8,128)S(1)}, f32[256,384]{1,0:T(8,128)S(1)}) custom-call(bf16[64,192]{1,0:T(8,128)(2,1)S(1)} %get-tuple-element.69.gy_refs_0_, bf16[64,192]{1,0:T(8,128)(2,1)S(1)} %collective-permute-done.3.gy_refs_1_, ...), custom_call_target="tpu_custom_call" | custom-call | flops 8000000000 | bytes 4000000 | tf_op jit(solution)/shard_map/rows_backward/pallas_call | solution.py:824
  37.3 0.0 copy-start.6
  37.3 0.0 copy-start.8
  37.3 0.1 collective-permute-start.6
  37.4 1.2 %collective-permute-done.6 = bf16[64,384]{1,0:T(8,128)(2,1)S(1)} collective-permute-done((bf16[64,384]{1,0:T(8,128)(2,1)S(1)}, bf16[64,384]{1,0:T(8,128)(2,1)S(1)}, u32[]{:S(2)}, u32[]{:S(2)}) %collective-permute-start.6) | collective-permute-done | bytes 49184 | tf_op jit(solution)/shard_map/ppermute | solution.py:840
  38.6 1.2 %collective-permute-start.9 = (bf16[64,384]{1,0:T(8,128)(2,1)S(1)}, bf16[64,384]{1,0:T(8,128)(2,1)S(1)}, u32[]{:S(2)}, u32[]{:S(2)}) collective-permute-start(bf16[64,384]{1,0:T(8,128)(2,1)S(1)} %add_convert_fusion.2), channel_id=1, source_target_pairs={{0,9},{1,8},{2,11},{3,10},{4,13},{5,12},{6,15},{7,14},{8,1},{9,0},... | collective-permute-start | bytes 147464 | tf_op jit(solution)/shard_map/ppermute | solution.py:845
  39.8 0.5 %collective-permute-start.8 = (bf16[64,384]{1,0:T(8,128)(2,1)S(1)}, bf16[64,384]{1,0:T(8,128)(2,1)S(1)}, u32[]{:S(2)}, u32[]{:S(2)}) collective-permute-start(bf16[64,384]{1,0:T(8,128)(2,1)S(1)} %add_convert_fusion.2), channel_id=1, source_target_pairs={{0,8},{1,9},{2,10},{3,11},{4,12},{5,13},{6,14},{7,15},{8,0},{9,1},... | collective-permute-start | bytes 147464 | tf_op jit(solution)/shard_map/ppermute | solution.py:845
  40.3 1.8 %collective-permute-start.7 = (bf16[64,384]{1,0:T(8,128)(2,1)S(1)}, bf16[64,384]{1,0:T(8,128)(2,1)S(1)}, u32[]{:S(2)}, u32[]{:S(2)}) collective-permute-start(bf16[64,384]{1,0:T(8,128)(2,1)S(1)} %add_convert_fusion.2), channel_id=1, source_target_pairs={{0,1},{1,0},{2,3},{3,2},{4,5},{5,4},{6,7},{7,6},{8,9},{9,8},{10,11... | collective-permute-start | bytes 147464 | tf_op jit(solution)/shard_map/ppermute | solution.py:845
  42.2 1.5 %columns_output.1 = bf16[256,192]{1,0:T(8,128)(2,1)} custom-call(f32[4,32,8,128]{3,2,1,0:T(8,128)S(1)} %get-tuple-element.94.kept__bc__, f32[4,16,192,128]{3,2,1,0:T(8,128)S(1)} %get-tuple-element.95.kept__h__, f32[4,192,128]{2,1,0:T(8,128)S(1)} %get-tuple-element.96.kept__u__, f32[17,192,128]{2,1,0:T(8,128)S(1)} %get-tuple-element.67.ready__rb__.gain), custom_call_target="tpu_custom_call" | custom-call | flops 1000000000 | bytes 4000000 | tf_op jit(solution)/shard_map/columns_output/pallas_call | solution.py:824
  43.7 0.1 collective-permute-done.9
  43.8 0.6 %collective-permute-done.8 = bf16[64,384]{1,0:T(8,128)(2,1)S(1)} collective-permute-done((bf16[64,384]{1,0:T(8,128)(2,1)S(1)}, bf16[64,384]{1,0:T(8,128)(2,1)S(1)}, u32[]{:S(2)}, u32[]{:S(2)}) %collective-permute-start.8) | collective-permute-done | bytes 49184 | tf_op jit(solution)/shard_map/ppermute | solution.py:845
  44.4 0.1 collective-permute-done.7
  44.5 3.8 %collective-permute-start.10 = (bf16[64,384]{1,0:T(8,128)(2,1)S(1)}, bf16[64,384]{1,0:T(8,128)(2,1)S(1)}, u32[]{:S(2)}, u32[]{:S(2)}) collective-permute-start(bf16[64,384]{1,0:T(8,128)(2,1)S(1)} %add_convert_fusion.1), channel_id=1, source_target_pairs={{0,2},{1,3},{2,0},{3,1},{4,6},{5,7},{6,4},{7,5},{8,10},{9,11},{10,... | collective-permute-start | bytes 147464 | tf_op jit(solution)/shard_map/ppermute | solution.py:845
  48.3 0.0 copy-done.8
  48.4 1.8 %rows_output.1 = bf16[192,256]{1,0:T(8,128)(2,1)} custom-call(s32[2]{0:T(128)S(1)} %bitcast.19, bf16[256,512]{1,0:T(8,128)(2,1)S(1)} %copy-done.8, f32[32,384]{1,0:T(8,128)S(1)} %get-tuple-element.63.after_ref.w__small__, f32[128,384]{1,0:T(8,128)S(1)} %get-tuple-element.75.w__x__, f32[256,384]{1,0:T(8,128)S(1)} %get-tuple-element.79.kept__dt__, ...), custom_call_target="tpu_custom_call" | custom-call | flops 1000000000 | bytes 4000000 | tf_op jit(solution)/shard_map/rows_output/pallas_call | solution.py:824
  50.2 0.8 %collective-permute-done.10 = bf16[64,384]{1,0:T(8,128)(2,1)S(1)} collective-permute-done((bf16[64,384]{1,0:T(8,128)(2,1)S(1)}, bf16[64,384]{1,0:T(8,128)(2,1)S(1)}, u32[]{:S(2)}, u32[]{:S(2)}) %collective-permute-start.10) | collective-permute-done | bytes 49184 | tf_op jit(solution)/shard_map/ppermute | solution.py:845
  51.0 0.1 collective-permute-start.11
  51.0 1.2 %collective-permute-done.11.theirs_ref = bf16[64,384]{1,0:T(8,128)(2,1)S(1)} collective-permute-done((bf16[64,384]{1,0:T(8,128)(2,1)S(1)}, bf16[64,384]{1,0:T(8,128)(2,1)S(1)}, u32[]{:S(2)}, u32[]{:S(2)}) %collective-permute-start.11) | collective-permute-done | bytes 49184 | tf_op jit(solution)/shard_map/ppermute | solution.py:840
  52.3 0.8 %unpack.1 = (f32[38,4,192]{2,1,0:T(4,128)}, f32[6,4,192]{2,1,0:T(4,128)}, f32[4,192]{1,0:T(4,128)}, f32[4,16,192]{2,1,0:T(8,128)}, f32[4,192]{1,0:T(4,128)}) custom-call(bf16[64,384]{1,0:T(8,128)(2,1)S(1)} %add_convert_fusion.mine_ref, bf16[64,384]{1,0:T(8,128)(2,1)S(1)} %collective-permute-done.11.theirs_ref), custom_call_target="tpu_custom_call" | custom-call | tf_op jit(solution)/shard_map/unpack/pallas_call | solution.py:931
  (7 shorter events, 0.1 us)
Async XLA Ops:
  0.6 12.4 %copy-start = (f32[4,192,38]{1,0,2:T(4,128)S(1)}, f32[4,192,38]{1,0,2:T(4,128)}, u32[]{:S(2)}) copy-start(f32[4,192,38]{1,0,2:T(4,128)} %param.14) | copy-start | bytes 350212
  0.6 12.4 %copy-start.1 = (bf16[1,4,64,192]{3,2,1,0:T(8,128)(2,1)S(1)}, bf16[1,4,64,192]{3,2,1,0:T(8,128)(2,1)}, u32[]{:S(2)}) copy-start(bf16[1,4,64,192]{3,2,1,0:T(8,128)(2,1)} %param.13) | copy-start | bytes 294916
  0.7 12.4 %copy-start.2 = (f32[4,16,192]{2,1,0:T(8,128)S(1)}, f32[4,16,192]{2,1,0:T(8,128)}, u32[]{:S(2)}) copy-start(f32[4,16,192]{2,1,0:T(8,128)} %alog_ref.1) | copy-start | bytes 147460
  0.7 12.4 %copy-start.3 = (f32[4,6,192]{2,0,1:T(4,128)S(1)}, f32[4,6,192]{2,0,1:T(4,128)}, u32[]{:S(2)}) copy-start(f32[4,6,192]{2,0,1:T(4,128)} %param.15) | copy-start | bytes 55300
  0.7 12.4 %copy-start.4 = (f32[4,192]{1,0:T(4,128)S(1)}, f32[4,192]{1,0:T(4,128)}, u32[]{:S(2)}) copy-start(f32[4,192]{1,0:T(4,128)} %bias_ref.1) | copy-start | bytes 9220
  0.7 12.4 %copy-start.5 = (f32[4,192]{1,0:T(4,128)S(1)}, f32[4,192]{1,0:T(4,128)}, u32[]{:S(2)}) copy-start(f32[4,192]{1,0:T(4,128)} %skip_ref.1) | copy-start | bytes 9220
  0.7 12.4 %copy-start.7 = (bf16[144,2176]{1,0:T(8,128)(2,1)S(1)}, bf16[144,2176]{1,0:T(8,128)(2,1)}, u32[]{:S(2)}) copy-start(bf16[144,2176]{1,0:T(8,128)(2,1)} %constant.8.clone.hot_ref) | copy-start | bytes 1880068
  7.3 6.3 %collective-permute-start = (bf16[64,256]{1,0:T(8,128)(2,1)S(1)}, bf16[64,256]{1,0:T(8,128)(2,1)S(1)}, u32[]{:S(2)}, u32[]{:S(2)}) collective-permute-start(bf16[64,256]{1,0:T(8,128)(2,1)S(1)} %get-tuple-element.60), channel_id=1, source_target_pairs={{0,1},{1,0},{2,3},{3,2},{4,5},{5,4},{6,7},{7,6},{8,9},{9,8},{10,11... | collective-permute-start | bytes 98312 | tf_op jit(solution)/shard_map/ppermute | solution.py:840
  10.4 5.4 %collective-permute-start.1 = (bf16[64,256]{1,0:T(8,128)(2,1)S(1)}, bf16[64,256]{1,0:T(8,128)(2,1)S(1)}, u32[]{:S(2)}, u32[]{:S(2)}) collective-permute-start(bf16[64,256]{1,0:T(8,128)(2,1)S(1)} %get-tuple-element.61), channel_id=1, source_target_pairs={{0,2},{1,3},{2,0},{3,1},{4,6},{5,7},{6,4},{7,5},{8,10},{9,11},{10,... | collective-permute-start | bytes 98312 | tf_op jit(solution)/shard_map/ppermute | solution.py:840
  13.0 5.7 %collective-permute-start.2 = (bf16[64,256]{1,0:T(8,128)(2,1)S(1)}, bf16[64,256]{1,0:T(8,128)(2,1)S(1)}, u32[]{:S(2)}, u32[]{:S(2)}) collective-permute-start(bf16[64,256]{1,0:T(8,128)(2,1)S(1)} %get-tuple-element.62), channel_id=1, source_target_pairs={{0,3},{1,2},{2,1},{3,0},{4,7},{5,6},{6,5},{7,4},{8,11},{9,10},{10,... | collective-permute-start | bytes 98312 | tf_op jit(solution)/shard_map/ppermute | solution.py:840
  18.7 12.3 %copy-start.9 = (bf16[256,512]{1,0:T(8,128)(2,1)S(1)}, bf16[256,512]{1,0:T(8,128)(2,1)}, u32[]{:S(2)}) copy-start(bf16[256,512]{1,0:T(8,128)(2,1)} %constant.6.clone.refs_2_.perm_ref) | copy-start | bytes 786436
  24.3 5.2 %collective-permute-start.3 = (bf16[64,192]{1,0:T(8,128)(2,1)S(1)}, bf16[64,192]{1,0:T(8,128)(2,1)S(1)}, u32[]{:S(2)}, u32[]{:S(2)}) collective-permute-start(bf16[64,192]{1,0:T(8,128)(2,1)S(1)} %get-tuple-element.70), channel_id=1, source_target_pairs={{0,1},{1,0},{2,3},{3,2},{4,5},{5,4},{6,7},{7,6},{8,9},{9,8},{10,11... | collective-permute-start | bytes 73736 | tf_op jit(solution)/shard_map/ppermute | solution.py:840
  24.4 5.1 %collective-permute-start.4 = (bf16[64,192]{1,0:T(8,128)(2,1)S(1)}, bf16[64,192]{1,0:T(8,128)(2,1)S(1)}, u32[]{:S(2)}, u32[]{:S(2)}) collective-permute-start(bf16[64,192]{1,0:T(8,128)(2,1)S(1)} %get-tuple-element.71), channel_id=1, source_target_pairs={{0,2},{1,3},{2,0},{3,1},{4,6},{5,7},{6,4},{7,5},{8,10},{9,11},{10,... | collective-permute-start | bytes 73736 | tf_op jit(solution)/shard_map/ppermute | solution.py:840
  25.3 5.7 %collective-permute-start.5 = (bf16[64,192]{1,0:T(8,128)(2,1)S(1)}, bf16[64,192]{1,0:T(8,128)(2,1)S(1)}, u32[]{:S(2)}, u32[]{:S(2)}) collective-permute-start(bf16[64,192]{1,0:T(8,128)(2,1)S(1)} %get-tuple-element.72), channel_id=1, source_target_pairs={{0,3},{1,2},{2,1},{3,0},{4,7},{5,6},{6,5},{7,4},{8,11},{9,10},{10,... | collective-permute-start | bytes 73736 | tf_op jit(solution)/shard_map/ppermute | solution.py:840
  37.3 11.1 %copy-start.6 = (s32[1,1,2]{2,1,0:T(1,128)S(1)}, s32[1,1,2]{2,1,0:T(1,128)}, u32[]{:S(2)}) copy-start(s32[1,1,2]{2,1,0:T(1,128)} %param.12) | copy-start | bytes 28
  37.3 11.1 %copy-start.8 = (bf16[256,512]{1,0:T(8,128)(2,1)S(1)}, bf16[256,512]{1,0:T(8,128)(2,1)}, u32[]{:S(2)}) copy-start(bf16[256,512]{1,0:T(8,128)(2,1)} %constant.7.clone.refs_3_.back_ref) | copy-start | bytes 786436
  37.3 1.3 %collective-permute-start.6 = (bf16[64,384]{1,0:T(8,128)(2,1)S(1)}, bf16[64,384]{1,0:T(8,128)(2,1)S(1)}, u32[]{:S(2)}, u32[]{:S(2)}) collective-permute-start(bf16[64,384]{1,0:T(8,128)(2,1)S(1)} %get-tuple-element.93), channel_id=1, source_target_pairs={{0,4},{4,0},{8,12},{12,8},{1,5},{5,1},{9,13},{13,9},{2,6},{6,2},{1... | collective-permute-start | bytes 147464 | tf_op jit(solution)/shard_map/ppermute | solution.py:840
  38.6 5.2 %collective-permute-start.9 = (bf16[64,384]{1,0:T(8,128)(2,1)S(1)}, bf16[64,384]{1,0:T(8,128)(2,1)S(1)}, u32[]{:S(2)}, u32[]{:S(2)}) collective-permute-start(bf16[64,384]{1,0:T(8,128)(2,1)S(1)} %add_convert_fusion.2), channel_id=1, source_target_pairs={{0,9},{1,8},{2,11},{3,10},{4,13},{5,12},{6,15},{7,14},{8,1},{9,0},... | collective-permute-start | bytes 147464 | tf_op jit(solution)/shard_map/ppermute | solution.py:845
  39.8 4.6 %collective-permute-start.8 = (bf16[64,384]{1,0:T(8,128)(2,1)S(1)}, bf16[64,384]{1,0:T(8,128)(2,1)S(1)}, u32[]{:S(2)}, u32[]{:S(2)}) collective-permute-start(bf16[64,384]{1,0:T(8,128)(2,1)S(1)} %add_convert_fusion.2), channel_id=1, source_target_pairs={{0,8},{1,9},{2,10},{3,11},{4,12},{5,13},{6,14},{7,15},{8,0},{9,1},... | collective-permute-start | bytes 147464 | tf_op jit(solution)/shard_map/ppermute | solution.py:845
  40.3 4.1 %collective-permute-start.7 = (bf16[64,384]{1,0:T(8,128)(2,1)S(1)}, bf16[64,384]{1,0:T(8,128)(2,1)S(1)}, u32[]{:S(2)}, u32[]{:S(2)}) collective-permute-start(bf16[64,384]{1,0:T(8,128)(2,1)S(1)} %add_convert_fusion.2), channel_id=1, source_target_pairs={{0,1},{1,0},{2,3},{3,2},{4,5},{5,4},{6,7},{7,6},{8,9},{9,8},{10,11... | collective-permute-start | bytes 147464 | tf_op jit(solution)/shard_map/ppermute | solution.py:845
  44.5 6.4 %collective-permute-start.10 = (bf16[64,384]{1,0:T(8,128)(2,1)S(1)}, bf16[64,384]{1,0:T(8,128)(2,1)S(1)}, u32[]{:S(2)}, u32[]{:S(2)}) collective-permute-start(bf16[64,384]{1,0:T(8,128)(2,1)S(1)} %add_convert_fusion.1), channel_id=1, source_target_pairs={{0,2},{1,3},{2,0},{3,1},{4,6},{5,7},{6,4},{7,5},{8,10},{9,11},{10,... | collective-permute-start | bytes 147464 | tf_op jit(solution)/shard_map/ppermute | solution.py:845
  51.0 1.3 %collective-permute-start.11 = (bf16[64,384]{1,0:T(8,128)(2,1)S(1)}, bf16[64,384]{1,0:T(8,128)(2,1)S(1)}, u32[]{:S(2)}, u32[]{:S(2)}) collective-permute-start(bf16[64,384]{1,0:T(8,128)(2,1)S(1)} %add_convert_fusion.mine_ref), channel_id=1, source_target_pairs={{0,4},{4,0},{8,12},{12,8},{1,5},{5,1},{9,13},{13,9},{2,6},{6,2},{1... | collective-permute-start | bytes 147464 | tf_op jit(solution)/shard_map/ppermute | solution.py:840
